TPU v7x, 32 devices: a whole 2x2x4 slice. The times are simulated.
32 devices in a mesh: row: 8 (over z, x), col: 4 (over y, core).
Axes of the slice: x: 2, y: 2, z: 4, core: 2. Of those that a mesh axis runs over, the one named last changes fastest.
Arguments:
- features: bfloat16 [8192, 256], P(('row', 'col')), may hold values from -6 to 6
- grad_out: bfloat16 [8192, 256], P(('row', 'col')), may hold values from -6 to 6
- degrees: int32 [8192], P(('row', 'col')), may hold values from 1 to 8236, as said below
- w_self: bfloat16 [256, 256], replicated, may hold values from -0.375 to 0.375
- w_neigh: bfloat16 [256, 256], replicated, may hold values from -0.375 to 0.375
- bias: float32 [256], replicated, may hold values from -4 to 4
- tile_slots: int32 [8, 4, 88], P('row', 'col'), may hold values from 0 to 127, as said below
- tile_count: int32 [8, 4], P('row', 'col'), may hold values from 22 to 88, as said below
- tile_masks: int32 [8, 4, 88, 16, 128], P('row', 'col'), may hold values from 0 to 255
Outputs:
- layer_out: bfloat16 [8192, 256], P(('row', 'col'))
- grad_in: bfloat16 [8192, 256], P(('row', 'col'))
- grad_w_self: float32 [256, 256], replicated
- grad_w_neigh: float32 [256, 256], replicated
Inputs may be any that keep to these rules, and one draw needn't show every extreme that they name: `tile_slots`: on each device the 88 slot numbers are distinct and rise; slot s names block row s % 8 of the device's row group and block column s // 8 of its panel. Only a device's first tile_count tiles are live; the others are ignored. Some device holds 88 live tiles. `degrees`: each node's degree is at least the number of ones in its row of A, and at least 1; some node has the largest degree.
All inputs are finite; a program needn't handle non-finite values.
Results may differ from a plain program's by a relative error of at most 0.014.
Values may be sent and summed in bfloat16 or wider, within the bound.
No kernel may reach another device: no remote copies, remote signals or barrier semaphores. Data moves between devices by JAX's collectives and lax.ppermute only.
A program may use at most 64 MiB of HBM per device.

v0:
```python
import functools
import math

import jax
import jax.numpy as jnp
from jax import lax
from jax.experimental import pallas as pl
from jax.experimental.pallas import tpu as pltpu
from jax.sharding import PartitionSpec as P


BOTH_FORMS_BYTES = 8 * 1024 * 1024
DIGIT_ROWS = 16

VMEM = pl.BlockSpec(memory_space=pltpu.VMEM)
ANY = pl.BlockSpec(memory_space=pl.ANY)
SMEM = pl.BlockSpec(memory_space=pltpu.SMEM)

f32 = jnp.float32
bf16 = jnp.bfloat16


def mm(a, b):
    return jnp.dot(a, b, preferred_element_type=f32)


def mm_nt(a, b):
    return lax.dot_general(a, b, (((1,), (1,)), ((), ())), preferred_element_type=f32)


def mm_tn(a, b):
    return lax.dot_general(a, b, (((0,), (0,)), ((), ())), preferred_element_type=f32)


def params(*arrays):
    held = sum(math.prod(array.shape) * jnp.dtype(array.dtype).itemsize for array in arrays)
    return pltpu.CompilerParams(vmem_limit_bytes=held + held // 8 + (4 << 20))


def cost(nanoseconds):
    return pl.CostEstimate(flops=nanoseconds * 10**6, bytes_accessed=0, transcendentals=0)


def span(index, size):
    return pl.ds(pl.multiple_of(index * size, size), size)


def unpack_kernel(block_rows, gather, slots_ref, count_ref, masks_ref, *refs):
    dense_ref = refs[-1]
    words, width = masks_ref.shape[1:]
    height, length = dense_ref.shape

    @pl.loop(0, height // width)
    def _(step):
        dense_ref[span(step, width), :] = jnp.zeros((width, length), bf16)

    shifts = lax.broadcasted_iota(jnp.int32, (words, 8, width), 1)

    @pl.loop(0, count_ref[0])
    def _(tile):
        slot = slots_ref[tile]
        row_block = lax.rem(slot, block_rows)
        column_block = lax.div(slot, block_rows)
        word = masks_ref[tile]
        spread_words = jnp.broadcast_to(word[:, None, :], (words, 8, width))
        bits = jnp.bitwise_and(jnp.right_shift(spread_words, shifts), 1)
        bits = bits.astype(f32).reshape(words * 8, width)
        if gather:
            dense_ref[span(row_block, width), span(column_block, width)] = bits.T.astype(bf16)
        else:
            dense_ref[span(column_block, width), span(row_block, width)] = bits.astype(bf16)


def unpack(gather, tiles, after, panel, group):
    slot_ids, live_count, masks = tiles
    shape = jax.ShapeDtypeStruct((group, panel) if gather else (panel, group), bf16)
    block_rows = group // masks.shape[2]
    return pl.pallas_call(
        functools.partial(unpack_kernel, block_rows, gather),
        out_shape=shape,
        in_specs=[SMEM, SMEM, VMEM] + [ANY] * len(after),
        out_specs=VMEM,
        compiler_params=params(masks, shape),
        cost_estimate=cost(4000),
        name="unpack_gather" if gather else "unpack_spread",
    )(slot_ids, live_count, masks, *after)


def near_kernel(degrees_ref, features_ref, cotangents_ref, near_ref):
    rows = features_ref.shape[0]
    near_ref[pl.ds(0, rows), :] = features_ref[...]
    near_ref[pl.ds(rows, rows), :] = cotangents_ref[...]
    degree = jnp.broadcast_to(degrees_ref[...], (DIGIT_ROWS, rows))
    place = lax.broadcasted_iota(jnp.int32, degree.shape, 0)
    digit = jnp.bitwise_and(jnp.right_shift(degree, 8 * jnp.minimum(place, 3)), 255)
    near_ref[pl.ds(2 * rows, DIGIT_ROWS), :] = digit.astype(f32).astype(bf16)


def pack_near(degrees, features, cotangents):
    rows, width = features.shape
    near = jax.ShapeDtypeStruct((2 * rows + DIGIT_ROWS, width), bf16)
    return pl.pallas_call(
        near_kernel,
        out_shape=near,
        in_specs=[VMEM] * 3,
        out_specs=VMEM,
        compiler_params=params(near, near),
        cost_estimate=cost(500),
        name="near",
    )(degrees.reshape(1, rows), features, cotangents)


def forward_kernel(n_row, n_col, natural, n_after, place_ref, adjacency_ref, *refs):
    blocks, refs = refs[:n_row], refs[n_row + n_after :]
    outs, panel_ref = refs[:2], refs[2]
    rows = blocks[0].shape[0]
    row, col = place_ref[0], place_ref[1]
    for d in range(n_row):
        panel_ref[span(jnp.bitwise_xor(row, d), rows), :] = blocks[d][...]
    for e in list(range(1, n_col, 2)) + list(range(0, n_col, 2)):
        where = span(jnp.bitwise_xor(col, e), rows)
        if natural:
            total = mm(adjacency_ref[where, :], panel_ref[...])
        else:
            total = mm_tn(adjacency_ref[:, where], panel_ref[...])
        out = outs[e % 2]
        out[pl.ds((e // 2) * rows, rows), :] = total.astype(out.dtype)


def forward(place, adjacency, natural, blocks, after, n_col):
    rows, width = blocks[0].shape
    n_row = len(blocks)
    half = rows * n_col // 2
    shapes = [jax.ShapeDtypeStruct((half, width), kind) for kind in (f32, bf16)]
    return pl.pallas_call(
        functools.partial(forward_kernel, n_row, n_col, natural, len(after)),
        out_shape=shapes,
        in_specs=[SMEM, VMEM] + [VMEM] * n_row + [ANY] * len(after),
        out_specs=[VMEM, VMEM],
        scratch_shapes=[pltpu.VMEM((rows * n_row, width), bf16)],
        compiler_params=params(adjacency, *blocks, *blocks, *shapes),
        cost_estimate=cost(2200),
        name="forward",
    )(place, adjacency, *blocks, *after)


def node_kernel(n_part, *refs):
    sums, refs = refs[:n_part], refs[n_part:]
    nears, refs = refs[:n_part], refs[n_part:]
    w_self, w_neigh, bias, out_ref, mean_ref, grad_ref, up_ref = refs
    rows = out_ref.shape[0]
    for h in range(n_part):
        parts = [sums[h2][pl.ds((h ^ h2) * rows, rows), :].astype(f32) for h2 in range(n_part)]
        while len(parts) > 1:
            parts = [parts[i] + parts[i + 1] for i in range(0, len(parts), 2)]
        digits = nears[h][pl.ds(2 * rows, DIGIT_ROWS), :].astype(f32)[:8, :]
        place = lax.broadcasted_iota(jnp.int32, digits.shape, 0)
        scales = jnp.where(place < 4, jnp.left_shift(1, 8 * jnp.minimum(place, 3)), 0).astype(f32)
        degree = jnp.sum((digits * scales).T, axis=1, keepdims=True)
        inverse = 1.0 / degree
        mean = (parts[0] * inverse).astype(bf16)
        preact = mm(nears[h][pl.ds(0, rows), :], w_self[...]) + mm(mean, w_neigh[...]) + bias[...]
        gate = jax.nn.sigmoid(preact)
        if h == 0:
            out_ref[...] = (preact * gate).astype(bf16)
        grad = nears[h][pl.ds(rows, rows), :].astype(f32) * gate * (1.0 + preact * (1.0 - gate))
        grad = grad.astype(bf16)
        here = pl.ds(h * rows, rows)
        mean_ref[here, :] = mean
        grad_ref[here, :] = grad
        up_ref[here, :] = (mm_nt(grad, w_neigh[...]) * inverse).astype(bf16)


def node(sums, nears, w_self, w_neigh, bias):
    n_part = len(sums)
    width = nears[0].shape[1]
    rows = sums[0].shape[0] // n_part
    all_rows = jax.ShapeDtypeStruct((rows * n_part, width), bf16)
    shapes = [jax.ShapeDtypeStruct((rows, width), bf16), all_rows, all_rows, all_rows]
    return pl.pallas_call(
        functools.partial(node_kernel, n_part),
        out_shape=shapes,
        in_specs=[VMEM] * (2 * n_part + 3),
        out_specs=[VMEM] * 4,
        compiler_params=params(*sums, *nears, w_self, w_neigh, *shapes),
        cost_estimate=cost(2000),
        name="node",
    )(*sums, *nears, w_self, w_neigh, bias)


def weight_kernel(n_part, place_ref, mean_ref, grad_ref, w_self, *refs):
    nears, (keep_ref, send_ref, base_ref, total_ref) = refs[:n_part], refs[n_part:]
    rows = base_ref.shape[0]
    here = pl.ds(0, rows)
    grad_self = mm_tn(nears[0][here, :], grad_ref[here, :])
    for h in range(1, n_part):
        grad_self = grad_self + mm_tn(nears[h][here, :], grad_ref[pl.ds(h * rows, rows), :])
    grad_neigh = mm_tn(mean_ref[...], grad_ref[...])
    first = lax.rem(place_ref[1], 2) == 0
    keep, send = total_ref.at[0], total_ref.at[1]
    keep[...] = jnp.where(first, grad_self, grad_neigh)
    send[...] = jnp.where(first, grad_neigh, grad_self)
    here = span(lax.div(place_ref[1], 2), keep_ref.shape[0])
    keep_ref[...] = keep[here, :]
    send_ref[...] = send[here, :].astype(bf16)
    base_ref[...] = mm_nt(grad_ref[pl.ds(0, rows), :], w_self[...])


def weight(place, mean, grad, w_self, nears):
    n_part = len(nears)
    rows, width = mean.shape[0] // n_part, mean.shape[1]
    return pl.pallas_call(
        functools.partial(weight_kernel, n_part),
        out_shape=[
            jax.ShapeDtypeStruct((width // n_part, width), f32),
            jax.ShapeDtypeStruct((width // n_part, width), bf16),
            jax.ShapeDtypeStruct((rows, width), f32),
        ],
        in_specs=[SMEM] + [VMEM] * (3 + n_part),
        out_specs=[VMEM] * 3,
        scratch_shapes=[pltpu.VMEM((2, width, width), f32)],
        compiler_params=params(mean, grad, w_self, *nears),
        cost_estimate=cost(1300),
        name="weight",
    )(place, mean, grad, w_self, *nears)


def backward_kernel(n_row, n_part, n_after, place_ref, adjacency_ref, mine_ref, other_ref, *refs):
    refs = refs[n_after:]
    outs, up_ref = refs[:n_row], refs[n_row]
    rows = outs[0].shape[0]
    row, col = place_ref[0], place_ref[1]
    for h in range(n_part):
        here = pl.ds(h * rows, rows)
        up_ref[span(jnp.bitwise_xor(col, 2 * h), rows), :] = mine_ref[here, :]
        up_ref[span(jnp.bitwise_xor(col, 2 * h + 1), rows), :] = other_ref[here, :]
    for d in list(range(1, n_row)) + [0]:
        block = adjacency_ref[span(jnp.bitwise_xor(row, d), rows), :]
        outs[d][...] = mm(block, up_ref[...]).astype(outs[d].dtype)


def backward(place, adjacency, mine, other, after, n_row, n_part):
    rows = mine.shape[0] // n_part
    width = mine.shape[1]
    shapes = [jax.ShapeDtypeStruct((rows, width), f32)]
    shapes += [jax.ShapeDtypeStruct((rows, width), bf16)] * (n_row - 1)
    return pl.pallas_call(
        functools.partial(backward_kernel, n_row, n_part, len(after)),
        out_shape=shapes,
        in_specs=[SMEM] + [VMEM] * 3 + [ANY] * len(after),
        out_specs=[VMEM] * n_row,
        scratch_shapes=[pltpu.VMEM((2 * n_part * rows, width), bf16)],
        compiler_params=params(adjacency, mine, other, mine, other, *shapes),
        cost_estimate=cost(1800),
        name="backward",
    )(place, adjacency, mine, other, *after)


def exchange(value, axis, distance):
    size = lax.axis_size(axis)
    return lax.ppermute(value, axis, [(i, i ^ distance) for i in range(size)])


def layer(features, grad_out, degrees, w_self, w_neigh, bias, tile_slots, tile_count, tile_masks):
    rows, width = features.shape
    n_row, n_col = lax.axis_size("row"), lax.axis_size("col")
    n_part = n_col // 2
    row, col = lax.axis_index("row"), lax.axis_index("col")
    place = jnp.stack([row, col]).astype(jnp.int32)
    tiles = (tile_slots[0, 0], tile_count[0], tile_masks[0, 0])
    panel, group = rows * n_row, rows * n_col
    both = 2 * panel * group * 2 <= BOTH_FORMS_BYTES

    blocks = [features] + [None] * (n_row - 1)
    far = sorted(range(2, n_row, 2), key=lambda d: (-(d & -d), d))
    for d in far:
        blocks[d] = exchange(features, "row", d)
    blocks[1] = exchange(features, "row", 1)
    for d in far:
        blocks[d ^ 1] = exchange(blocks[d], "row", 1)
    near = pack_near(degrees, features, grad_out)
    nears = [near] + [exchange(near, "col", 2 * h) for h in range(1, n_part)]

    dense = unpack(both, tiles, [place], panel, group)
    mine, other = forward(place, dense, both, blocks, nears[1:], n_col)
    other = exchange(other, "col", 1)
    pair = (mine + other.astype(f32)).astype(bf16)
    sums = [pair] + [exchange(pair, "col", 2 * h) for h in range(1, n_part)]
    if both:
        dense = unpack(False, tiles, [pair], panel, group)

    layer_out, mean, grad, up = node(sums, nears, w_self, w_neigh, bias.reshape(1, width))
    up_other = exchange(up, "col", 1)
    keep, send, base = weight(place, mean, grad, w_self, nears)
    rounded = (keep + exchange(send, "col", 1).astype(f32)).astype(bf16)
    backs = backward(place, dense, up, up_other, [rounded], n_row, n_part)

    total = base + backs[0].astype(f32)
    pairs = {}
    for d in far + [0]:
        came = exchange(backs[d ^ 1], "row", 1).astype(f32)
        pairs[d] = backs[d].astype(f32) + came if d else total + came
    total = pairs[0]
    for d in far:
        total = total + exchange(pairs[d].astype(bf16), "row", d).astype(f32)
    grad_in = total.astype(bf16)

    distances = [1]
    distance = n_row // 2
    while distance > 1:
        distances.append(distance)
        distance //= 2
    for distance in distances:
        came = exchange(rounded, "row", distance)
        grads = rounded.astype(f32) + came.astype(f32)
        rounded = grads.astype(bf16)
    grads = grads * (1.0 / math.sqrt(panel * n_col))
    slices = [grads] + [exchange(grads, "col", 2 * h) for h in range(1, n_part)]
    part = lax.div(col, 2)
    ordered = []
    for p in range(n_part):
        chosen = slices[0]
        for h in range(1, n_part):
            chosen = jnp.where(jnp.bitwise_xor(part, h) == p, slices[h], chosen)
        ordered.append(chosen)
    grads = jnp.concatenate(ordered, axis=0)
    other_grads = exchange(grads, "col", 1)
    first = lax.rem(col, 2) == 0
    grad_self = jnp.where(first, grads, other_grads)
    grad_neigh = jnp.where(first, other_grads, grads)
    return layer_out, grad_in, grad_self, grad_neigh


def solution(mesh):
    placed = (
        P(("row", "col"), None),
        P(("row", "col"), None),
        P(("row", "col")),
        P(),
        P(),
        P(),
        P("row", "col", None),
        P("row", "col"),
        P("row", "col", None, None, None),
    )
    return jax.shard_map(
        layer,
        mesh=mesh,
        in_specs=placed,
        out_specs=(P(("row", "col"), None), P(("row", "col"), None), P(), P()),
        check_vma=False,
    )
```

profile of v0, /device:TPU:0, one launch (start us, length us, event | category | flops | bytes accessed | tf_op | source)
XLA Modules:
  0.0 80.2 jit_solution(656306143329972592)
XLA Ops:
  0.6 3.0 %collective-permute-start = (bf16[256,256]{1,0:T(8,128)(2,1)}, bf16[256,256]{1,0:T(8,128)(2,1)S(1)}, u32[]{:S(2)}, u32[]{:S(2)}) collective-permute-start(bf16[256,256]{1,0:T(8,128)(2,1)} %refs_0_.1), channel_id=1, source_target_pairs={{0,4},{4,0},{8,12},{12,8},{16,20},{20,16},{24,28},{28,24},{1,5},{5... | collective-permute-start | bytes 393224 | tf_op jit(solution)/shard_map/ppermute | solution.py:261
  3.7 1.6 %collective-permute-start.1 = (bf16[256,256]{1,0:T(8,128)(2,1)}, bf16[256,256]{1,0:T(8,128)(2,1)S(1)}, u32[]{:S(2)}, u32[]{:S(2)}) collective-permute-start(bf16[256,256]{1,0:T(8,128)(2,1)} %refs_0_.1), channel_id=1, source_target_pairs={{0,8},{4,12},{8,0},{12,4},{16,24},{20,28},{24,16},{28,20},{1,9},{5... | collective-permute-start | bytes 393224 | tf_op jit(solution)/shard_map/ppermute | solution.py:261
  5.2 2.6 %collective-permute-start.3 = (bf16[256,256]{1,0:T(8,128)(2,1)}, bf16[256,256]{1,0:T(8,128)(2,1)S(1)}, u32[]{:S(2)}, u32[]{:S(2)}) collective-permute-start(bf16[256,256]{1,0:T(8,128)(2,1)} %refs_0_.1), channel_id=1, source_target_pairs={{0,16},{4,20},{8,24},{12,28},{16,0},{20,4},{24,8},{28,12},{1,17},{... | collective-permute-start | bytes 393224 | tf_op jit(solution)/shard_map/ppermute | solution.py:261
  7.8 0.2 collective-permute-start.5
  8.1 0.9 %copy-done.2 = bf16[256,256]{1,0:T(8,128)(2,1)S(1)} copy-done((bf16[256,256]{1,0:T(8,128)(2,1)S(1)}, bf16[256,256]{1,0:T(8,128)(2,1)}, u32[]{:S(2)}) %copy-start.2) | copy-done | bytes 131096
  9.0 0.9 %copy-done.3 = bf16[256,256]{1,0:T(8,128)(2,1)S(1)} copy-done((bf16[256,256]{1,0:T(8,128)(2,1)S(1)}, bf16[256,256]{1,0:T(8,128)(2,1)}, u32[]{:S(2)}) %copy-start.3) | copy-done | bytes 131096
  9.9 0.7 copy-done.7
  10.6 1.6 %collective-permute-start.7 = (bf16[528,256]{1,0:T(8,128)(2,1)S(1)}, bf16[528,256]{1,0:T(8,128)(2,1)S(1)}, u32[]{:S(2)}, u32[]{:S(2)}) collective-permute-start(bf16[528,256]{1,0:T(8,128)(2,1)S(1)} %near.1.refs_2_.refs_0_), channel_id=1, source_target_pairs={{0,2},{1,3},{2,0},{3,1},{4,6},{5,7},{6,4},{7,5},{8,10},{9,11},{10,... | collective-permute-start | bytes 811016 | tf_op jit(solution)/shard_map/ppermute | solution.py:261
  12.8 0.1 pad_add_fusion.refs_0_.place_ref
  12.9 0.0 collective-permute-done.1.refs_2_
  12.9 0.5 collective-permute-start.2
  13.4 4.7 %collective-permute-done.3.refs_4_ = bf16[256,256]{1,0:T(8,128)(2,1)S(1)} collective-permute-done((bf16[256,256]{1,0:T(8,128)(2,1)}, bf16[256,256]{1,0:T(8,128)(2,1)S(1)}, u32[]{:S(2)}, u32[]{:S(2)}) %collective-permute-start.3) | collective-permute-done | bytes 131104 | tf_op jit(solution)/shard_map/ppermute | solution.py:261
  18.1 0.5 collective-permute-start.4
  18.6 0.0 collective-permute-done.5.refs_6_
  18.6 1.5 %collective-permute-start.6 = (bf16[256,256]{1,0:T(8,128)(2,1)S(1)}, bf16[256,256]{1,0:T(8,128)(2,1)S(1)}, u32[]{:S(2)}, u32[]{:S(2)}) collective-permute-start(bf16[256,256]{1,0:T(8,128)(2,1)S(1)} %collective-permute-done.5.refs_6_), channel_id=1, source_target_pairs={{0,4},{4,0},{8,12},{12,8},{16,20},{20,16},{24,28},{28,24},{1,5},{5... | collective-permute-start | bytes 393224 | tf_op jit(solution)/shard_map/ppermute | solution.py:261
  20.1 1.1 %copy-done = s32[1,1,88,16,128]{4,3,2,1,0:T(8,128)S(1)} copy-done((s32[1,1,88,16,128]{4,3,2,1,0:T(8,128)S(1)}, s32[1,1,88,16,128]{4,3,2,1,0:T(8,128)}, u32[]{:S(2)}) %copy-start) | copy-done | bytes 720920
  21.2 0.7 copy-done.9
  21.9 10.6 %unpack_gather.1.adjacency_ref = bf16[1024,2048]{1,0:T(8,128)(2,1)S(1)} custom-call(s32[88]{0:T(128)S(1)} %bitcast.13, s32[1]{0:T(128)} %bitcast.7.count_ref, s32[88,16,128]{2,1,0:T(8,128)S(1)} %bitcast.9, s32[2]{0:T(128)S(1)} %pad_add_fusion.refs_0_.place_ref), custom_call_target="tpu_custom_call" | custom-call | flops 4000000000 | tf_op jit(solution)/shard_map/unpack_gather/pallas_call | solution.py:78
  32.5 0.0 copy-start.5
  32.5 0.0 copy-start.6
  32.5 0.0 copy-start.8
  32.5 0.0 collective-permute-done.refs_1_
  32.5 0.0 collective-permute-done.2.refs_3_
  32.5 0.0 collective-permute-done.4.refs_5_
  32.5 0.0 collective-permute-done.6.refs_7_
  32.5 0.0 collective-permute-done.7.refs_8_.refs_3_.refs_1_
  32.6 1.9 %forward.1 = (f32[512,256]{1,0:T(8,128)S(1)}, bf16[512,256]{1,0:T(8,128)(2,1)S(1)}) custom-call(s32[2]{0:T(128)S(1)} %pad_add_fusion.refs_0_.place_ref, bf16[1024,2048]{1,0:T(8,128)(2,1)S(1)} %unpack_gather.1.adjacency_ref, bf16[256,256]{1,0:T(8,128)(2,1)S(1)} %copy-done.4, bf16[256,256]{1,0:T(8,128)(2,1)S(1)} %collective-permute-done.refs_1_, ...), custom_call_target="tpu_custom_call" | custom-call | flops 2200000000 | tf_op jit(solution)/shard_map/forward/pallas_call | solution.py:135
  34.4 0.1 collective-permute-start.8
  34.5 1.5 %collective-permute-done.8 = bf16[512,256]{1,0:T(8,128)(2,1)S(1)} collective-permute-done((bf16[512,256]{1,0:T(8,128)(2,1)S(1)}, bf16[512,256]{1,0:T(8,128)(2,1)S(1)}, u32[]{:S(2)}, u32[]{:S(2)}) %collective-permute-start.8) | collective-permute-done | bytes 262176 | tf_op jit(solution)/shard_map/ppermute | solution.py:261
  36.0 0.1 add_convert_fusion.refs_0_
  36.1 1.6 %collective-permute-start.9 = (bf16[512,256]{1,0:T(8,128)(2,1)S(1)}, bf16[512,256]{1,0:T(8,128)(2,1)S(1)}, u32[]{:S(2)}, u32[]{:S(2)}) collective-permute-start(bf16[512,256]{1,0:T(8,128)(2,1)S(1)} %add_convert_fusion.refs_0_), channel_id=1, source_target_pairs={{0,2},{1,3},{2,0},{3,1},{4,6},{5,7},{6,4},{7,5},{8,10},{9,11},{10,... | collective-permute-start | bytes 786440 | tf_op jit(solution)/shard_map/ppermute | solution.py:261
  37.7 6.8 %collective-permute-done.9.refs_1_ = bf16[512,256]{1,0:T(8,128)(2,1)S(1)} collective-permute-done((bf16[512,256]{1,0:T(8,128)(2,1)S(1)}, bf16[512,256]{1,0:T(8,128)(2,1)S(1)}, u32[]{:S(2)}, u32[]{:S(2)}) %collective-permute-start.9) | collective-permute-done | bytes 262176 | tf_op jit(solution)/shard_map/ppermute | solution.py:261
  44.5 1.2 %node.1 = (bf16[256,256]{1,0:T(8,128)(2,1)}, bf16[512,256]{1,0:T(8,128)(2,1)S(1)}, bf16[512,256]{1,0:T(8,128)(2,1)S(1)}, bf16[512,256]{1,0:T(8,128)(2,1)S(1)}) custom-call(bf16[512,256]{1,0:T(8,128)(2,1)S(1)} %add_convert_fusion.refs_0_, bf16[512,256]{1,0:T(8,128)(2,1)S(1)} %collective-permute-done.9.refs_1_, bf16[528,256]{1,0:T(8,128)(2,1)S(1)} %near.1.refs_2_.refs_0_, ...), custom_call_target="tpu_custom_call" | custom-call | flops 2000000000 | tf_op jit(solution)/shard_map/node/pallas_call | solution.py:180
  45.8 0.9 %weight.1 = (f32[128,256]{1,0:T(8,128)S(1)}, bf16[128,256]{1,0:T(8,128)(2,1)S(1)}, f32[256,256]{1,0:T(8,128)S(1)}) custom-call(s32[2]{0:T(128)S(1)} %pad_add_fusion.refs_0_.place_ref, bf16[512,256]{1,0:T(8,128)(2,1)S(1)} %get-tuple-element.24.mean_ref, bf16[512,256]{1,0:T(8,128)(2,1)S(1)} %get-tuple-element.25.grad_ref, bf16[256,256]{1,0:T(8,128)(2,1)S(1)} %copy-done.6, ...), custom_call_target="tpu_custom_call" | custom-call | flops 1300000000 | tf_op jit(solution)/shard_map/weight/pallas_call | solution.py:212
  46.7 0.1 collective-permute-start.11
  46.8 1.2 %collective-permute-done.11 = bf16[128,256]{1,0:T(8,128)(2,1)S(1)} collective-permute-done((bf16[128,256]{1,0:T(8,128)(2,1)S(1)}, bf16[128,256]{1,0:T(8,128)(2,1)S(1)}, u32[]{:S(2)}, u32[]{:S(2)}) %collective-permute-start.11) | collective-permute-done | bytes 65568 | tf_op jit(solution)/shard_map/ppermute | solution.py:261
  48.0 0.1 collective-permute-start.19
  48.1 0.2 collective-permute-start.10
  48.3 4.0 %collective-permute-done.19 = bf16[128,256]{1,0:T(8,128)(2,1)S(1)} collective-permute-done((bf16[128,256]{1,0:T(8,128)(2,1)S(1)}, bf16[128,256]{1,0:T(8,128)(2,1)S(1)}, u32[]{:S(2)}, u32[]{:S(2)}) %collective-permute-start.19) | collective-permute-done | bytes 65568 | tf_op jit(solution)/shard_map/ppermute | solution.py:261
  52.4 0.1 collective-permute-start.20
  52.5 2.7 %unpack_spread.1.adjacency_ref = bf16[2048,1024]{1,0:T(8,128)(2,1)S(1)} custom-call(s32[88]{0:T(128)S(1)} %bitcast.14, s32[1]{0:T(128)} %bitcast.8.count_ref, s32[88,16,128]{2,1,0:T(8,128)S(1)} %bitcast.10, bf16[512,256]{1,0:T(8,128)(2,1)S(1)} %add_convert_fusion.refs_0_), custom_call_target="tpu_custom_call" | custom-call | flops 4000000000 | tf_op jit(solution)/shard_map/unpack_spread/pallas_call | solution.py:78
  55.1 2.9 %collective-permute-done.20 = bf16[128,256]{1,0:T(8,128)(2,1)S(1)} collective-permute-done((bf16[128,256]{1,0:T(8,128)(2,1)S(1)}, bf16[128,256]{1,0:T(8,128)(2,1)S(1)}, u32[]{:S(2)}, u32[]{:S(2)}) %collective-permute-start.20) | collective-permute-done | bytes 65568 | tf_op jit(solution)/shard_map/ppermute | solution.py:261
  58.0 0.1 collective-permute-start.21
  58.1 0.0 collective-permute-done.10.other_ref
  58.1 1.8 %backward.1 = (f32[256,256]{1,0:T(8,128)S(1)}, bf16[256,256]{1,0:T(8,128)(2,1)S(1)}, bf16[256,256]{1,0:T(8,128)(2,1)S(1)}, bf16[256,256]{1,0:T(8,128)(2,1)S(1)},...) custom-call(s32[2]{0:T(128)S(1)} %pad_add_fusion.refs_0_.place_ref, ...), custom_call_target="tpu_custom_call" | custom-call | flops 1800000000 | tf_op jit(solution)/shard_map/backward/pallas_call | solution.py:247
  60.0 1.4 %collective-permute-start.17 = (bf16[256,256]{1,0:T(8,128)(2,1)S(1)}, bf16[256,256]{1,0:T(8,128)(2,1)S(1)}, u32[]{:S(2)}, u32[]{:S(2)}) collective-permute-start(bf16[256,256]{1,0:T(8,128)(2,1)S(1)} %get-tuple-element.37), channel_id=1, source_target_pairs={{0,4},{4,0},{8,12},{12,8},{16,20},{20,16},{24,28},{28,24},{1,5},{5... | collective-permute-start | bytes 393224 | tf_op jit(solution)/shard_map/ppermute | solution.py:261
  61.4 0.7 collective-permute-start.15
  62.1 1.3 %collective-permute-start.13 = (bf16[256,256]{1,0:T(8,128)(2,1)S(1)}, bf16[256,256]{1,0:T(8,128)(2,1)S(1)}, u32[]{:S(2)}, u32[]{:S(2)}) collective-permute-start(bf16[256,256]{1,0:T(8,128)(2,1)S(1)} %get-tuple-element.33), channel_id=1, source_target_pairs={{0,4},{4,0},{8,12},{12,8},{16,20},{20,16},{24,28},{28,24},{1,5},{5... | collective-permute-start | bytes 393224 | tf_op jit(solution)/shard_map/ppermute | solution.py:261
  63.4 0.7 collective-permute-start.12
  64.1 1.8 %collective-permute-start.22 = (f32[128,256]{1,0:T(8,128)S(1)}, f32[128,256]{1,0:T(8,128)S(1)}, u32[]{:S(2)}, u32[]{:S(2)}) collective-permute-start(f32[128,256]{1,0:T(8,128)S(1)} %add_multiply_fusion), channel_id=1, source_target_pairs={{0,2},{1,3},{2,0},{3,1},{4,6},{5,7},{6,4},{7,5},{8,10},{9,11},{10,... | collective-permute-start | bytes 393224 | tf_op jit(solution)/shard_map/ppermute | solution.py:261
  65.9 0.5 collective-permute-done.17
  66.4 2.0 %collective-permute-start.18 = (bf16[256,256]{1,0:T(8,128)(2,1)S(1)}, bf16[256,256]{1,0:T(8,128)(2,1)S(1)}, u32[]{:S(2)}, u32[]{:S(2)}) collective-permute-start(bf16[256,256]{1,0:T(8,128)(2,1)S(1)} %add_convert_fusion.2), channel_id=1, source_target_pairs={{0,24},{4,28},{8,16},{12,20},{16,8},{20,12},{24,0},{28,4},{1,25},{... | collective-permute-start | bytes 393224 | tf_op jit(solution)/shard_map/ppermute | solution.py:261
  68.5 0.5 collective-permute-done.15
  69.0 1.8 %collective-permute-start.16 = (bf16[256,256]{1,0:T(8,128)(2,1)S(1)}, bf16[256,256]{1,0:T(8,128)(2,1)S(1)}, u32[]{:S(2)}, u32[]{:S(2)}) collective-permute-start(bf16[256,256]{1,0:T(8,128)(2,1)S(1)} %add_convert_fusion.3), channel_id=1, source_target_pairs={{0,8},{4,12},{8,0},{12,4},{16,24},{20,28},{24,16},{28,20},{1,9},{5... | collective-permute-start | bytes 393224 | tf_op jit(solution)/shard_map/ppermute | solution.py:261
  70.8 0.0 collective-permute-done.13
  70.8 2.5 %collective-permute-start.14 = (bf16[256,256]{1,0:T(8,128)(2,1)S(1)}, bf16[256,256]{1,0:T(8,128)(2,1)S(1)}, u32[]{:S(2)}, u32[]{:S(2)}) collective-permute-start(bf16[256,256]{1,0:T(8,128)(2,1)S(1)} %add_convert_fusion.4), channel_id=1, source_target_pairs={{0,16},{4,20},{8,24},{12,28},{16,0},{20,4},{24,8},{28,12},{1,17},{... | collective-permute-start | bytes 393224 | tf_op jit(solution)/shard_map/ppermute | solution.py:261
  73.4 0.1 collective-permute-start.23
  73.5 0.0 collective-permute-done.12
  73.5 0.1 collective-permute-done.18
  73.6 2.2 %collective-permute-done.16 = bf16[256,256]{1,0:T(8,128)(2,1)S(1)} collective-permute-done((bf16[256,256]{1,0:T(8,128)(2,1)S(1)}, bf16[256,256]{1,0:T(8,128)(2,1)S(1)}, u32[]{:S(2)}, u32[]{:S(2)}) %collective-permute-start.16) | collective-permute-done | bytes 131104 | tf_op jit(solution)/shard_map/ppermute | solution.py:261
  75.8 2.8 %collective-permute-done.14 = bf16[256,256]{1,0:T(8,128)(2,1)S(1)} collective-permute-done((bf16[256,256]{1,0:T(8,128)(2,1)S(1)}, bf16[256,256]{1,0:T(8,128)(2,1)S(1)}, u32[]{:S(2)}, u32[]{:S(2)}) %collective-permute-start.14) | collective-permute-done | bytes 131104 | tf_op jit(solution)/shard_map/ppermute | solution.py:261
  78.6 0.7 add_convert_fusion.1
  79.4 0.0 collective-permute-done.23
  79.4 0.8 %broadcast_select_fusion = (f32[256,256]{1,0:T(8,128)}, f32[256,256]{1,0:T(8,128)}) fusion(f32[256,256]{1,0:T(8,128)S(1)} %collective-permute-done.23, pred[]{:T(512)S(6)} %eq.9, f32[128,256]{1,0:T(8,128)S(1)} %get-tuple-element.41, f32[128,256]{1,0:T(8,128)S(1)} %get-tuple-element.40), kind=kLoop, calls=%fused_computation.10 | loop fusion | flops 196608 | bytes 1048577 | tf_op jit(solution)/shard_map/jit(_where)/select_n | solution.py:330
  (26 shorter events, 0.3 us)
Async XLA Ops:
  0.6 31.9 %collective-permute-start = (bf16[256,256]{1,0:T(8,128)(2,1)}, bf16[256,256]{1,0:T(8,128)(2,1)S(1)}, u32[]{:S(2)}, u32[]{:S(2)}) collective-permute-start(bf16[256,256]{1,0:T(8,128)(2,1)} %refs_0_.1), channel_id=1, source_target_pairs={{0,4},{4,0},{8,12},{12,8},{16,20},{20,16},{24,28},{28,24},{1,5},{5... | collective-permute-start | bytes 393224 | tf_op jit(solution)/shard_map/ppermute | solution.py:261
  3.7 9.2 %collective-permute-start.1 = (bf16[256,256]{1,0:T(8,128)(2,1)}, bf16[256,256]{1,0:T(8,128)(2,1)S(1)}, u32[]{:S(2)}, u32[]{:S(2)}) collective-permute-start(bf16[256,256]{1,0:T(8,128)(2,1)} %refs_0_.1), channel_id=1, source_target_pairs={{0,8},{4,12},{8,0},{12,4},{16,24},{20,28},{24,16},{28,20},{1,9},{5... | collective-permute-start | bytes 393224 | tf_op jit(solution)/shard_map/ppermute | solution.py:261
  5.2 12.9 %collective-permute-start.3 = (bf16[256,256]{1,0:T(8,128)(2,1)}, bf16[256,256]{1,0:T(8,128)(2,1)S(1)}, u32[]{:S(2)}, u32[]{:S(2)}) collective-permute-start(bf16[256,256]{1,0:T(8,128)(2,1)} %refs_0_.1), channel_id=1, source_target_pairs={{0,16},{4,20},{8,24},{12,28},{16,0},{20,4},{24,8},{28,12},{1,17},{... | collective-permute-start | bytes 393224 | tf_op jit(solution)/shard_map/ppermute | solution.py:261
  7.8 10.8 %collective-permute-start.5 = (bf16[256,256]{1,0:T(8,128)(2,1)}, bf16[256,256]{1,0:T(8,128)(2,1)S(1)}, u32[]{:S(2)}, u32[]{:S(2)}) collective-permute-start(bf16[256,256]{1,0:T(8,128)(2,1)} %refs_0_.1), channel_id=1, source_target_pairs={{0,24},{4,28},{8,16},{12,20},{16,8},{20,12},{24,0},{28,4},{1,25},{... | collective-permute-start | bytes 393224 | tf_op jit(solution)/shard_map/ppermute | solution.py:261
  8.1 0.9 %copy-start.2 = (bf16[256,256]{1,0:T(8,128)(2,1)S(1)}, bf16[256,256]{1,0:T(8,128)(2,1)}, u32[]{:S(2)}) copy-start(bf16[256,256]{1,0:T(8,128)(2,1)} %cotangents_ref.1) | copy-start | bytes 393220
  9.0 0.9 %copy-start.3 = (bf16[256,256]{1,0:T(8,128)(2,1)S(1)}, bf16[256,256]{1,0:T(8,128)(2,1)}, u32[]{:S(2)}) copy-start(bf16[256,256]{1,0:T(8,128)(2,1)} %refs_0_.1) | copy-start | bytes 393220
  9.9 0.7 copy-start.7
  10.6 22.0 %collective-permute-start.7 = (bf16[528,256]{1,0:T(8,128)(2,1)S(1)}, bf16[528,256]{1,0:T(8,128)(2,1)S(1)}, u32[]{:S(2)}, u32[]{:S(2)}) collective-permute-start(bf16[528,256]{1,0:T(8,128)(2,1)S(1)} %near.1.refs_2_.refs_0_), channel_id=1, source_target_pairs={{0,2},{1,3},{2,0},{3,1},{4,6},{5,7},{6,4},{7,5},{8,10},{9,11},{10,... | collective-permute-start | bytes 811016 | tf_op jit(solution)/shard_map/ppermute | solution.py:261
  12.9 19.6 %collective-permute-start.2 = (bf16[256,256]{1,0:T(8,128)(2,1)S(1)}, bf16[256,256]{1,0:T(8,128)(2,1)S(1)}, u32[]{:S(2)}, u32[]{:S(2)}) collective-permute-start(bf16[256,256]{1,0:T(8,128)(2,1)S(1)} %collective-permute-done.1.refs_2_), channel_id=1, source_target_pairs={{0,4},{4,0},{8,12},{12,8},{16,20},{20,16},{24,28},{28,24},{1,5},{5... | collective-permute-start | bytes 393224 | tf_op jit(solution)/shard_map/ppermute | solution.py:261
  18.1 14.4 %collective-permute-start.4 = (bf16[256,256]{1,0:T(8,128)(2,1)S(1)}, bf16[256,256]{1,0:T(8,128)(2,1)S(1)}, u32[]{:S(2)}, u32[]{:S(2)}) collective-permute-start(bf16[256,256]{1,0:T(8,128)(2,1)S(1)} %collective-permute-done.3.refs_4_), channel_id=1, source_target_pairs={{0,4},{4,0},{8,12},{12,8},{16,20},{20,16},{24,28},{28,24},{1,5},{5... | collective-permute-start | bytes 393224 | tf_op jit(solution)/shard_map/ppermute | solution.py:261
  18.6 13.9 %collective-permute-start.6 = (bf16[256,256]{1,0:T(8,128)(2,1)S(1)}, bf16[256,256]{1,0:T(8,128)(2,1)S(1)}, u32[]{:S(2)}, u32[]{:S(2)}) collective-permute-start(bf16[256,256]{1,0:T(8,128)(2,1)S(1)} %collective-permute-done.5.refs_6_), channel_id=1, source_target_pairs={{0,4},{4,0},{8,12},{12,8},{16,20},{20,16},{24,28},{28,24},{1,5},{5... | collective-permute-start | bytes 393224 | tf_op jit(solution)/shard_map/ppermute | solution.py:261
  20.1 1.1 %copy-start = (s32[1,1,88,16,128]{4,3,2,1,0:T(8,128)S(1)}, s32[1,1,88,16,128]{4,3,2,1,0:T(8,128)}, u32[]{:S(2)}) copy-start(s32[1,1,88,16,128]{4,3,2,1,0:T(8,128)} %param.17) | copy-start | bytes 2162692
  21.2 0.7 copy-start.9
  21.9 10.7 %copy-start.4 = (bf16[256,256]{1,0:T(8,128)(2,1)S(1)}, bf16[256,256]{1,0:T(8,128)(2,1)}, u32[]{:S(2)}) copy-start(bf16[256,256]{1,0:T(8,128)(2,1)} %refs_0_.1) | copy-start | bytes 393220
  32.5 12.0 %copy-start.5 = (bf16[256,256]{1,0:T(8,128)(2,1)S(1)}, bf16[256,256]{1,0:T(8,128)(2,1)}, u32[]{:S(2)}) copy-start(bf16[256,256]{1,0:T(8,128)(2,1)} %refs_5_.1) | copy-start | bytes 393220
  32.5 12.0 %copy-start.6 = (bf16[256,256]{1,0:T(8,128)(2,1)S(1)}, bf16[256,256]{1,0:T(8,128)(2,1)}, u32[]{:S(2)}) copy-start(bf16[256,256]{1,0:T(8,128)(2,1)} %w_self.1) | copy-start | bytes 393220
  32.5 12.0 %copy-start.8 = (f32[256]{0:T(256)S(1)}, f32[256]{0:T(256)}, u32[]{:S(2)}) copy-start(f32[256]{0:T(256)} %param.14) | copy-start | bytes 3076
  34.4 1.6 %collective-permute-start.8 = (bf16[512,256]{1,0:T(8,128)(2,1)S(1)}, bf16[512,256]{1,0:T(8,128)(2,1)S(1)}, u32[]{:S(2)}, u32[]{:S(2)}) collective-permute-start(bf16[512,256]{1,0:T(8,128)(2,1)S(1)} %get-tuple-element.22), channel_id=1, source_target_pairs={{0,1},{1,0},{2,3},{3,2},{4,5},{5,4},{6,7},{7,6},{8,9},{9,8},{10,11... | collective-permute-start | bytes 786440 | tf_op jit(solution)/shard_map/ppermute | solution.py:261
  36.1 8.4 %collective-permute-start.9 = (bf16[512,256]{1,0:T(8,128)(2,1)S(1)}, bf16[512,256]{1,0:T(8,128)(2,1)S(1)}, u32[]{:S(2)}, u32[]{:S(2)}) collective-permute-start(bf16[512,256]{1,0:T(8,128)(2,1)S(1)} %add_convert_fusion.refs_0_), channel_id=1, source_target_pairs={{0,2},{1,3},{2,0},{3,1},{4,6},{5,7},{6,4},{7,5},{8,10},{9,11},{10,... | collective-permute-start | bytes 786440 | tf_op jit(solution)/shard_map/ppermute | solution.py:261
  45.7 6.7 %copy-start.1 = (s32[1,1,88,16,128]{4,3,2,1,0:T(8,128)S(1)}, s32[1,1,88,16,128]{4,3,2,1,0:T(8,128)}, u32[]{:S(2)}) copy-start(s32[1,1,88,16,128]{4,3,2,1,0:T(8,128)} %param.17) | copy-start | bytes 2162692
  45.8 6.7 %copy-start.10 = (s32[1,1,88]{2,1,0:T(1,128)S(1)}, s32[1,1,88]{2,1,0:T(1,128)}, u32[]{:S(2)}) copy-start(s32[1,1,88]{2,1,0:T(1,128)} %param.15) | copy-start | bytes 1060
  46.7 1.3 %collective-permute-start.11 = (bf16[128,256]{1,0:T(8,128)(2,1)S(1)}, bf16[128,256]{1,0:T(8,128)(2,1)S(1)}, u32[]{:S(2)}, u32[]{:S(2)}) collective-permute-start(bf16[128,256]{1,0:T(8,128)(2,1)S(1)} %get-tuple-element.29), channel_id=1, source_target_pairs={{0,1},{1,0},{2,3},{3,2},{4,5},{5,4},{6,7},{7,6},{8,9},{9,8},{10,11... | collective-permute-start | bytes 196616 | tf_op jit(solution)/shard_map/ppermute | solution.py:261
  48.0 4.3 %collective-permute-start.19 = (bf16[128,256]{1,0:T(8,128)(2,1)S(1)}, bf16[128,256]{1,0:T(8,128)(2,1)S(1)}, u32[]{:S(2)}, u32[]{:S(2)}) collective-permute-start(bf16[128,256]{1,0:T(8,128)(2,1)S(1)} %add_convert_fusion.7.refs_0_), channel_id=1, source_target_pairs={{0,4},{4,0},{8,12},{12,8},{16,20},{20,16},{24,28},{28,24},{1,5},{5... | collective-permute-start | bytes 196616 | tf_op jit(solution)/shard_map/ppermute | solution.py:261
  48.1 10.0 %collective-permute-start.10 = (bf16[512,256]{1,0:T(8,128)(2,1)S(1)}, bf16[512,256]{1,0:T(8,128)(2,1)S(1)}, u32[]{:S(2)}, u32[]{:S(2)}) collective-permute-start(bf16[512,256]{1,0:T(8,128)(2,1)S(1)} %get-tuple-element.27.mine_ref), channel_id=1, source_target_pairs={{0,1},{1,0},{2,3},{3,2},{4,5},{5,4},{6,7},{7,6},{8,9},{9,8},{10,11... | collective-permute-start | bytes 786440 | tf_op jit(solution)/shard_map/ppermute | solution.py:261
  52.4 5.6 %collective-permute-start.20 = (bf16[128,256]{1,0:T(8,128)(2,1)S(1)}, bf16[128,256]{1,0:T(8,128)(2,1)S(1)}, u32[]{:S(2)}, u32[]{:S(2)}) collective-permute-start(bf16[128,256]{1,0:T(8,128)(2,1)S(1)} %add_convert_fusion.6), channel_id=1, source_target_pairs={{0,16},{4,20},{8,24},{12,28},{16,0},{20,4},{24,8},{28,12},{1,17},{... | collective-permute-start | bytes 196616 | tf_op jit(solution)/shard_map/ppermute | solution.py:261
  58.0 6.0 %collective-permute-start.21 = (bf16[128,256]{1,0:T(8,128)(2,1)S(1)}, bf16[128,256]{1,0:T(8,128)(2,1)S(1)}, u32[]{:S(2)}, u32[]{:S(2)}) collective-permute-start(bf16[128,256]{1,0:T(8,128)(2,1)S(1)} %add_convert_fusion.5), channel_id=1, source_target_pairs={{0,8},{4,12},{8,0},{12,4},{16,24},{20,28},{24,16},{28,20},{1,9},{5... | collective-permute-start | bytes 196616 | tf_op jit(solution)/shard_map/ppermute | solution.py:261
  60.0 6.4 %collective-permute-start.17 = (bf16[256,256]{1,0:T(8,128)(2,1)S(1)}, bf16[256,256]{1,0:T(8,128)(2,1)S(1)}, u32[]{:S(2)}, u32[]{:S(2)}) collective-permute-start(bf16[256,256]{1,0:T(8,128)(2,1)S(1)} %get-tuple-element.37), channel_id=1, source_target_pairs={{0,4},{4,0},{8,12},{12,8},{16,20},{20,16},{24,28},{28,24},{1,5},{5... | collective-permute-start | bytes 393224 | tf_op jit(solution)/shard_map/ppermute | solution.py:261
  61.4 7.6 %collective-permute-start.15 = (bf16[256,256]{1,0:T(8,128)(2,1)S(1)}, bf16[256,256]{1,0:T(8,128)(2,1)S(1)}, u32[]{:S(2)}, u32[]{:S(2)}) collective-permute-start(bf16[256,256]{1,0:T(8,128)(2,1)S(1)} %get-tuple-element.35), channel_id=1, source_target_pairs={{0,4},{4,0},{8,12},{12,8},{16,20},{20,16},{24,28},{28,24},{1,5},{5... | collective-permute-start | bytes 393224 | tf_op jit(solution)/shard_map/ppermute | solution.py:261
  62.1 8.7 %collective-permute-start.13 = (bf16[256,256]{1,0:T(8,128)(2,1)S(1)}, bf16[256,256]{1,0:T(8,128)(2,1)S(1)}, u32[]{:S(2)}, u32[]{:S(2)}) collective-permute-start(bf16[256,256]{1,0:T(8,128)(2,1)S(1)} %get-tuple-element.33), channel_id=1, source_target_pairs={{0,4},{4,0},{8,12},{12,8},{16,20},{20,16},{24,28},{28,24},{1,5},{5... | collective-permute-start | bytes 393224 | tf_op jit(solution)/shard_map/ppermute | solution.py:261
  63.4 10.1 %collective-permute-start.12 = (bf16[256,256]{1,0:T(8,128)(2,1)S(1)}, bf16[256,256]{1,0:T(8,128)(2,1)S(1)}, u32[]{:S(2)}, u32[]{:S(2)}) collective-permute-start(bf16[256,256]{1,0:T(8,128)(2,1)S(1)} %get-tuple-element.31), channel_id=1, source_target_pairs={{0,4},{4,0},{8,12},{12,8},{16,20},{20,16},{24,28},{28,24},{1,5},{5... | collective-permute-start | bytes 393224 | tf_op jit(solution)/shard_map/ppermute | solution.py:261
  64.1 9.2 %collective-permute-start.22 = (f32[128,256]{1,0:T(8,128)S(1)}, f32[128,256]{1,0:T(8,128)S(1)}, u32[]{:S(2)}, u32[]{:S(2)}) collective-permute-start(f32[128,256]{1,0:T(8,128)S(1)} %add_multiply_fusion), channel_id=1, source_target_pairs={{0,2},{1,3},{2,0},{3,1},{4,6},{5,7},{6,4},{7,5},{8,10},{9,11},{10,... | collective-permute-start | bytes 393224 | tf_op jit(solution)/shard_map/ppermute | solution.py:261
  66.4 7.2 %collective-permute-start.18 = (bf16[256,256]{1,0:T(8,128)(2,1)S(1)}, bf16[256,256]{1,0:T(8,128)(2,1)S(1)}, u32[]{:S(2)}, u32[]{:S(2)}) collective-permute-start(bf16[256,256]{1,0:T(8,128)(2,1)S(1)} %add_convert_fusion.2), channel_id=1, source_target_pairs={{0,24},{4,28},{8,16},{12,20},{16,8},{20,12},{24,0},{28,4},{1,25},{... | collective-permute-start | bytes 393224 | tf_op jit(solution)/shard_map/ppermute | solution.py:261
  69.0 6.9 %collective-permute-start.16 = (bf16[256,256]{1,0:T(8,128)(2,1)S(1)}, bf16[256,256]{1,0:T(8,128)(2,1)S(1)}, u32[]{:S(2)}, u32[]{:S(2)}) collective-permute-start(bf16[256,256]{1,0:T(8,128)(2,1)S(1)} %add_convert_fusion.3), channel_id=1, source_target_pairs={{0,8},{4,12},{8,0},{12,4},{16,24},{20,28},{24,16},{28,20},{1,9},{5... | collective-permute-start | bytes 393224 | tf_op jit(solution)/shard_map/ppermute | solution.py:261
  70.8 7.8 %collective-permute-start.14 = (bf16[256,256]{1,0:T(8,128)(2,1)S(1)}, bf16[256,256]{1,0:T(8,128)(2,1)S(1)}, u32[]{:S(2)}, u32[]{:S(2)}) collective-permute-start(bf16[256,256]{1,0:T(8,128)(2,1)S(1)} %add_convert_fusion.4), channel_id=1, source_target_pairs={{0,16},{4,20},{8,24},{12,28},{16,0},{20,4},{24,8},{28,12},{1,17},{... | collective-permute-start | bytes 393224 | tf_op jit(solution)/shard_map/ppermute | solution.py:261
  73.4 6.0 %collective-permute-start.23 = (f32[256,256]{1,0:T(8,128)S(1)}, f32[256,256]{1,0:T(8,128)S(1)}, u32[]{:S(2)}, u32[]{:S(2)}) collective-permute-start(f32[256,256]{1,0:T(8,128)S(1)} %pad_maximum_fusion), channel_id=1, source_target_pairs={{0,1},{1,0},{2,3},{3,2},{4,5},{5,4},{6,7},{7,6},{8,9},{9,8},{10,11... | collective-permute-start | bytes 786440 | tf_op jit(solution)/shard_map/ppermute | solution.py:261
where the time goes:
time: 80.4 us; the launch traced here: 80.2 us
  waiting for transfers between devices  27.3 us (34%)
  starting transfers between devices  26.1 us (32%)
  Pallas kernels  19.1 us (24%)
  local copies, waits for them, and re-layouts  4.28 us (5%)
  other arithmetic  1.93 us (2%)
  between operations  1.56 us (2%)
    ppermute x24, waiting for transfers between devices, exchange(): return lax.ppermute(value, axis, [(i, i ^ distance) for i in range(size)])  27.3 us
    ppermute x24, starting transfers between devices, exchange(): return lax.ppermute(value, axis, [(i, i ^ distance) for i in range(size)])  26.1 us
    pallas_call x2, Pallas kernels, unpack(): pl.pallas_call(functools.partial(unpack_kernel, block_rows, gather), out_...  13.2 us
    unnamed x22, local copies, waits for them, and re-layouts  4.28 us
    pallas_call x1, Pallas kernels, forward(): pl.pallas_call(functools.partial(forward_kernel, n_row, n_col, natural, l...  1.86 us
    pallas_call x1, Pallas kernels, backward(): pl.pallas_call(functools.partial(backward_kernel, n_row, n_part, len(afte...  1.83 us
  transfers between devices with their start and end apart: 24, of which 11 were waited for; matrix products, arithmetic and copies ran while one was open for 1% of the time, Pallas kernels for 19%

commit v1 on v0

v1 whole, which is shorter than its diff:
```python
import functools
import math

import jax
import jax.numpy as jnp
from jax import lax
from jax.experimental import pallas as pl
from jax.experimental.pallas import tpu as pltpu
from jax.sharding import PartitionSpec as P


BOTH_FORMS_BYTES = 8 * 1024 * 1024
DIGIT_ROWS = 16

VMEM = pl.BlockSpec(memory_space=pltpu.VMEM)
HBM = pl.BlockSpec(memory_space=pltpu.HBM)
ANY = pl.BlockSpec(memory_space=pl.ANY)
SMEM = pl.BlockSpec(memory_space=pltpu.SMEM)

f32 = jnp.float32
bf16 = jnp.bfloat16


def mm(a, b):
    return jnp.dot(a, b, preferred_element_type=f32)


def mm_nt(a, b):
    return lax.dot_general(a, b, (((1,), (1,)), ((), ())), preferred_element_type=f32)


def mm_tn(a, b):
    return lax.dot_general(a, b, (((0,), (0,)), ((), ())), preferred_element_type=f32)


def params(*arrays):
    held = sum(math.prod(array.shape) * jnp.dtype(array.dtype).itemsize for array in arrays)
    return pltpu.CompilerParams(vmem_limit_bytes=held + held // 8 + (4 << 20))


def in_hbm(array):
    return pltpu.with_memory_space_constraint(array, pltpu.HBM)


def cost(nanoseconds):
    return pl.CostEstimate(flops=nanoseconds * 10**6, bytes_accessed=0, transcendentals=0)


def span(index, size):
    return pl.ds(pl.multiple_of(index * size, size), size)


def unpack_kernel(block_rows, gather, split, place_ref, count_ref, slots_hbm, masks_hbm, *refs):
    if split:
        last_ref, refs = refs[-5], refs[:-5] + refs[-4:]
    dense_ref, slots_ref, masks_ref, slots_sem, masks_sem = refs[-5:]
    slots_copy = pltpu.make_async_copy(slots_hbm, slots_ref, slots_sem)
    masks_copy = pltpu.make_async_copy(masks_hbm, masks_ref, masks_sem)
    slots_copy.start()
    masks_copy.start()
    tiles, words, width = masks_ref.shape
    height, length = dense_ref.shape
    together = math.gcd(tiles, 8)

    @pl.loop(0, height // width)
    def _(step):
        dense_ref[span(step, width), :] = jnp.zeros((width, length), bf16)

    if split:

        @pl.loop(0, last_ref.shape[0] // width)
        def _(step):
            last_ref[span(step, width), :] = jnp.zeros((width, length), bf16)

    slots_copy.wait()
    masks_copy.wait()

    def blocks(tile):
        slot = slots_ref[0, tile]
        return lax.rem(slot, block_rows), lax.div(slot, block_rows)

    if not gather:
        shifts = lax.broadcasted_iota(jnp.int32, (words, 8, width), 1)

        @pl.loop(0, count_ref[0])
        def _(tile):
            row_block, column_block = blocks(tile)
            word = jnp.broadcast_to(masks_ref[tile][:, None, :], (words, 8, width))
            bits = jnp.bitwise_and(jnp.right_shift(word, shifts), 1)
            bits = bits.astype(f32).reshape(words * 8, width).astype(bf16)
            if not split:
                dense_ref[span(column_block, width), span(row_block, width)] = bits
                return
            own, within = lax.div(column_block, split), lax.rem(column_block, split)
            spot = jnp.bitwise_xor(place_ref[0], own) * split + within
            edge = height // width

            @pl.when(spot < edge)
            def _():
                dense_ref[span(spot, width), span(row_block, width)] = bits

            @pl.when(spot >= edge)
            def _():
                last_ref[span(spot - edge, width), span(row_block, width)] = bits

        return

    stacked = together * words
    source = lax.broadcasted_iota(jnp.int32, (stacked, together * words * 8), 0)
    target = lax.broadcasted_iota(jnp.int32, (stacked, together * words * 8), 1)
    repeat = (source == lax.div(target, 8)).astype(f32).astype(bf16)
    shifts = lax.rem(lax.broadcasted_iota(jnp.int32, (width, words * 8), 1), 8)

    @pl.loop(0, lax.div(count_ref[0] + together - 1, together))
    def _(step):
        first = step * together
        live = [
            masks_ref[first + t] * (first + t < count_ref[0]).astype(jnp.int32)
            for t in range(together)
        ]
        turned = jnp.concatenate(live, axis=0).astype(f32).T.astype(bf16)
        word = mm(turned, repeat)
        for t in range(together):
            row_block, column_block = blocks(first + t)
            own = word[:, t * words * 8 : (t + 1) * words * 8].astype(jnp.int32)
            bits = jnp.bitwise_and(jnp.right_shift(own, shifts), 1).astype(f32).astype(bf16)
            dense_ref[span(row_block, width), span(column_block, width)] = bits


def unpack(gather, place, tiles, after, panel, group, rows=0):
    slot_ids, live_count, masks = tiles
    width = masks.shape[2]
    heights = [panel - 2 * rows, 2 * rows] if rows else [group if gather else panel]
    shapes = [jax.ShapeDtypeStruct((h, panel if gather else group), bf16) for h in heights]
    return pl.pallas_call(
        functools.partial(unpack_kernel, group // width, gather, rows // width),
        out_shape=shapes,
        in_specs=[SMEM, SMEM, HBM, HBM] + [ANY] * len(after),
        out_specs=[VMEM] * len(shapes),
        scratch_shapes=[
            pltpu.SMEM(slot_ids.shape, jnp.int32),
            pltpu.VMEM(masks.shape, jnp.int32),
            pltpu.SemaphoreType.DMA,
            pltpu.SemaphoreType.DMA,
        ],
        compiler_params=params(masks, *shapes),
        cost_estimate=cost(2000),
        name="unpack_gather" if gather else "unpack_spread",
    )(place, live_count, in_hbm(slot_ids), in_hbm(masks), *after)


def near_kernel(degrees_hbm, features_hbm, cotangents_hbm, near_ref, degrees_ref, sems):
    rows = features_hbm.shape[0]
    copies = [
        pltpu.make_async_copy(degrees_hbm, degrees_ref, sems.at[0]),
        pltpu.make_async_copy(features_hbm, near_ref.at[pl.ds(0, rows), :], sems.at[1]),
        pltpu.make_async_copy(cotangents_hbm, near_ref.at[pl.ds(rows, rows), :], sems.at[2]),
    ]
    for copy in copies:
        copy.start()
    copies[0].wait()
    degree = jnp.broadcast_to(degrees_ref[...], (DIGIT_ROWS, rows))
    place = lax.broadcasted_iota(jnp.int32, degree.shape, 0)
    digit = jnp.bitwise_and(jnp.right_shift(degree, 8 * jnp.minimum(place, 3)), 255)
    near_ref[pl.ds(2 * rows, DIGIT_ROWS), :] = digit.astype(f32).astype(bf16)
    copies[1].wait()
    copies[2].wait()


def pack_near(degrees, features, cotangents):
    rows, width = features.shape
    near = jax.ShapeDtypeStruct((2 * rows + DIGIT_ROWS, width), bf16)
    return pl.pallas_call(
        near_kernel,
        out_shape=near,
        in_specs=[HBM] * 3,
        out_specs=VMEM,
        scratch_shapes=[pltpu.VMEM((1, rows), jnp.int32), pltpu.SemaphoreType.DMA((3,))],
        compiler_params=params(near, near),
        cost_estimate=cost(500),
        name="near",
    )(in_hbm(degrees.reshape(1, rows)), in_hbm(features), in_hbm(cotangents))


def forward_kernel(distances, n_col, natural, last, place_ref, adjacency_ref, *refs):
    blocks, refs = refs[: len(distances)], refs[len(distances) :]
    rows = blocks[0].shape[0]
    row, col = place_ref[0], place_ref[1]
    for e in list(range(1, n_col, 2)) + list(range(0, n_col, 2)):
        own = span(jnp.bitwise_xor(col, e), rows)
        total = refs[0][pl.ds(e * rows, rows), :] if last else None
        for d, block in zip(distances, blocks):
            panel = span(jnp.bitwise_xor(row, d), rows)
            if natural:
                term = mm(adjacency_ref[own, panel], block[...])
            else:
                term = mm_tn(adjacency_ref[panel, own], block[...])
            total = term if total is None else total + term
        if last:
            out = refs[1 + e % 2]
            out[pl.ds((e // 2) * rows, rows), :] = total.astype(out.dtype)
        else:
            refs[0][pl.ds(e * rows, rows), :] = total


def forward(place, adjacency, natural, blocks, total, n_col):
    distances, arrays = list(blocks), list(blocks.values())
    rows, width = arrays[0].shape
    last = total is not None
    if last:
        half = rows * n_col // 2
        shapes = [jax.ShapeDtypeStruct((half, width), kind) for kind in (f32, bf16)]
    else:
        shapes = [jax.ShapeDtypeStruct((rows * n_col, width), f32)]
    inputs = arrays + ([total] if last else [])
    return pl.pallas_call(
        functools.partial(forward_kernel, distances, n_col, natural, last),
        out_shape=shapes,
        in_specs=[SMEM] + [VMEM] * (1 + len(inputs)),
        out_specs=[VMEM] * len(shapes),
        compiler_params=params(adjacency, *inputs, *shapes),
        cost_estimate=cost(250 * len(distances)),
        name="forward_last" if last else "forward",
    )(place, adjacency, *inputs)


def node_kernel(n_part, *refs):
    sums, refs = refs[:n_part], refs[n_part:]
    nears, refs = refs[:n_part], refs[n_part:]
    w_self, w_neigh, bias, out_ref, mean_ref, grad_ref, up_ref = refs
    rows = out_ref.shape[0]
    for h in range(n_part):
        parts = [sums[h2][pl.ds((h ^ h2) * rows, rows), :].astype(f32) for h2 in range(n_part)]
        while len(parts) > 1:
            parts = [parts[i] + parts[i + 1] for i in range(0, len(parts), 2)]
        digits = nears[h][pl.ds(2 * rows, DIGIT_ROWS), :].astype(f32)[:8, :]
        place = lax.broadcasted_iota(jnp.int32, digits.shape, 0)
        scales = jnp.where(place < 4, jnp.left_shift(1, 8 * jnp.minimum(place, 3)), 0).astype(f32)
        degree = jnp.sum((digits * scales).T, axis=1, keepdims=True)
        inverse = 1.0 / degree
        mean = (parts[0] * inverse).astype(bf16)
        preact = mm(nears[h][pl.ds(0, rows), :], w_self[...]) + mm(mean, w_neigh[...]) + bias[...]
        gate = jax.nn.sigmoid(preact)
        if h == 0:
            out_ref[...] = (preact * gate).astype(bf16)
        grad = nears[h][pl.ds(rows, rows), :].astype(f32) * gate * (1.0 + preact * (1.0 - gate))
        grad = grad.astype(bf16)
        here = pl.ds(h * rows, rows)
        mean_ref[here, :] = mean
        grad_ref[here, :] = grad
        up_ref[here, :] = (mm_nt(grad, w_neigh[...]) * inverse).astype(bf16)


def node(sums, nears, w_self, w_neigh, bias):
    n_part = len(sums)
    width = nears[0].shape[1]
    rows = sums[0].shape[0] // n_part
    all_rows = jax.ShapeDtypeStruct((rows * n_part, width), bf16)
    shapes = [jax.ShapeDtypeStruct((rows, width), bf16), all_rows, all_rows, all_rows]
    return pl.pallas_call(
        functools.partial(node_kernel, n_part),
        out_shape=shapes,
        in_specs=[VMEM] * (2 * n_part + 3),
        out_specs=[VMEM] * 4,
        compiler_params=params(*sums, *nears, w_self, w_neigh, *shapes),
        cost_estimate=cost(2000),
        name="node",
    )(*sums, *nears, w_self, w_neigh, bias)


def weight_kernel(n_part, place_ref, mean_ref, grad_ref, w_self, *refs):
    nears, (slice_ref, base_ref, total_ref) = refs[:n_part], refs[n_part:]
    rows = base_ref.shape[0]
    here = pl.ds(0, rows)
    grad_self = mm_tn(nears[0][here, :], grad_ref[here, :])
    for h in range(1, n_part):
        grad_self = grad_self + mm_tn(nears[h][here, :], grad_ref[pl.ds(h * rows, rows), :])
    grad_neigh = mm_tn(mean_ref[...], grad_ref[...])
    total_ref[0], total_ref[1] = grad_self, grad_neigh
    here = span(lax.div(place_ref[1], 2), slice_ref.shape[1])
    slice_ref[0] = total_ref[0, here, :].astype(bf16)
    slice_ref[1] = total_ref[1, here, :].astype(bf16)
    base_ref[...] = mm_nt(grad_ref[pl.ds(0, rows), :], w_self[...])


def weight(place, mean, grad, w_self, nears):
    n_part = len(nears)
    rows, width = mean.shape[0] // n_part, mean.shape[1]
    return pl.pallas_call(
        functools.partial(weight_kernel, n_part),
        out_shape=[
            jax.ShapeDtypeStruct((2, width // n_part, width), bf16),
            jax.ShapeDtypeStruct((rows, width), f32),
        ],
        in_specs=[SMEM] + [VMEM] * (3 + n_part),
        out_specs=[VMEM] * 2,
        scratch_shapes=[pltpu.VMEM((2, width, width), f32)],
        compiler_params=params(mean, grad, w_self, *nears),
        cost_estimate=cost(1300),
        name="weight",
    )(place, mean, grad, w_self, *nears)


def backward_kernel(distances, n_part, n_after, place_ref, adjacency_ref, mine_ref, other_ref, *refs):
    outs, up_ref = refs[n_after:-1], refs[-1]
    rows = outs[0].shape[0]
    row, col = place_ref[0], place_ref[1]
    for h in range(n_part):
        here = pl.ds(h * rows, rows)
        up_ref[span(jnp.bitwise_xor(col, 2 * h), rows), :] = mine_ref[here, :]
        up_ref[span(jnp.bitwise_xor(col, 2 * h + 1), rows), :] = other_ref[here, :]
    whole = adjacency_ref.shape[0] > len(distances) * rows
    for index, (d, out) in enumerate(zip(distances, outs)):
        if whole:
            block = adjacency_ref[span(jnp.bitwise_xor(row, d), rows), :]
        else:
            block = adjacency_ref[pl.ds(index * rows, rows), :]
        out[...] = mm(block, up_ref[...]).astype(out.dtype)


def backward(place, adjacency, mine, other, after, distances, n_part):
    rows = mine.shape[0] // n_part
    width = mine.shape[1]
    shapes = [jax.ShapeDtypeStruct((rows, width), bf16 if d else f32) for d in distances]
    outs = pl.pallas_call(
        functools.partial(backward_kernel, distances, n_part, len(after)),
        out_shape=shapes,
        in_specs=[SMEM] + [VMEM] * 3 + [ANY] * len(after),
        out_specs=[VMEM] * len(shapes),
        scratch_shapes=[pltpu.VMEM((2 * n_part * rows, width), bf16)],
        compiler_params=params(adjacency, mine, other, mine, other, *shapes),
        cost_estimate=cost(200 * len(distances)),
        name="backward" if 0 in distances else "backward_far",
    )(place, adjacency, mine, other, *after)
    return dict(zip(distances, outs))


def final_kernel(n_part, n_terms, scale, place_ref, *refs):
    terms, refs = refs[:n_terms], refs[n_terms:]
    mine, others, refs = refs[:n_part], refs[n_part : 2 * n_part], refs[2 * n_part :]
    grad_in_ref, self_ref, neigh_ref = refs
    total = terms[0][...]
    for term in terms[1:]:
        total = total + term[...].astype(f32)
    grad_in_ref[...] = total.astype(bf16)
    first = lax.rem(place_ref[1], 2) == 0
    for h in range(n_part):
        here = span(jnp.bitwise_xor(lax.div(place_ref[1], 2), h), mine[h].shape[0])
        one, two = mine[h][...] * scale, others[h][...] * scale
        self_ref[here, :] = jnp.where(first, one, two)
        neigh_ref[here, :] = jnp.where(first, two, one)


def final(place, terms, mine, others, scale):
    n_part = len(mine)
    rows, width = terms[0].shape
    shapes = [
        jax.ShapeDtypeStruct((rows, width), bf16),
        jax.ShapeDtypeStruct((width, width), f32),
        jax.ShapeDtypeStruct((width, width), f32),
    ]
    return pl.pallas_call(
        functools.partial(final_kernel, n_part, len(terms), scale),
        out_shape=shapes,
        in_specs=[SMEM] + [VMEM] * (len(terms) + 2 * n_part),
        out_specs=[VMEM] * 3,
        compiler_params=params(*terms, *mine, *others, *shapes),
        cost_estimate=cost(800),
        name="final",
    )(place, *terms, *mine, *others)


def exchange(value, axis, distance):
    size = lax.axis_size(axis)
    return lax.ppermute(value, axis, [(i, i ^ distance) for i in range(size)])


def layer(features, grad_out, degrees, w_self, w_neigh, bias, tile_slots, tile_count, tile_masks):
    rows, width = features.shape
    n_row, n_col = lax.axis_size("row"), lax.axis_size("col")
    n_part = n_col // 2
    row, col = lax.axis_index("row"), lax.axis_index("col")
    place = jnp.stack([row, col]).astype(jnp.int32)
    tiles = (tile_slots[0], tile_count[0], tile_masks[0, 0])
    panel, group = rows * n_row, rows * n_col
    both = 2 * panel * group * 2 <= BOTH_FORMS_BYTES

    blocks = [features] + [None] * (n_row - 1)
    far = sorted(range(2, n_row, 2), key=lambda d: (-(d & -d), d))
    for d in far:
        blocks[d] = exchange(features, "row", d)
    blocks[1] = exchange(features, "row", 1)
    for d in far:
        blocks[d ^ 1] = exchange(blocks[d], "row", 1)
    near = pack_near(degrees, features, grad_out)
    nears = [near] + [exchange(near, "col", 2 * h) for h in range(1, n_part)]

    (dense,) = unpack(both, place, tiles, [], panel, group)
    late = far[-1] ^ 1
    early = {d: blocks[d] for d in range(n_row) if d != late}
    (total,) = forward(place, dense, both, early, None, n_col)
    mine, other = forward(place, dense, both, {late: blocks[late]}, total, n_col)
    other = exchange(other, "col", 1)
    pair = (mine + other.astype(f32)).astype(bf16)
    sums = [pair] + [exchange(pair, "col", 2 * h) for h in range(1, n_part)]

    layer_out, mean, grad, up = node(sums, nears, w_self, w_neigh, bias.reshape(1, width))
    up_other = exchange(up, "col", 1)
    slices, base = weight(place, mean, grad, w_self, nears)
    every = list(range(n_row))
    if both:
        near_part, far_part = unpack(False, place, tiles, [pair], panel, group, rows)
        backs = backward(place, far_part, up, up_other, [slices], every[-2:], n_part)
        backs.update(backward(place, near_part, up, up_other, [], every[:-2], n_part))
    else:
        backs = backward(place, dense, up, up_other, [slices], every, n_part)

    terms = [base, backs[0]]
    for d in reversed(far):
        came = exchange(backs[d ^ 1], "row", 1)
        both_x = (backs[d].astype(f32) + came.astype(f32)).astype(bf16)
        terms.append(exchange(both_x, "row", d))
    terms.append(exchange(backs[1], "row", 1))

    sums = slices.astype(f32) + exchange(slices, "row", 1).astype(f32)
    core = lax.rem(col, 2) == 0
    keep = jnp.where(core, sums[0], sums[1])
    send = jnp.where(core, sums[1], sums[0]).astype(bf16)
    grads = keep + exchange(send, "col", 1).astype(f32)
    distance = n_row // 2
    while distance > 1:
        rounded = grads.astype(bf16)
        came = exchange(rounded, "row", distance)
        grads = rounded.astype(f32) + came.astype(f32)
        distance //= 2
    mine = [grads] + [exchange(grads, "col", 2 * h) for h in range(1, n_part)]
    others = [exchange(value, "col", 1) for value in mine]
    scale = 1.0 / math.sqrt(panel * n_col)
    grad_in, grad_self, grad_neigh = final(place, terms, mine, others, scale)
    return layer_out, grad_in, grad_self, grad_neigh


def solution(mesh):
    placed = (
        P(("row", "col"), None),
        P(("row", "col"), None),
        P(("row", "col")),
        P(),
        P(),
        P(),
        P("row", "col", None),
        P("row", "col"),
        P("row", "col", None, None, None),
    )
    return jax.shard_map(
        layer,
        mesh=mesh,
        in_specs=placed,
        out_specs=(P(("row", "col"), None), P(("row", "col"), None), P(), P()),
        check_vma=False,
    )
```

time: 80.4 us -> 84.8 us (1.055)
  waiting for transfers between devices: 27.3 us -> 38.9 us
  local copies, waits for them, and re-layouts: 4.28 us -> 0.03 us
  starting transfers between devices: 26.1 us -> 24.1 us
  other arithmetic: 1.93 us -> 0.34 us
    ppermute x24 -> x25, waiting for transfers between devices: 27.3 us -> 38.9 us  [exchange(): return lax.ppermute(value, axis, [(i, i ^ distance) for i in range(size)])]
    unnamed x22 -> x8, local copies, waits for them, and re-layouts: 4.28 us -> 0.03 us
    ppermute x24 -> x25, starting transfers between devices: 26.1 us -> 24.1 us  [exchange(): return lax.ppermute(value, axis, [(i, i ^ distance) for i in range(size)])]
    select_n x2 -> x0, other arithmetic: 0.86 us -> none  [the longest x1 0.83 us: layer(): grad_neigh = jnp.where(first, other_grads, grads)]
    pallas_call x5 -> x8, Pallas kernels: 16.9 us -> 17.5 us  [the longest x2 9.99 us: unpack(): pl.pallas_call(functools.partial(unpack_kernel, group // width, gather, r...]
  transfers between devices with their start and end apart: 24 -> 25, of which waited for: 11 -> 14; matrix products, arithmetic and copies ran while one was open for 1% -> 0% of each run, Pallas kernels for 19% -> 18%
where the time goes in v1:
time: 84.8 us; the launch traced here: 84.7 us
  waiting for transfers between devices  38.9 us (46%)
  starting transfers between devices  24.1 us (28%)
  Pallas kernels  19.7 us (23%)
  between operations  1.54 us (2%)
    ppermute x25, waiting for transfers between devices, exchange(): return lax.ppermute(value, axis, [(i, i ^ distance) for i in range(size)])  38.9 us
    ppermute x25, starting transfers between devices, exchange(): return lax.ppermute(value, axis, [(i, i ^ distance) for i in range(size)])  24.1 us
    pallas_call x2, Pallas kernels, unpack(): pl.pallas_call(functools.partial(unpack_kernel, group // width, gather, r...  9.99 us
    pallas_call x2, Pallas kernels, backward(): pl.pallas_call(functools.partial(backward_kernel, distances, n_part, len(...  2.58 us
    pallas_call x2, Pallas kernels, forward(): pl.pallas_call(functools.partial(forward_kernel, distances, n_col, natura...  2.52 us
  transfers between devices with their start and end apart: 25, of which 14 were waited for; matrix products, arithmetic and copies ran while one was open for 0% of the time, Pallas kernels for 18%

profile of v1, /device:TPU:0, one launch (start us, length us, event | category | flops | bytes accessed | tf_op | source)
XLA Modules:
  0.0 84.7 jit_solution(330198451423419941)
XLA Ops:
  0.6 0.0 copy-start
  0.6 3.1 %collective-permute-start.3 = (bf16[256,256]{1,0:T(8,128)(2,1)}, bf16[256,256]{1,0:T(8,128)(2,1)S(1)}, u32[]{:S(2)}, u32[]{:S(2)}) collective-permute-start(bf16[256,256]{1,0:T(8,128)(2,1)} %features_hbm.1), channel_id=1, source_target_pairs={{0,8},{4,12},{8,0},{12,4},{16,24},{20,28},{24,16},{28,20},{1,9},{5... | collective-permute-start | bytes 393224 | tf_op jit(solution)/shard_map/ppermute | solution.py:375
  3.8 2.6 %collective-permute-start.5 = (bf16[256,256]{1,0:T(8,128)(2,1)}, bf16[256,256]{1,0:T(8,128)(2,1)S(1)}, u32[]{:S(2)}, u32[]{:S(2)}) collective-permute-start(bf16[256,256]{1,0:T(8,128)(2,1)} %features_hbm.1), channel_id=1, source_target_pairs={{0,16},{4,20},{8,24},{12,28},{16,0},{20,4},{24,8},{28,12},{1,17},{... | collective-permute-start | bytes 393224 | tf_op jit(solution)/shard_map/ppermute | solution.py:375
  6.3 0.0 collective-permute-start
  6.4 1.7 %collective-permute-start.2 = (bf16[256,256]{1,0:T(8,128)(2,1)}, bf16[256,256]{1,0:T(8,128)(2,1)S(1)}, u32[]{:S(2)}, u32[]{:S(2)}) collective-permute-start(bf16[256,256]{1,0:T(8,128)(2,1)} %features_hbm.1), channel_id=1, source_target_pairs={{0,4},{4,0},{8,12},{12,8},{16,20},{20,16},{24,28},{28,24},{1,5},{5... | collective-permute-start | bytes 393224 | tf_op jit(solution)/shard_map/ppermute | solution.py:375
  8.7 0.1 pad_add_fusion.place_ref
  8.8 0.3 collective-permute-done.3.refs_2_
  9.0 1.7 %collective-permute-start.4 = (bf16[256,256]{1,0:T(8,128)(2,1)S(1)}, bf16[256,256]{1,0:T(8,128)(2,1)S(1)}, u32[]{:S(2)}, u32[]{:S(2)}) collective-permute-start(bf16[256,256]{1,0:T(8,128)(2,1)S(1)} %collective-permute-done.3.refs_2_), channel_id=1, source_target_pairs={{0,4},{4,0},{8,12},{12,8},{16,20},{20,16},{24,28},{28,24},{1,5},{5... | collective-permute-start | bytes 393224 | tf_op jit(solution)/shard_map/ppermute | solution.py:375
  10.8 6.1 %collective-permute-done.5.refs_4_ = bf16[256,256]{1,0:T(8,128)(2,1)S(1)} collective-permute-done((bf16[256,256]{1,0:T(8,128)(2,1)}, bf16[256,256]{1,0:T(8,128)(2,1)S(1)}, u32[]{:S(2)}, u32[]{:S(2)}) %collective-permute-start.5) | collective-permute-done | bytes 131104 | tf_op jit(solution)/shard_map/ppermute | solution.py:375
  16.9 1.5 %collective-permute-start.6 = (bf16[256,256]{1,0:T(8,128)(2,1)S(1)}, bf16[256,256]{1,0:T(8,128)(2,1)S(1)}, u32[]{:S(2)}, u32[]{:S(2)}) collective-permute-start(bf16[256,256]{1,0:T(8,128)(2,1)S(1)} %collective-permute-done.5.refs_4_), channel_id=1, source_target_pairs={{0,4},{4,0},{8,12},{12,8},{16,20},{20,16},{24,28},{28,24},{1,5},{5... | collective-permute-start | bytes 393224 | tf_op jit(solution)/shard_map/ppermute | solution.py:375
  18.3 5.5 %unpack_gather.1.adjacency_ref = bf16[1024,2048]{1,0:T(8,128)(2,1)S(1)} custom-call(s32[2]{0:T(128)S(1)} %pad_add_fusion.place_ref, s32[1]{0:T(128)} %bitcast.13.count_ref, s32[1,88]{1,0:T(1,128)} %bitcast.19, s32[88,16,128]{2,1,0:T(8,128)} %bitcast.16), custom_call_target="tpu_custom_call" | custom-call | flops 2000000000 | tf_op jit(solution)/shard_map/unpack_gather/pallas_call | solution.py:135
  23.9 0.0 collective-permute-done.refs_6_
  23.9 0.1 collective-permute-start.1
  24.0 0.0 collective-permute-done.6.refs_5_
  24.0 1.7 %forward.1.refs_1_ = f32[1024,256]{1,0:T(8,128)S(1)} custom-call(s32[2]{0:T(128)S(1)} %pad_add_fusion.place_ref, bf16[1024,2048]{1,0:T(8,128)(2,1)S(1)} %unpack_gather.1.adjacency_ref, bf16[256,256]{1,0:T(8,128)(2,1)S(1)} %copy-done, bf16[256,256]{1,0:T(8,128)(2,1)S(1)} %collective-permute-done.2.refs_1_, ...), custom_call_target="tpu_custom_call" | custom-call | flops 1750000000 | tf_op jit(solution)/shard_map/forward/pallas_call | solution.py:216
  25.7 0.0 copy-start.1
  25.7 0.0 copy-start.2
  25.7 0.0 copy-start.3
  25.7 3.2 %collective-permute-done.1.refs_0_ = bf16[256,256]{1,0:T(8,128)(2,1)S(1)} collective-permute-done((bf16[256,256]{1,0:T(8,128)(2,1)S(1)}, bf16[256,256]{1,0:T(8,128)(2,1)S(1)}, u32[]{:S(2)}, u32[]{:S(2)}) %collective-permute-start.1) | collective-permute-done | bytes 131104 | tf_op jit(solution)/shard_map/ppermute | solution.py:375
  28.9 0.8 forward_last.1
  29.8 0.1 collective-permute-start.7
  29.8 1.0 %near.1.refs_2_.refs_0_ = bf16[528,256]{1,0:T(8,128)(2,1)S(1)} custom-call(s32[1,256]{1,0:T(1,128)} %bitcast.18, bf16[256,256]{1,0:T(8,128)(2,1)} %features_hbm.1, bf16[256,256]{1,0:T(8,128)(2,1)} %cotangents_hbm.1), custom_call_target="tpu_custom_call" | custom-call | flops 500000000 | tf_op jit(solution)/shard_map/near/pallas_call | solution.py:173
  30.9 1.6 %collective-permute-start.9 = (bf16[528,256]{1,0:T(8,128)(2,1)S(1)}, bf16[528,256]{1,0:T(8,128)(2,1)S(1)}, u32[]{:S(2)}, u32[]{:S(2)}) collective-permute-start(bf16[528,256]{1,0:T(8,128)(2,1)S(1)} %near.1.refs_2_.refs_0_), channel_id=1, source_target_pairs={{0,2},{1,3},{2,0},{3,1},{4,6},{5,7},{6,4},{7,5},{8,10},{9,11},{10,... | collective-permute-start | bytes 811016 | tf_op jit(solution)/shard_map/ppermute | solution.py:375
  32.4 0.0 collective-permute-done.7
  32.4 0.1 add_convert_fusion.refs_0_
  32.5 0.6 collective-permute-start.8
  33.1 7.2 %collective-permute-done.9.refs_3_.refs_1_ = bf16[528,256]{1,0:T(8,128)(2,1)S(1)} collective-permute-done((bf16[528,256]{1,0:T(8,128)(2,1)S(1)}, bf16[528,256]{1,0:T(8,128)(2,1)S(1)}, u32[]{:S(2)}, u32[]{:S(2)}) %collective-permute-start.9) | collective-permute-done | bytes 270368 | tf_op jit(solution)/shard_map/ppermute | solution.py:375
  40.3 5.1 %collective-permute-done.8.refs_1_ = bf16[512,256]{1,0:T(8,128)(2,1)S(1)} collective-permute-done((bf16[512,256]{1,0:T(8,128)(2,1)S(1)}, bf16[512,256]{1,0:T(8,128)(2,1)S(1)}, u32[]{:S(2)}, u32[]{:S(2)}) %collective-permute-start.8) | collective-permute-done | bytes 262176 | tf_op jit(solution)/shard_map/ppermute | solution.py:375
  45.4 1.2 %node.1 = (bf16[256,256]{1,0:T(8,128)(2,1)}, bf16[512,256]{1,0:T(8,128)(2,1)S(1)}, bf16[512,256]{1,0:T(8,128)(2,1)S(1)}, bf16[512,256]{1,0:T(8,128)(2,1)S(1)}) custom-call(bf16[512,256]{1,0:T(8,128)(2,1)S(1)} %add_convert_fusion.refs_0_, bf16[512,256]{1,0:T(8,128)(2,1)S(1)} %collective-permute-done.8.refs_1_, bf16[528,256]{1,0:T(8,128)(2,1)S(1)} %near.1.refs_2_.refs_0_, ...), custom_call_target="tpu_custom_call" | custom-call | flops 2000000000 | tf_op jit(solution)/shard_map/node/pallas_call | solution.py:260
  46.7 0.9 %weight.1 = (bf16[2,128,256]{2,1,0:T(8,128)(2,1)S(1)}, f32[256,256]{1,0:T(8,128)S(1)}) custom-call(s32[2]{0:T(128)S(1)} %pad_add_fusion.place_ref, bf16[512,256]{1,0:T(8,128)(2,1)S(1)} %get-tuple-element.28.mean_ref, bf16[512,256]{1,0:T(8,128)(2,1)S(1)} %get-tuple-element.29.grad_ref, bf16[256,256]{1,0:T(8,128)(2,1)S(1)} %copy-done.2, ...), custom_call_target="tpu_custom_call" | custom-call | flops 1300000000 | tf_op jit(solution)/shard_map/weight/pallas_call | solution.py:289
  47.6 0.1 collective-permute-start.18
  47.7 5.0 %collective-permute-done.18 = bf16[2,128,256]{2,1,0:T(8,128)(2,1)S(1)} collective-permute-done((bf16[2,128,256]{2,1,0:T(8,128)(2,1)S(1)}, bf16[2,128,256]{2,1,0:T(8,128)(2,1)S(1)}, u32[]{:S(2)}, u32[]{:S(2)}) %collective-permute-start.18) | collective-permute-done | bytes 131104 | tf_op jit(solution)/shard_map/ppermute | solution.py:375
  52.8 0.1 collective-permute-start.19
  52.8 0.5 collective-permute-start.10
  53.3 0.7 collective-permute-done.19
  54.1 0.1 collective-permute-start.20
  54.2 4.5 %unpack_spread.1 = (bf16[1536,1024]{1,0:T(8,128)(2,1)S(1)}, bf16[512,1024]{1,0:T(8,128)(2,1)S(1)}) custom-call(s32[2]{0:T(128)S(1)} %pad_add_fusion.place_ref, s32[1]{0:T(128)} %bitcast.14.count_ref, s32[1,88]{1,0:T(1,128)} %bitcast.20, s32[88,16,128]{2,1,0:T(8,128)} %bitcast.17, bf16[512,256]{1,0:T(8,128)(2,1)S(1)} %add_convert_fusion.refs_0_), custom_call_target="tpu_custom_call" | custom-call | flops 2000000000 | tf_op jit(solution)/shard_map/unpack_spread/pallas_call | solution.py:135
  58.7 0.0 collective-permute-done.10.other_ref
  58.7 1.0 %backward_far.1 = (bf16[256,256]{1,0:T(8,128)(2,1)S(1)}, bf16[256,256]{1,0:T(8,128)(2,1)S(1)}) custom-call(s32[2]{0:T(128)S(1)} %pad_add_fusion.place_ref, bf16[512,1024]{1,0:T(8,128)(2,1)S(1)} %get-tuple-element.34.adjacency_ref, bf16[512,256]{1,0:T(8,128)(2,1)S(1)} %get-tuple-element.32.mine_ref, bf16[512,256]{1,0:T(8,128)(2,1)S(1)} %collective-permute-done.10.other_ref, ...), custom_call_target="tpu_custom_call" | custom-call | flops 400000000 | tf_op jit(solution)/shard_map/backward_far/pallas_call | solution.py:325
  59.7 0.1 collective-permute-start.11
  59.8 0.5 collective-permute-done.20
  60.3 1.0 %collective-permute-start.21 = (bf16[128,256]{1,0:T(8,128)(2,1)S(1)}, bf16[128,256]{1,0:T(8,128)(2,1)S(1)}, u32[]{:S(2)}, u32[]{:S(2)}) collective-permute-start(bf16[128,256]{1,0:T(8,128)(2,1)S(1)} %add_convert_fusion.4), channel_id=1, source_target_pairs={{0,8},{4,12},{8,0},{12,4},{16,24},{20,28},{24,16},{28,20},{1,9},{5... | collective-permute-start | bytes 196616 | tf_op jit(solution)/shard_map/ppermute | solution.py:375
  61.3 1.6 %backward.1 = (f32[256,256]{1,0:T(8,128)S(1)}, bf16[256,256]{1,0:T(8,128)(2,1)S(1)}, bf16[256,256]{1,0:T(8,128)(2,1)S(1)}, bf16[256,256]{1,0:T(8,128)(2,1)S(1)},...) custom-call(s32[2]{0:T(128)S(1)} %pad_add_fusion.place_ref, ...), custom_call_target="tpu_custom_call" | custom-call | flops 1200000000 | tf_op jit(solution)/shard_map/backward/pallas_call | solution.py:325
  62.9 2.1 %collective-permute-start.13 = (bf16[256,256]{1,0:T(8,128)(2,1)S(1)}, bf16[256,256]{1,0:T(8,128)(2,1)S(1)}, u32[]{:S(2)}, u32[]{:S(2)}) collective-permute-start(bf16[256,256]{1,0:T(8,128)(2,1)S(1)} %get-tuple-element.39), channel_id=1, source_target_pairs={{0,4},{4,0},{8,12},{12,8},{16,20},{20,16},{24,28},{28,24},{1,5},{5... | collective-permute-start | bytes 393224 | tf_op jit(solution)/shard_map/ppermute | solution.py:375
  65.0 0.1 collective-permute-start.15
  65.0 1.9 %collective-permute-start.17 = (bf16[256,256]{1,0:T(8,128)(2,1)S(1)}, bf16[256,256]{1,0:T(8,128)(2,1)S(1)}, u32[]{:S(2)}, u32[]{:S(2)}) collective-permute-start(bf16[256,256]{1,0:T(8,128)(2,1)S(1)} %get-tuple-element.42), channel_id=1, source_target_pairs={{0,4},{4,0},{8,12},{12,8},{16,20},{20,16},{24,28},{28,24},{1,5},{5... | collective-permute-start | bytes 393224 | tf_op jit(solution)/shard_map/ppermute | solution.py:375
  67.0 0.0 collective-permute-done.21
  67.0 2.0 %collective-permute-start.22 = (f32[128,256]{1,0:T(8,128)S(1)}, f32[128,256]{1,0:T(8,128)S(1)}, u32[]{:S(2)}, u32[]{:S(2)}) collective-permute-start(f32[128,256]{1,0:T(8,128)S(1)} %convert_add_fusion.1.refs_6_), channel_id=1, source_target_pairs={{0,2},{1,3},{2,0},{3,1},{4,6},{5,7},{6,4},{7,5},{8,10},{9,11},{10,... | collective-permute-start | bytes 393224 | tf_op jit(solution)/shard_map/ppermute | solution.py:375
  69.0 0.0 collective-permute-done.11
  69.0 0.0 collective-permute-start.23
  69.1 0.3 collective-permute-done.13
  69.3 1.5 %collective-permute-start.12 = (bf16[256,256]{1,0:T(8,128)(2,1)S(1)}, bf16[256,256]{1,0:T(8,128)(2,1)S(1)}, u32[]{:S(2)}, u32[]{:S(2)}) collective-permute-start(bf16[256,256]{1,0:T(8,128)(2,1)S(1)} %add_convert_fusion.3), channel_id=1, source_target_pairs={{0,24},{4,28},{8,16},{12,20},{16,8},{20,12},{24,0},{28,4},{1,25},{... | collective-permute-start | bytes 393224 | tf_op jit(solution)/shard_map/ppermute | solution.py:375
  70.9 1.3 %collective-permute-done.15 = bf16[256,256]{1,0:T(8,128)(2,1)S(1)} collective-permute-done((bf16[256,256]{1,0:T(8,128)(2,1)S(1)}, bf16[256,256]{1,0:T(8,128)(2,1)S(1)}, u32[]{:S(2)}, u32[]{:S(2)}) %collective-permute-start.15) | collective-permute-done | bytes 131104 | tf_op jit(solution)/shard_map/ppermute | solution.py:375
  72.1 1.0 %collective-permute-start.14 = (bf16[256,256]{1,0:T(8,128)(2,1)S(1)}, bf16[256,256]{1,0:T(8,128)(2,1)S(1)}, u32[]{:S(2)}, u32[]{:S(2)}) collective-permute-start(bf16[256,256]{1,0:T(8,128)(2,1)S(1)} %add_convert_fusion.2), channel_id=1, source_target_pairs={{0,8},{4,12},{8,0},{12,4},{16,24},{20,28},{24,16},{28,20},{1,9},{5... | collective-permute-start | bytes 393224 | tf_op jit(solution)/shard_map/ppermute | solution.py:375
  73.2 0.6 collective-permute-done.17.refs_5_
  73.9 0.8 collective-permute-start.16
  74.6 0.0 collective-permute-done.22.refs_7_
  74.6 0.0 collective-permute-start.24
  74.7 0.0 collective-permute-done.23.refs_8_
  74.7 2.9 %collective-permute-done.12.refs_2_ = bf16[256,256]{1,0:T(8,128)(2,1)S(1)} collective-permute-done((bf16[256,256]{1,0:T(8,128)(2,1)S(1)}, bf16[256,256]{1,0:T(8,128)(2,1)S(1)}, u32[]{:S(2)}, u32[]{:S(2)}) %collective-permute-start.12) | collective-permute-done | bytes 131104 | tf_op jit(solution)/shard_map/ppermute | solution.py:375
  77.6 3.0 %collective-permute-done.14.refs_3_ = bf16[256,256]{1,0:T(8,128)(2,1)S(1)} collective-permute-done((bf16[256,256]{1,0:T(8,128)(2,1)S(1)}, bf16[256,256]{1,0:T(8,128)(2,1)S(1)}, u32[]{:S(2)}, u32[]{:S(2)}) %collective-permute-start.14) | collective-permute-done | bytes 131104 | tf_op jit(solution)/shard_map/ppermute | solution.py:375
  80.5 2.7 %collective-permute-done.16.refs_4_ = bf16[256,256]{1,0:T(8,128)(2,1)S(1)} collective-permute-done((bf16[256,256]{1,0:T(8,128)(2,1)S(1)}, bf16[256,256]{1,0:T(8,128)(2,1)S(1)}, u32[]{:S(2)}, u32[]{:S(2)}) %collective-permute-start.16) | collective-permute-done | bytes 131104 | tf_op jit(solution)/shard_map/ppermute | solution.py:375
  83.2 0.0 collective-permute-done.24.refs_9_
  83.2 1.4 %final.1 = (bf16[256,256]{1,0:T(8,128)(2,1)}, f32[256,256]{1,0:T(8,128)}, f32[256,256]{1,0:T(8,128)}) custom-call(s32[2]{0:T(128)S(1)} %pad_add_fusion.place_ref, f32[256,256]{1,0:T(8,128)S(1)} %get-tuple-element.30.refs_0_, f32[256,256]{1,0:T(8,128)S(1)} %get-tuple-element.33.refs_1_, bf16[256,256]{1,0:T(8,128)(2,1)S(1)} %collective-permute-done.12.refs_2_, ...), custom_call_target="tpu_custom_call" | custom-call | flops 800000000 | tf_op jit(solution)/shard_map/final/pallas_call | solution.py:362
  (14 shorter events, 0.2 us)
Async XLA Ops:
  0.6 23.4 %copy-start = (bf16[256,256]{1,0:T(8,128)(2,1)S(1)}, bf16[256,256]{1,0:T(8,128)(2,1)}, u32[]{:S(2)}) copy-start(bf16[256,256]{1,0:T(8,128)(2,1)} %features_hbm.1) | copy-start | bytes 393220
  0.6 8.4 %collective-permute-start.3 = (bf16[256,256]{1,0:T(8,128)(2,1)}, bf16[256,256]{1,0:T(8,128)(2,1)S(1)}, u32[]{:S(2)}, u32[]{:S(2)}) collective-permute-start(bf16[256,256]{1,0:T(8,128)(2,1)} %features_hbm.1), channel_id=1, source_target_pairs={{0,8},{4,12},{8,0},{12,4},{16,24},{20,28},{24,16},{28,20},{1,9},{5... | collective-permute-start | bytes 393224 | tf_op jit(solution)/shard_map/ppermute | solution.py:375
  3.8 13.1 %collective-permute-start.5 = (bf16[256,256]{1,0:T(8,128)(2,1)}, bf16[256,256]{1,0:T(8,128)(2,1)S(1)}, u32[]{:S(2)}, u32[]{:S(2)}) collective-permute-start(bf16[256,256]{1,0:T(8,128)(2,1)} %features_hbm.1), channel_id=1, source_target_pairs={{0,16},{4,20},{8,24},{12,28},{16,0},{20,4},{24,8},{28,12},{1,17},{... | collective-permute-start | bytes 393224 | tf_op jit(solution)/shard_map/ppermute | solution.py:375
  6.3 17.5 %collective-permute-start = (bf16[256,256]{1,0:T(8,128)(2,1)}, bf16[256,256]{1,0:T(8,128)(2,1)S(1)}, u32[]{:S(2)}, u32[]{:S(2)}) collective-permute-start(bf16[256,256]{1,0:T(8,128)(2,1)} %features_hbm.1), channel_id=1, source_target_pairs={{0,24},{4,28},{8,16},{12,20},{16,8},{20,12},{24,0},{28,4},{1,25},{... | collective-permute-start | bytes 393224 | tf_op jit(solution)/shard_map/ppermute | solution.py:375
  6.4 17.6 %collective-permute-start.2 = (bf16[256,256]{1,0:T(8,128)(2,1)}, bf16[256,256]{1,0:T(8,128)(2,1)S(1)}, u32[]{:S(2)}, u32[]{:S(2)}) collective-permute-start(bf16[256,256]{1,0:T(8,128)(2,1)} %features_hbm.1), channel_id=1, source_target_pairs={{0,4},{4,0},{8,12},{12,8},{16,20},{20,16},{24,28},{28,24},{1,5},{5... | collective-permute-start | bytes 393224 | tf_op jit(solution)/shard_map/ppermute | solution.py:375
  9.0 14.9 %collective-permute-start.4 = (bf16[256,256]{1,0:T(8,128)(2,1)S(1)}, bf16[256,256]{1,0:T(8,128)(2,1)S(1)}, u32[]{:S(2)}, u32[]{:S(2)}) collective-permute-start(bf16[256,256]{1,0:T(8,128)(2,1)S(1)} %collective-permute-done.3.refs_2_), channel_id=1, source_target_pairs={{0,4},{4,0},{8,12},{12,8},{16,20},{20,16},{24,28},{28,24},{1,5},{5... | collective-permute-start | bytes 393224 | tf_op jit(solution)/shard_map/ppermute | solution.py:375
  16.9 7.1 %collective-permute-start.6 = (bf16[256,256]{1,0:T(8,128)(2,1)S(1)}, bf16[256,256]{1,0:T(8,128)(2,1)S(1)}, u32[]{:S(2)}, u32[]{:S(2)}) collective-permute-start(bf16[256,256]{1,0:T(8,128)(2,1)S(1)} %collective-permute-done.5.refs_4_), channel_id=1, source_target_pairs={{0,4},{4,0},{8,12},{12,8},{16,20},{20,16},{24,28},{28,24},{1,5},{5... | collective-permute-start | bytes 393224 | tf_op jit(solution)/shard_map/ppermute | solution.py:375
  23.9 5.0 %collective-permute-start.1 = (bf16[256,256]{1,0:T(8,128)(2,1)S(1)}, bf16[256,256]{1,0:T(8,128)(2,1)S(1)}, u32[]{:S(2)}, u32[]{:S(2)}) collective-permute-start(bf16[256,256]{1,0:T(8,128)(2,1)S(1)} %collective-permute-done.refs_6_), channel_id=1, source_target_pairs={{0,4},{4,0},{8,12},{12,8},{16,20},{20,16},{24,28},{28,24},{1,5},{5... | collective-permute-start | bytes 393224 | tf_op jit(solution)/shard_map/ppermute | solution.py:375
  25.7 19.7 %copy-start.1 = (bf16[256,256]{1,0:T(8,128)(2,1)S(1)}, bf16[256,256]{1,0:T(8,128)(2,1)}, u32[]{:S(2)}) copy-start(bf16[256,256]{1,0:T(8,128)(2,1)} %refs_5_.1) | copy-start | bytes 393220
  25.7 19.7 %copy-start.2 = (bf16[256,256]{1,0:T(8,128)(2,1)S(1)}, bf16[256,256]{1,0:T(8,128)(2,1)}, u32[]{:S(2)}) copy-start(bf16[256,256]{1,0:T(8,128)(2,1)} %w_self.1) | copy-start | bytes 393220
  25.7 19.7 %copy-start.3 = (f32[256]{0:T(256)S(1)}, f32[256]{0:T(256)}, u32[]{:S(2)}) copy-start(f32[256]{0:T(256)} %param.14) | copy-start | bytes 3076
  29.8 2.7 %collective-permute-start.7 = (bf16[512,256]{1,0:T(8,128)(2,1)S(1)}, bf16[512,256]{1,0:T(8,128)(2,1)S(1)}, u32[]{:S(2)}, u32[]{:S(2)}) collective-permute-start(bf16[512,256]{1,0:T(8,128)(2,1)S(1)} %get-tuple-element.26), channel_id=1, source_target_pairs={{0,1},{1,0},{2,3},{3,2},{4,5},{5,4},{6,7},{7,6},{8,9},{9,8},{10,11... | collective-permute-start | bytes 786440 | tf_op jit(solution)/shard_map/ppermute | solution.py:375
  30.9 9.4 %collective-permute-start.9 = (bf16[528,256]{1,0:T(8,128)(2,1)S(1)}, bf16[528,256]{1,0:T(8,128)(2,1)S(1)}, u32[]{:S(2)}, u32[]{:S(2)}) collective-permute-start(bf16[528,256]{1,0:T(8,128)(2,1)S(1)} %near.1.refs_2_.refs_0_), channel_id=1, source_target_pairs={{0,2},{1,3},{2,0},{3,1},{4,6},{5,7},{6,4},{7,5},{8,10},{9,11},{10,... | collective-permute-start | bytes 811016 | tf_op jit(solution)/shard_map/ppermute | solution.py:375
  32.5 12.9 %collective-permute-start.8 = (bf16[512,256]{1,0:T(8,128)(2,1)S(1)}, bf16[512,256]{1,0:T(8,128)(2,1)S(1)}, u32[]{:S(2)}, u32[]{:S(2)}) collective-permute-start(bf16[512,256]{1,0:T(8,128)(2,1)S(1)} %add_convert_fusion.refs_0_), channel_id=1, source_target_pairs={{0,2},{1,3},{2,0},{3,1},{4,6},{5,7},{6,4},{7,5},{8,10},{9,11},{10,... | collective-permute-start | bytes 786440 | tf_op jit(solution)/shard_map/ppermute | solution.py:375
  47.6 5.1 %collective-permute-start.18 = (bf16[2,128,256]{2,1,0:T(8,128)(2,1)S(1)}, bf16[2,128,256]{2,1,0:T(8,128)(2,1)S(1)}, u32[]{:S(2)}, u32[]{:S(2)}) collective-permute-start(bf16[2,128,256]{2,1,0:T(8,128)(2,1)S(1)} %get-tuple-element.35.refs_0_), channel_id=1, source_target_pairs={{0,4},{4,0},{8,12},{12,8},{16,20},{20,16},{24,28},{28,24},{1,5},{5... | collective-permute-start | bytes 393224 | tf_op jit(solution)/shard_map/ppermute | solution.py:375
  52.8 1.3 %collective-permute-start.19 = (bf16[128,256]{1,0:T(8,128)(2,1)S(1)}, bf16[128,256]{1,0:T(8,128)(2,1)S(1)}, u32[]{:S(2)}, u32[]{:S(2)}) collective-permute-start(bf16[128,256]{1,0:T(8,128)(2,1)S(1)} %fusion.1), channel_id=1, source_target_pairs={{0,1},{1,0},{2,3},{3,2},{4,5},{5,4},{6,7},{7,6},{8,9},{9,8},{10,11... | collective-permute-start | bytes 196616 | tf_op jit(solution)/shard_map/ppermute | solution.py:375
  52.8 5.8 %collective-permute-start.10 = (bf16[512,256]{1,0:T(8,128)(2,1)S(1)}, bf16[512,256]{1,0:T(8,128)(2,1)S(1)}, u32[]{:S(2)}, u32[]{:S(2)}) collective-permute-start(bf16[512,256]{1,0:T(8,128)(2,1)S(1)} %get-tuple-element.32.mine_ref), channel_id=1, source_target_pairs={{0,1},{1,0},{2,3},{3,2},{4,5},{5,4},{6,7},{7,6},{8,9},{9,8},{10,11... | collective-permute-start | bytes 786440 | tf_op jit(solution)/shard_map/ppermute | solution.py:375
  54.1 6.2 %collective-permute-start.20 = (bf16[128,256]{1,0:T(8,128)(2,1)S(1)}, bf16[128,256]{1,0:T(8,128)(2,1)S(1)}, u32[]{:S(2)}, u32[]{:S(2)}) collective-permute-start(bf16[128,256]{1,0:T(8,128)(2,1)S(1)} %fusion), channel_id=1, source_target_pairs={{0,16},{4,20},{8,24},{12,28},{16,0},{20,4},{24,8},{28,12},{1,17},{... | collective-permute-start | bytes 196616 | tf_op jit(solution)/shard_map/ppermute | solution.py:375
  59.7 9.3 %collective-permute-start.11 = (bf16[256,256]{1,0:T(8,128)(2,1)S(1)}, bf16[256,256]{1,0:T(8,128)(2,1)S(1)}, u32[]{:S(2)}, u32[]{:S(2)}) collective-permute-start(bf16[256,256]{1,0:T(8,128)(2,1)S(1)} %get-tuple-element.37), channel_id=1, source_target_pairs={{0,4},{4,0},{8,12},{12,8},{16,20},{20,16},{24,28},{28,24},{1,5},{5... | collective-permute-start | bytes 393224 | tf_op jit(solution)/shard_map/ppermute | solution.py:375
  60.3 6.7 %collective-permute-start.21 = (bf16[128,256]{1,0:T(8,128)(2,1)S(1)}, bf16[128,256]{1,0:T(8,128)(2,1)S(1)}, u32[]{:S(2)}, u32[]{:S(2)}) collective-permute-start(bf16[128,256]{1,0:T(8,128)(2,1)S(1)} %add_convert_fusion.4), channel_id=1, source_target_pairs={{0,8},{4,12},{8,0},{12,4},{16,24},{20,28},{24,16},{28,20},{1,9},{5... | collective-permute-start | bytes 196616 | tf_op jit(solution)/shard_map/ppermute | solution.py:375
  62.9 6.4 %collective-permute-start.13 = (bf16[256,256]{1,0:T(8,128)(2,1)S(1)}, bf16[256,256]{1,0:T(8,128)(2,1)S(1)}, u32[]{:S(2)}, u32[]{:S(2)}) collective-permute-start(bf16[256,256]{1,0:T(8,128)(2,1)S(1)} %get-tuple-element.39), channel_id=1, source_target_pairs={{0,4},{4,0},{8,12},{12,8},{16,20},{20,16},{24,28},{28,24},{1,5},{5... | collective-permute-start | bytes 393224 | tf_op jit(solution)/shard_map/ppermute | solution.py:375
  65.0 7.2 %collective-permute-start.15 = (bf16[256,256]{1,0:T(8,128)(2,1)S(1)}, bf16[256,256]{1,0:T(8,128)(2,1)S(1)}, u32[]{:S(2)}, u32[]{:S(2)}) collective-permute-start(bf16[256,256]{1,0:T(8,128)(2,1)S(1)} %get-tuple-element.41), channel_id=1, source_target_pairs={{0,4},{4,0},{8,12},{12,8},{16,20},{20,16},{24,28},{28,24},{1,5},{5... | collective-permute-start | bytes 393224 | tf_op jit(solution)/shard_map/ppermute | solution.py:375
  65.0 8.8 %collective-permute-start.17 = (bf16[256,256]{1,0:T(8,128)(2,1)S(1)}, bf16[256,256]{1,0:T(8,128)(2,1)S(1)}, u32[]{:S(2)}, u32[]{:S(2)}) collective-permute-start(bf16[256,256]{1,0:T(8,128)(2,1)S(1)} %get-tuple-element.42), channel_id=1, source_target_pairs={{0,4},{4,0},{8,12},{12,8},{16,20},{20,16},{24,28},{28,24},{1,5},{5... | collective-permute-start | bytes 393224 | tf_op jit(solution)/shard_map/ppermute | solution.py:375
  67.0 7.6 %collective-permute-start.22 = (f32[128,256]{1,0:T(8,128)S(1)}, f32[128,256]{1,0:T(8,128)S(1)}, u32[]{:S(2)}, u32[]{:S(2)}) collective-permute-start(f32[128,256]{1,0:T(8,128)S(1)} %convert_add_fusion.1.refs_6_), channel_id=1, source_target_pairs={{0,2},{1,3},{2,0},{3,1},{4,6},{5,7},{6,4},{7,5},{8,10},{9,11},{10,... | collective-permute-start | bytes 393224 | tf_op jit(solution)/shard_map/ppermute | solution.py:375
  69.0 5.6 %collective-permute-start.23 = (f32[128,256]{1,0:T(8,128)S(1)}, f32[128,256]{1,0:T(8,128)S(1)}, u32[]{:S(2)}, u32[]{:S(2)}) collective-permute-start(f32[128,256]{1,0:T(8,128)S(1)} %convert_add_fusion.1.refs_6_), channel_id=1, source_target_pairs={{0,1},{1,0},{2,3},{3,2},{4,5},{5,4},{6,7},{7,6},{8,9},{9,8},{10,11... | collective-permute-start | bytes 393224 | tf_op jit(solution)/shard_map/ppermute | solution.py:375
  69.3 8.2 %collective-permute-start.12 = (bf16[256,256]{1,0:T(8,128)(2,1)S(1)}, bf16[256,256]{1,0:T(8,128)(2,1)S(1)}, u32[]{:S(2)}, u32[]{:S(2)}) collective-permute-start(bf16[256,256]{1,0:T(8,128)(2,1)S(1)} %add_convert_fusion.3), channel_id=1, source_target_pairs={{0,24},{4,28},{8,16},{12,20},{16,8},{20,12},{24,0},{28,4},{1,25},{... | collective-permute-start | bytes 393224 | tf_op jit(solution)/shard_map/ppermute | solution.py:375
  72.1 8.4 %collective-permute-start.14 = (bf16[256,256]{1,0:T(8,128)(2,1)S(1)}, bf16[256,256]{1,0:T(8,128)(2,1)S(1)}, u32[]{:S(2)}, u32[]{:S(2)}) collective-permute-start(bf16[256,256]{1,0:T(8,128)(2,1)S(1)} %add_convert_fusion.2), channel_id=1, source_target_pairs={{0,8},{4,12},{8,0},{12,4},{16,24},{20,28},{24,16},{28,20},{1,9},{5... | collective-permute-start | bytes 393224 | tf_op jit(solution)/shard_map/ppermute | solution.py:375
  73.9 9.3 %collective-permute-start.16 = (bf16[256,256]{1,0:T(8,128)(2,1)S(1)}, bf16[256,256]{1,0:T(8,128)(2,1)S(1)}, u32[]{:S(2)}, u32[]{:S(2)}) collective-permute-start(bf16[256,256]{1,0:T(8,128)(2,1)S(1)} %add_convert_fusion.1), channel_id=1, source_target_pairs={{0,16},{4,20},{8,24},{12,28},{16,0},{20,4},{24,8},{28,12},{1,17},{... | collective-permute-start | bytes 393224 | tf_op jit(solution)/shard_map/ppermute | solution.py:375
  74.6 8.6 %collective-permute-start.24 = (f32[128,256]{1,0:T(8,128)S(1)}, f32[128,256]{1,0:T(8,128)S(1)}, u32[]{:S(2)}, u32[]{:S(2)}) collective-permute-start(f32[128,256]{1,0:T(8,128)S(1)} %collective-permute-done.22.refs_7_), channel_id=1, source_target_pairs={{0,1},{1,0},{2,3},{3,2},{4,5},{5,4},{6,7},{7,6},{8,9},{9,8},{10,11... | collective-permute-start | bytes 393224 | tf_op jit(solution)/shard_map/ppermute | solution.py:375

commit v2 on v1

--- a/solution.py
+++ b/solution.py
@@ -105,26 +105,18 @@
 
         return
 
-    stacked = together * words
-    source = lax.broadcasted_iota(jnp.int32, (stacked, together * words * 8), 0)
-    target = lax.broadcasted_iota(jnp.int32, (stacked, together * words * 8), 1)
-    repeat = (source == lax.div(target, 8)).astype(f32).astype(bf16)
-    shifts = lax.rem(lax.broadcasted_iota(jnp.int32, (width, words * 8), 1), 8)
+    places = jnp.left_shift(1, lax.broadcasted_iota(jnp.int32, (words, 8, width), 1))
 
     @pl.loop(0, lax.div(count_ref[0] + together - 1, together))
     def _(step):
-        first = step * together
-        live = [
-            masks_ref[first + t] * (first + t < count_ref[0]).astype(jnp.int32)
-            for t in range(together)
-        ]
-        turned = jnp.concatenate(live, axis=0).astype(f32).T.astype(bf16)
-        word = mm(turned, repeat)
         for t in range(together):
-            row_block, column_block = blocks(first + t)
-            own = word[:, t * words * 8 : (t + 1) * words * 8].astype(jnp.int32)
-            bits = jnp.bitwise_and(jnp.right_shift(own, shifts), 1).astype(f32).astype(bf16)
-            dense_ref[span(row_block, width), span(column_block, width)] = bits
+            tile = step * together + t
+            row_block, column_block = blocks(tile)
+            word = masks_ref[tile] * (tile < count_ref[0]).astype(jnp.int32)
+            word = jnp.broadcast_to(word[:, None, :], (words, 8, width))
+            bits = jnp.where(jnp.bitwise_and(word, places) != 0, 1.0, 0.0).astype(f32)
+            bits = bits.reshape(words * 8, width).astype(bf16)
+            dense_ref[span(row_block, width), span(column_block, width)] = bits.T
 
 
 def unpack(gather, place, tiles, after, panel, group, rows=0):
@@ -301,48 +293,46 @@
     )(place, mean, grad, w_self, *nears)
 
 
-def backward_kernel(distances, n_part, n_after, place_ref, adjacency_ref, mine_ref, other_ref, *refs):
+def backward_kernel(groups, place_of, n_part, n_after, place_ref, adjacency_ref, mine_ref, other_ref, *refs):
     outs, up_ref = refs[n_after:-1], refs[-1]
-    rows = outs[0].shape[0]
+    rows = mine_ref.shape[0] // n_part
     row, col = place_ref[0], place_ref[1]
     for h in range(n_part):
         here = pl.ds(h * rows, rows)
         up_ref[span(jnp.bitwise_xor(col, 2 * h), rows), :] = mine_ref[here, :]
         up_ref[span(jnp.bitwise_xor(col, 2 * h + 1), rows), :] = other_ref[here, :]
-    whole = adjacency_ref.shape[0] > len(distances) * rows
-    for index, (d, out) in enumerate(zip(distances, outs)):
-        if whole:
-            block = adjacency_ref[span(jnp.bitwise_xor(row, d), rows), :]
-        else:
-            block = adjacency_ref[pl.ds(index * rows, rows), :]
-        out[...] = mm(block, up_ref[...]).astype(out.dtype)
-
-
-def backward(place, adjacency, mine, other, after, distances, n_part):
+    for group, out in zip(groups, outs):
+        for index, d in enumerate(group):
+            if place_of is None:
+                where = span(jnp.bitwise_xor(row, d), rows)
+            else:
+                where = pl.ds(place_of[d] * rows, rows)
+            product = mm(adjacency_ref[where, :], up_ref[...])
+            out[pl.ds(index * rows, rows), :] = product.astype(out.dtype)
+
+
+def backward(place, adjacency, place_of, mine, other, after, groups, n_part):
     rows = mine.shape[0] // n_part
     width = mine.shape[1]
-    shapes = [jax.ShapeDtypeStruct((rows, width), bf16 if d else f32) for d in distances]
+    shapes = [
+        jax.ShapeDtypeStruct((len(group) * rows, width), f32 if group == (0,) else bf16)
+        for group in groups
+    ]
     outs = pl.pallas_call(
-        functools.partial(backward_kernel, distances, n_part, len(after)),
+        functools.partial(backward_kernel, groups, place_of, n_part, len(after)),
         out_shape=shapes,
         in_specs=[SMEM] + [VMEM] * 3 + [ANY] * len(after),
         out_specs=[VMEM] * len(shapes),
         scratch_shapes=[pltpu.VMEM((2 * n_part * rows, width), bf16)],
         compiler_params=params(adjacency, mine, other, mine, other, *shapes),
-        cost_estimate=cost(200 * len(distances)),
-        name="backward" if 0 in distances else "backward_far",
+        cost_estimate=cost(200 * sum(len(group) for group in groups)),
+        name="backward" if (0,) in groups else "backward_far",
     )(place, adjacency, mine, other, *after)
-    return dict(zip(distances, outs))
-
-
-def final_kernel(n_part, n_terms, scale, place_ref, *refs):
-    terms, refs = refs[:n_terms], refs[n_terms:]
-    mine, others, refs = refs[:n_part], refs[n_part : 2 * n_part], refs[2 * n_part :]
-    grad_in_ref, self_ref, neigh_ref = refs
-    total = terms[0][...]
-    for term in terms[1:]:
-        total = total + term[...].astype(f32)
-    grad_in_ref[...] = total.astype(bf16)
+    return dict(zip(groups, outs))
+
+
+def join_kernel(n_part, scale, place_ref, *refs):
+    mine, others, (self_ref, neigh_ref) = refs[:n_part], refs[n_part:-2], refs[-2:]
     first = lax.rem(place_ref[1], 2) == 0
     for h in range(n_part):
         here = span(jnp.bitwise_xor(lax.div(place_ref[1], 2), h), mine[h].shape[0])
@@ -351,23 +341,19 @@
         neigh_ref[here, :] = jnp.where(first, two, one)
 
 
-def final(place, terms, mine, others, scale):
+def join(place, mine, others, scale):
     n_part = len(mine)
-    rows, width = terms[0].shape
-    shapes = [
-        jax.ShapeDtypeStruct((rows, width), bf16),
-        jax.ShapeDtypeStruct((width, width), f32),
-        jax.ShapeDtypeStruct((width, width), f32),
-    ]
-    return pl.pallas_call(
-        functools.partial(final_kernel, n_part, len(terms), scale),
+    width = mine[0].shape[1]
+    shapes = [jax.ShapeDtypeStruct((width, width), f32)] * 2
+    return pl.pallas_call(
+        functools.partial(join_kernel, n_part, scale),
         out_shape=shapes,
-        in_specs=[SMEM] + [VMEM] * (len(terms) + 2 * n_part),
-        out_specs=[VMEM] * 3,
-        compiler_params=params(*terms, *mine, *others, *shapes),
+        in_specs=[SMEM] + [VMEM] * (2 * n_part),
+        out_specs=[VMEM] * 2,
+        compiler_params=params(*mine, *others, *shapes),
         cost_estimate=cost(800),
-        name="final",
-    )(place, *terms, *mine, *others)
+        name="join",
+    )(place, *mine, *others)
 
 
 def exchange(value, axis, distance):
@@ -407,22 +393,41 @@
     layer_out, mean, grad, up = node(sums, nears, w_self, w_neigh, bias.reshape(1, width))
     up_other = exchange(up, "col", 1)
     slices, base = weight(place, mean, grad, w_self, nears)
-    every = list(range(n_row))
+    top = n_row // 2
+    apart = [d for d in reversed(sorted(far)) if d >= top]
+    joined = tuple(d ^ 1 for d in [0] + sorted(far) if d < top)
+    first = [(apart[0] ^ 1,), (apart[0],)]
+    rest = [(d ^ e,) for d in apart[1:] for e in (1, 0)]
+    rest += [joined] + [(d ^ 1,) for d in joined]
     if both:
         near_part, far_part = unpack(False, place, tiles, [pair], panel, group, rows)
-        backs = backward(place, far_part, up, up_other, [slices], every[-2:], n_part)
-        backs.update(backward(place, near_part, up, up_other, [], every[:-2], n_part))
+        near_places = {d: d for d in range(n_row - 2)}
+        far_places = {n_row - 2: 0, n_row - 1: 1}
+        backs = backward(place, far_part, far_places, up, up_other, [slices], first, n_part)
+        backs.update(backward(place, near_part, near_places, up, up_other, [], rest, n_part))
     else:
-        backs = backward(place, dense, up, up_other, [slices], every, n_part)
-
-    terms = [base, backs[0]]
-    for d in reversed(far):
-        came = exchange(backs[d ^ 1], "row", 1)
-        both_x = (backs[d].astype(f32) + came.astype(f32)).astype(bf16)
-        terms.append(exchange(both_x, "row", d))
-    terms.append(exchange(backs[1], "row", 1))
-
-    sums = slices.astype(f32) + exchange(slices, "row", 1).astype(f32)
+        backs = backward(place, dense, None, up, up_other, [slices], first + rest, n_part)
+
+    pairs = {}
+    for d in apart:
+        came = exchange(backs[(d ^ 1,)], "row", 1)
+        pairs[d] = backs[(d,)].astype(f32) + came.astype(f32)
+    near_came = exchange(backs[joined], "row", 1)
+    for index, d in enumerate(joined):
+        came = near_came[index * rows : (index + 1) * rows].astype(f32)
+        pairs[d ^ 1] = backs[(d ^ 1,)].astype(f32) + came
+    for d in apart:
+        if d > top:
+            came = exchange(pairs[d].astype(bf16), "row", d ^ top)
+            pairs[top] = pairs[top] + came.astype(f32)
+    total = base + pairs[0]
+    for d in sorted(far):
+        if d <= top:
+            total = total + exchange(pairs[d].astype(bf16), "row", d).astype(f32)
+    grad_in = total.astype(bf16)
+
+    came = exchange(slices, "row", 1)
+    sums = slices.astype(f32) + came.astype(f32)
     core = lax.rem(col, 2) == 0
     keep = jnp.where(core, sums[0], sums[1])
     send = jnp.where(core, sums[1], sums[0]).astype(bf16)
@@ -436,7 +441,7 @@
     mine = [grads] + [exchange(grads, "col", 2 * h) for h in range(1, n_part)]
     others = [exchange(value, "col", 1) for value in mine]
     scale = 1.0 / math.sqrt(panel * n_col)
-    grad_in, grad_self, grad_neigh = final(place, terms, mine, others, scale)
+    grad_self, grad_neigh = join(place, mine, others, scale)
     return layer_out, grad_in, grad_self, grad_neigh
 
 

time: 84.8 us -> 79.8 us (0.941)
  waiting for transfers between devices: 38.9 us -> 36.6 us
  Pallas kernels: 19.7 us -> 17.8 us
  starting transfers between devices: 24.1 us -> 22.6 us
    ppermute x25 -> x24, waiting for transfers between devices: 38.9 us -> 36.6 us  [exchange(): return lax.ppermute(value, axis, [(i, i ^ distance) for i in range(size)])]
    pallas_call x2, Pallas kernels: 9.99 us -> 8.2 us  [unpack(): pl.pallas_call(functools.partial(unpack_kernel, group // width, gather, r...]
    ppermute x25 -> x24, starting transfers between devices: 24.1 us -> 22.6 us  [exchange(): return lax.ppermute(value, axis, [(i, i ^ distance) for i in range(size)])]
  transfers between devices with their start and end apart: 25 -> 24, of which waited for: 14 -> 13; matrix products, arithmetic and copies ran while one was open for 0% -> 0% of each run, Pallas kernels for 18% -> 19%
where the time goes in v2:
time: 79.8 us; the launch traced here: 79.6 us
  waiting for transfers between devices  36.6 us (46%)
  starting transfers between devices  22.6 us (28%)
  Pallas kernels  17.8 us (22%)
  between operations  1.54 us (2%)
  other arithmetic  1.09 us (1%)
    ppermute x24, waiting for transfers between devices, exchange(): return lax.ppermute(value, axis, [(i, i ^ distance) for i in range(size)])  36.6 us
    ppermute x24, starting transfers between devices, exchange(): return lax.ppermute(value, axis, [(i, i ^ distance) for i in range(size)])  22.6 us
    pallas_call x2, Pallas kernels, unpack(): pl.pallas_call(functools.partial(unpack_kernel, group // width, gather, r...  8.2 us
    pallas_call x2, Pallas kernels, backward(): pl.pallas_call(functools.partial(backward_kernel, groups, place_of, n_par...  2.58 us
    pallas_call x2, Pallas kernels, forward(): pl.pallas_call(functools.partial(forward_kernel, distances, n_col, natura...  2.51 us
  transfers between devices with their start and end apart: 24, of which 13 were waited for; matrix products, arithmetic and copies ran while one was open for 0% of the time, Pallas kernels for 19%

profile of v2, /device:TPU:0, one launch (start us, length us, event | category | flops | bytes accessed | tf_op | source)
XLA Modules:
  0.0 79.6 jit_solution(10849566409545979070)
XLA Ops:
  0.6 0.0 copy-start
  0.6 3.1 %collective-permute-start.3 = (bf16[256,256]{1,0:T(8,128)(2,1)}, bf16[256,256]{1,0:T(8,128)(2,1)S(1)}, u32[]{:S(2)}, u32[]{:S(2)}) collective-permute-start(bf16[256,256]{1,0:T(8,128)(2,1)} %features_hbm.1), channel_id=1, source_target_pairs={{0,8},{4,12},{8,0},{12,4},{16,24},{20,28},{24,16},{28,20},{1,9},{5... | collective-permute-start | bytes 393224 | tf_op jit(solution)/shard_map/ppermute | solution.py:361
  3.8 2.6 %collective-permute-start.5 = (bf16[256,256]{1,0:T(8,128)(2,1)}, bf16[256,256]{1,0:T(8,128)(2,1)S(1)}, u32[]{:S(2)}, u32[]{:S(2)}) collective-permute-start(bf16[256,256]{1,0:T(8,128)(2,1)} %features_hbm.1), channel_id=1, source_target_pairs={{0,16},{4,20},{8,24},{12,28},{16,0},{20,4},{24,8},{28,12},{1,17},{... | collective-permute-start | bytes 393224 | tf_op jit(solution)/shard_map/ppermute | solution.py:361
  6.3 0.0 collective-permute-start
  6.4 1.7 %collective-permute-start.2 = (bf16[256,256]{1,0:T(8,128)(2,1)}, bf16[256,256]{1,0:T(8,128)(2,1)S(1)}, u32[]{:S(2)}, u32[]{:S(2)}) collective-permute-start(bf16[256,256]{1,0:T(8,128)(2,1)} %features_hbm.1), channel_id=1, source_target_pairs={{0,4},{4,0},{8,12},{12,8},{16,20},{20,16},{24,28},{28,24},{1,5},{5... | collective-permute-start | bytes 393224 | tf_op jit(solution)/shard_map/ppermute | solution.py:361
  8.7 0.1 pad_add_fusion.place_ref
  8.8 0.3 collective-permute-done.3.refs_2_
  9.0 1.7 %collective-permute-start.4 = (bf16[256,256]{1,0:T(8,128)(2,1)S(1)}, bf16[256,256]{1,0:T(8,128)(2,1)S(1)}, u32[]{:S(2)}, u32[]{:S(2)}) collective-permute-start(bf16[256,256]{1,0:T(8,128)(2,1)S(1)} %collective-permute-done.3.refs_2_), channel_id=1, source_target_pairs={{0,4},{4,0},{8,12},{12,8},{16,20},{20,16},{24,28},{28,24},{1,5},{5... | collective-permute-start | bytes 393224 | tf_op jit(solution)/shard_map/ppermute | solution.py:361
  10.8 6.1 %collective-permute-done.5.refs_4_ = bf16[256,256]{1,0:T(8,128)(2,1)S(1)} collective-permute-done((bf16[256,256]{1,0:T(8,128)(2,1)}, bf16[256,256]{1,0:T(8,128)(2,1)S(1)}, u32[]{:S(2)}, u32[]{:S(2)}) %collective-permute-start.5) | collective-permute-done | bytes 131104 | tf_op jit(solution)/shard_map/ppermute | solution.py:361
  16.9 1.5 %collective-permute-start.6 = (bf16[256,256]{1,0:T(8,128)(2,1)S(1)}, bf16[256,256]{1,0:T(8,128)(2,1)S(1)}, u32[]{:S(2)}, u32[]{:S(2)}) collective-permute-start(bf16[256,256]{1,0:T(8,128)(2,1)S(1)} %collective-permute-done.5.refs_4_), channel_id=1, source_target_pairs={{0,4},{4,0},{8,12},{12,8},{16,20},{20,16},{24,28},{28,24},{1,5},{5... | collective-permute-start | bytes 393224 | tf_op jit(solution)/shard_map/ppermute | solution.py:361
  18.3 3.7 %unpack_gather.1.adjacency_ref = bf16[1024,2048]{1,0:T(8,128)(2,1)S(1)} custom-call(s32[2]{0:T(128)S(1)} %pad_add_fusion.place_ref, s32[1]{0:T(128)} %bitcast.13.count_ref, s32[1,88]{1,0:T(1,128)} %bitcast.19, s32[88,16,128]{2,1,0:T(8,128)} %bitcast.16), custom_call_target="tpu_custom_call" | custom-call | flops 2000000000 | tf_op jit(solution)/shard_map/unpack_gather/pallas_call | solution.py:127
  22.1 0.0 collective-permute-done.refs_6_
  22.1 0.1 collective-permute-start.1
  22.2 0.0 collective-permute-done.2.refs_1_
  22.2 0.0 collective-permute-done.4.refs_3_
  22.2 0.0 collective-permute-done.6.refs_5_
  22.2 1.7 %forward.1.refs_1_ = f32[1024,256]{1,0:T(8,128)S(1)} custom-call(s32[2]{0:T(128)S(1)} %pad_add_fusion.place_ref, bf16[1024,2048]{1,0:T(8,128)(2,1)S(1)} %unpack_gather.1.adjacency_ref, bf16[256,256]{1,0:T(8,128)(2,1)S(1)} %copy-done, bf16[256,256]{1,0:T(8,128)(2,1)S(1)} %collective-permute-done.2.refs_1_, ...), custom_call_target="tpu_custom_call" | custom-call | flops 1750000000 | tf_op jit(solution)/shard_map/forward/pallas_call | solution.py:208
  23.9 0.0 copy-start.1
  23.9 0.0 copy-start.2
  23.9 0.0 copy-start.3
  23.9 3.2 %collective-permute-done.1.refs_0_ = bf16[256,256]{1,0:T(8,128)(2,1)S(1)} collective-permute-done((bf16[256,256]{1,0:T(8,128)(2,1)S(1)}, bf16[256,256]{1,0:T(8,128)(2,1)S(1)}, u32[]{:S(2)}, u32[]{:S(2)}) %collective-permute-start.1) | collective-permute-done | bytes 131104 | tf_op jit(solution)/shard_map/ppermute | solution.py:361
  27.1 0.8 %forward_last.1 = (f32[512,256]{1,0:T(8,128)S(1)}, bf16[512,256]{1,0:T(8,128)(2,1)S(1)}) custom-call(s32[2]{0:T(128)S(1)} %pad_add_fusion.place_ref, bf16[1024,2048]{1,0:T(8,128)(2,1)S(1)} %unpack_gather.1.adjacency_ref, bf16[256,256]{1,0:T(8,128)(2,1)S(1)} %collective-permute-done.1.refs_0_, f32[1024,256]{1,0:T(8,128)S(1)} %forward.1.refs_1_), custom_call_target="tpu_custom_call" | custom-call | flops 250000000 | tf_op jit(solution)/shard_map/forward_last/pallas_call | solution.py:208
  28.0 0.1 collective-permute-start.7
  28.1 1.0 %near.1.refs_2_.refs_0_ = bf16[528,256]{1,0:T(8,128)(2,1)S(1)} custom-call(s32[1,256]{1,0:T(1,128)} %bitcast.18, bf16[256,256]{1,0:T(8,128)(2,1)} %features_hbm.1, bf16[256,256]{1,0:T(8,128)(2,1)} %cotangents_hbm.1), custom_call_target="tpu_custom_call" | custom-call | flops 500000000 | tf_op jit(solution)/shard_map/near/pallas_call | solution.py:165
  29.1 1.6 %collective-permute-start.9 = (bf16[528,256]{1,0:T(8,128)(2,1)S(1)}, bf16[528,256]{1,0:T(8,128)(2,1)S(1)}, u32[]{:S(2)}, u32[]{:S(2)}) collective-permute-start(bf16[528,256]{1,0:T(8,128)(2,1)S(1)} %near.1.refs_2_.refs_0_), channel_id=1, source_target_pairs={{0,2},{1,3},{2,0},{3,1},{4,6},{5,7},{6,4},{7,5},{8,10},{9,11},{10,... | collective-permute-start | bytes 811016 | tf_op jit(solution)/shard_map/ppermute | solution.py:361
  30.7 0.0 collective-permute-done.7
  30.7 0.1 add_convert_fusion.refs_0_
  30.7 0.6 collective-permute-start.8
  31.3 7.2 %collective-permute-done.9.refs_3_.refs_1_ = bf16[528,256]{1,0:T(8,128)(2,1)S(1)} collective-permute-done((bf16[528,256]{1,0:T(8,128)(2,1)S(1)}, bf16[528,256]{1,0:T(8,128)(2,1)S(1)}, u32[]{:S(2)}, u32[]{:S(2)}) %collective-permute-start.9) | collective-permute-done | bytes 270368 | tf_op jit(solution)/shard_map/ppermute | solution.py:361
  38.5 5.1 %collective-permute-done.8.refs_1_ = bf16[512,256]{1,0:T(8,128)(2,1)S(1)} collective-permute-done((bf16[512,256]{1,0:T(8,128)(2,1)S(1)}, bf16[512,256]{1,0:T(8,128)(2,1)S(1)}, u32[]{:S(2)}, u32[]{:S(2)}) %collective-permute-start.8) | collective-permute-done | bytes 262176 | tf_op jit(solution)/shard_map/ppermute | solution.py:361
  43.6 1.2 %node.1 = (bf16[256,256]{1,0:T(8,128)(2,1)}, bf16[512,256]{1,0:T(8,128)(2,1)S(1)}, bf16[512,256]{1,0:T(8,128)(2,1)S(1)}, bf16[512,256]{1,0:T(8,128)(2,1)S(1)}) custom-call(bf16[512,256]{1,0:T(8,128)(2,1)S(1)} %add_convert_fusion.refs_0_, bf16[512,256]{1,0:T(8,128)(2,1)S(1)} %collective-permute-done.8.refs_1_, bf16[528,256]{1,0:T(8,128)(2,1)S(1)} %near.1.refs_2_.refs_0_, ...), custom_call_target="tpu_custom_call" | custom-call | flops 2000000000 | tf_op jit(solution)/shard_map/node/pallas_call | solution.py:252
  44.9 0.9 %weight.1 = (bf16[2,128,256]{2,1,0:T(8,128)(2,1)S(1)}, f32[256,256]{1,0:T(8,128)S(1)}) custom-call(s32[2]{0:T(128)S(1)} %pad_add_fusion.place_ref, bf16[512,256]{1,0:T(8,128)(2,1)S(1)} %get-tuple-element.26.mean_ref, bf16[512,256]{1,0:T(8,128)(2,1)S(1)} %get-tuple-element.27.grad_ref, bf16[256,256]{1,0:T(8,128)(2,1)S(1)} %copy-done.2, ...), custom_call_target="tpu_custom_call" | custom-call | flops 1300000000 | tf_op jit(solution)/shard_map/weight/pallas_call | solution.py:281
  45.8 0.1 collective-permute-start.17
  45.9 5.0 %collective-permute-done.17 = bf16[2,128,256]{2,1,0:T(8,128)(2,1)S(1)} collective-permute-done((bf16[2,128,256]{2,1,0:T(8,128)(2,1)S(1)}, bf16[2,128,256]{2,1,0:T(8,128)(2,1)S(1)}, u32[]{:S(2)}, u32[]{:S(2)}) %collective-permute-start.17) | collective-permute-done | bytes 131104 | tf_op jit(solution)/shard_map/ppermute | solution.py:361
  51.0 0.1 collective-permute-start.18
  51.0 0.5 collective-permute-start.10
  51.5 0.7 collective-permute-done.18
  52.3 0.1 collective-permute-start.19
  52.4 4.5 %unpack_spread.1 = (bf16[1536,1024]{1,0:T(8,128)(2,1)S(1)}, bf16[512,1024]{1,0:T(8,128)(2,1)S(1)}) custom-call(s32[2]{0:T(128)S(1)} %pad_add_fusion.place_ref, s32[1]{0:T(128)} %bitcast.14.count_ref, s32[1,88]{1,0:T(1,128)} %bitcast.20, s32[88,16,128]{2,1,0:T(8,128)} %bitcast.17, bf16[512,256]{1,0:T(8,128)(2,1)S(1)} %add_convert_fusion.refs_0_), custom_call_target="tpu_custom_call" | custom-call | flops 2000000000 | tf_op jit(solution)/shard_map/unpack_spread/pallas_call | solution.py:127
  56.9 1.0 %backward_far.1 = (bf16[256,256]{1,0:T(8,128)(2,1)S(1)}, bf16[256,256]{1,0:T(8,128)(2,1)S(1)}) custom-call(s32[2]{0:T(128)S(1)} %pad_add_fusion.place_ref, bf16[512,1024]{1,0:T(8,128)(2,1)S(1)} %get-tuple-element.36.adjacency_ref, bf16[512,256]{1,0:T(8,128)(2,1)S(1)} %get-tuple-element.30.mine_ref, bf16[512,256]{1,0:T(8,128)(2,1)S(1)} %collective-permute-done.10.other_ref, ...), custom_call_target="tpu_custom_call" | custom-call | flops 400000000 | tf_op jit(solution)/shard_map/backward_far/pallas_call | solution.py:321
  57.9 0.1 collective-permute-start.14
  58.0 0.5 collective-permute-done.19
  58.5 1.0 %collective-permute-start.20 = (bf16[128,256]{1,0:T(8,128)(2,1)S(1)}, bf16[128,256]{1,0:T(8,128)(2,1)S(1)}, u32[]{:S(2)}, u32[]{:S(2)}) collective-permute-start(bf16[128,256]{1,0:T(8,128)(2,1)S(1)} %add_convert_fusion.5), channel_id=1, source_target_pairs={{0,8},{4,12},{8,0},{12,4},{16,24},{20,28},{24,16},{28,20},{1,9},{5... | collective-permute-start | bytes 196616 | tf_op jit(solution)/shard_map/ppermute | solution.py:361
  59.5 1.6 %backward.1 = (bf16[256,256]{1,0:T(8,128)(2,1)S(1)}, bf16[256,256]{1,0:T(8,128)(2,1)S(1)}, bf16[512,256]{1,0:T(8,128)(2,1)S(1)}, f32[256,256]{1,0:T(8,128)S(1)}, bf16[256,256]{1,0:T(8,128)(2,1)S(1)}) custom-call(s32[2]{0:T(128)S(1)} %pad_add_fusion.place_ref, bf16[1536,1024]{1,0:T(8,128)(2,1)S(1)} %get-tuple-element.29.adjacency_ref, ...), custom_call_target="tpu_custom_call" | custom-call | flops 1200000000 | tf_op jit(solution)/shard_map/backward/pallas_call | solution.py:321
  61.1 2.1 %collective-permute-start.13 = (bf16[256,256]{1,0:T(8,128)(2,1)S(1)}, bf16[256,256]{1,0:T(8,128)(2,1)S(1)}, u32[]{:S(2)}, u32[]{:S(2)}) collective-permute-start(bf16[256,256]{1,0:T(8,128)(2,1)S(1)} %get-tuple-element.35), channel_id=1, source_target_pairs={{0,4},{4,0},{8,12},{12,8},{16,20},{20,16},{24,28},{28,24},{1,5},{5... | collective-permute-start | bytes 393224 | tf_op jit(solution)/shard_map/ppermute | solution.py:361
  63.2 2.1 %collective-permute-start.21 = (f32[128,256]{1,0:T(8,128)S(1)}, f32[128,256]{1,0:T(8,128)S(1)}, u32[]{:S(2)}, u32[]{:S(2)}) collective-permute-start(f32[128,256]{1,0:T(8,128)S(1)} %convert_add_fusion.1.refs_0_), channel_id=1, source_target_pairs={{0,2},{1,3},{2,0},{3,1},{4,6},{5,7},{6,4},{7,5},{8,10},{9,11},{10,... | collective-permute-start | bytes 393224 | tf_op jit(solution)/shard_map/ppermute | solution.py:361
  65.3 0.0 collective-permute-done.14
  65.3 2.1 %collective-permute-start.15 = (bf16[256,256]{1,0:T(8,128)(2,1)S(1)}, bf16[256,256]{1,0:T(8,128)(2,1)S(1)}, u32[]{:S(2)}, u32[]{:S(2)}) collective-permute-start(bf16[256,256]{1,0:T(8,128)(2,1)S(1)} %add_convert_fusion.3), channel_id=1, source_target_pairs={{0,8},{4,12},{8,0},{12,4},{16,24},{20,28},{24,16},{28,20},{1,9},{5... | collective-permute-start | bytes 393224 | tf_op jit(solution)/shard_map/ppermute | solution.py:361
  67.4 0.3 collective-permute-start.11
  67.7 0.0 collective-permute-start.22
  67.7 0.5 collective-permute-done.21.refs_1_
  68.2 0.0 collective-permute-start.23
  68.2 0.0 collective-permute-done.13
  68.3 2.1 %collective-permute-done.15 = bf16[256,256]{1,0:T(8,128)(2,1)S(1)} collective-permute-done((bf16[256,256]{1,0:T(8,128)(2,1)S(1)}, bf16[256,256]{1,0:T(8,128)(2,1)S(1)}, u32[]{:S(2)}, u32[]{:S(2)}) %collective-permute-start.15) | collective-permute-done | bytes 131104 | tf_op jit(solution)/shard_map/ppermute | solution.py:361
  70.3 0.1 add_convert_fusion.2
  70.4 0.8 %collective-permute-start.16 = (bf16[256,256]{1,0:T(8,128)(2,1)S(1)}, bf16[256,256]{1,0:T(8,128)(2,1)S(1)}, u32[]{:S(2)}, u32[]{:S(2)}) collective-permute-start(bf16[256,256]{1,0:T(8,128)(2,1)S(1)} %add_convert_fusion.2), channel_id=1, source_target_pairs={{0,16},{4,20},{8,24},{12,28},{16,0},{20,4},{24,8},{28,12},{1,17},{... | collective-permute-start | bytes 393224 | tf_op jit(solution)/shard_map/ppermute | solution.py:361
  71.2 2.6 %collective-permute-done.11 = bf16[512,256]{1,0:T(8,128)(2,1)S(1)} collective-permute-done((bf16[512,256]{1,0:T(8,128)(2,1)S(1)}, bf16[512,256]{1,0:T(8,128)(2,1)S(1)}, u32[]{:S(2)}, u32[]{:S(2)}) %collective-permute-start.11) | collective-permute-done | bytes 262176 | tf_op jit(solution)/shard_map/ppermute | solution.py:361
  73.8 0.4 collective-permute-start.12
  74.3 0.0 collective-permute-done.22.refs_2_
  74.3 0.0 collective-permute-done.23.refs_3_
  74.3 1.4 %join.1 = (f32[256,256]{1,0:T(8,128)}, f32[256,256]{1,0:T(8,128)}) custom-call(s32[2]{0:T(128)S(1)} %pad_add_fusion.place_ref, f32[128,256]{1,0:T(8,128)S(1)} %convert_add_fusion.1.refs_0_, f32[128,256]{1,0:T(8,128)S(1)} %collective-permute-done.21.refs_1_, f32[128,256]{1,0:T(8,128)S(1)} %collective-permute-done.22.refs_2_, ...), custom_call_target="tpu_custom_call" | custom-call | flops 800000000 | tf_op jit(solution)/shard_map/join/pallas_call | solution.py:348
  75.7 1.2 %collective-permute-done.16 = bf16[256,256]{1,0:T(8,128)(2,1)S(1)} collective-permute-done((bf16[256,256]{1,0:T(8,128)(2,1)S(1)}, bf16[256,256]{1,0:T(8,128)(2,1)S(1)}, u32[]{:S(2)}, u32[]{:S(2)}) %collective-permute-start.16) | collective-permute-done | bytes 131104 | tf_op jit(solution)/shard_map/ppermute | solution.py:361
  76.8 2.0 %collective-permute-done.12 = bf16[256,256]{1,0:T(8,128)(2,1)S(1)} collective-permute-done((bf16[256,256]{1,0:T(8,128)(2,1)S(1)}, bf16[256,256]{1,0:T(8,128)(2,1)S(1)}, u32[]{:S(2)}, u32[]{:S(2)}) %collective-permute-start.12) | collective-permute-done | bytes 131104 | tf_op jit(solution)/shard_map/ppermute | solution.py:361
  78.9 0.7 add_convert_fusion.1
  (13 shorter events, 0.2 us)
Async XLA Ops:
  0.6 21.6 %copy-start = (bf16[256,256]{1,0:T(8,128)(2,1)S(1)}, bf16[256,256]{1,0:T(8,128)(2,1)}, u32[]{:S(2)}) copy-start(bf16[256,256]{1,0:T(8,128)(2,1)} %features_hbm.1) | copy-start | bytes 393220
  0.6 8.4 %collective-permute-start.3 = (bf16[256,256]{1,0:T(8,128)(2,1)}, bf16[256,256]{1,0:T(8,128)(2,1)S(1)}, u32[]{:S(2)}, u32[]{:S(2)}) collective-permute-start(bf16[256,256]{1,0:T(8,128)(2,1)} %features_hbm.1), channel_id=1, source_target_pairs={{0,8},{4,12},{8,0},{12,4},{16,24},{20,28},{24,16},{28,20},{1,9},{5... | collective-permute-start | bytes 393224 | tf_op jit(solution)/shard_map/ppermute | solution.py:361
  3.8 13.1 %collective-permute-start.5 = (bf16[256,256]{1,0:T(8,128)(2,1)}, bf16[256,256]{1,0:T(8,128)(2,1)S(1)}, u32[]{:S(2)}, u32[]{:S(2)}) collective-permute-start(bf16[256,256]{1,0:T(8,128)(2,1)} %features_hbm.1), channel_id=1, source_target_pairs={{0,16},{4,20},{8,24},{12,28},{16,0},{20,4},{24,8},{28,12},{1,17},{... | collective-permute-start | bytes 393224 | tf_op jit(solution)/shard_map/ppermute | solution.py:361
  6.3 15.7 %collective-permute-start = (bf16[256,256]{1,0:T(8,128)(2,1)}, bf16[256,256]{1,0:T(8,128)(2,1)S(1)}, u32[]{:S(2)}, u32[]{:S(2)}) collective-permute-start(bf16[256,256]{1,0:T(8,128)(2,1)} %features_hbm.1), channel_id=1, source_target_pairs={{0,24},{4,28},{8,16},{12,20},{16,8},{20,12},{24,0},{28,4},{1,25},{... | collective-permute-start | bytes 393224 | tf_op jit(solution)/shard_map/ppermute | solution.py:361
  6.4 15.8 %collective-permute-start.2 = (bf16[256,256]{1,0:T(8,128)(2,1)}, bf16[256,256]{1,0:T(8,128)(2,1)S(1)}, u32[]{:S(2)}, u32[]{:S(2)}) collective-permute-start(bf16[256,256]{1,0:T(8,128)(2,1)} %features_hbm.1), channel_id=1, source_target_pairs={{0,4},{4,0},{8,12},{12,8},{16,20},{20,16},{24,28},{28,24},{1,5},{5... | collective-permute-start | bytes 393224 | tf_op jit(solution)/shard_map/ppermute | solution.py:361
  9.0 13.1 %collective-permute-start.4 = (bf16[256,256]{1,0:T(8,128)(2,1)S(1)}, bf16[256,256]{1,0:T(8,128)(2,1)S(1)}, u32[]{:S(2)}, u32[]{:S(2)}) collective-permute-start(bf16[256,256]{1,0:T(8,128)(2,1)S(1)} %collective-permute-done.3.refs_2_), channel_id=1, source_target_pairs={{0,4},{4,0},{8,12},{12,8},{16,20},{20,16},{24,28},{28,24},{1,5},{5... | collective-permute-start | bytes 393224 | tf_op jit(solution)/shard_map/ppermute | solution.py:361
  16.9 5.3 %collective-permute-start.6 = (bf16[256,256]{1,0:T(8,128)(2,1)S(1)}, bf16[256,256]{1,0:T(8,128)(2,1)S(1)}, u32[]{:S(2)}, u32[]{:S(2)}) collective-permute-start(bf16[256,256]{1,0:T(8,128)(2,1)S(1)} %collective-permute-done.5.refs_4_), channel_id=1, source_target_pairs={{0,4},{4,0},{8,12},{12,8},{16,20},{20,16},{24,28},{28,24},{1,5},{5... | collective-permute-start | bytes 393224 | tf_op jit(solution)/shard_map/ppermute | solution.py:361
  22.1 5.0 %collective-permute-start.1 = (bf16[256,256]{1,0:T(8,128)(2,1)S(1)}, bf16[256,256]{1,0:T(8,128)(2,1)S(1)}, u32[]{:S(2)}, u32[]{:S(2)}) collective-permute-start(bf16[256,256]{1,0:T(8,128)(2,1)S(1)} %collective-permute-done.refs_6_), channel_id=1, source_target_pairs={{0,4},{4,0},{8,12},{12,8},{16,20},{20,16},{24,28},{28,24},{1,5},{5... | collective-permute-start | bytes 393224 | tf_op jit(solution)/shard_map/ppermute | solution.py:361
  23.9 19.7 %copy-start.1 = (bf16[256,256]{1,0:T(8,128)(2,1)S(1)}, bf16[256,256]{1,0:T(8,128)(2,1)}, u32[]{:S(2)}) copy-start(bf16[256,256]{1,0:T(8,128)(2,1)} %refs_5_.1) | copy-start | bytes 393220
  23.9 19.7 %copy-start.2 = (bf16[256,256]{1,0:T(8,128)(2,1)S(1)}, bf16[256,256]{1,0:T(8,128)(2,1)}, u32[]{:S(2)}) copy-start(bf16[256,256]{1,0:T(8,128)(2,1)} %w_self.1) | copy-start | bytes 393220
  23.9 19.7 %copy-start.3 = (f32[256]{0:T(256)S(1)}, f32[256]{0:T(256)}, u32[]{:S(2)}) copy-start(f32[256]{0:T(256)} %param.14) | copy-start | bytes 3076
  28.0 2.7 %collective-permute-start.7 = (bf16[512,256]{1,0:T(8,128)(2,1)S(1)}, bf16[512,256]{1,0:T(8,128)(2,1)S(1)}, u32[]{:S(2)}, u32[]{:S(2)}) collective-permute-start(bf16[512,256]{1,0:T(8,128)(2,1)S(1)} %get-tuple-element.24), channel_id=1, source_target_pairs={{0,1},{1,0},{2,3},{3,2},{4,5},{5,4},{6,7},{7,6},{8,9},{9,8},{10,11... | collective-permute-start | bytes 786440 | tf_op jit(solution)/shard_map/ppermute | solution.py:361
  29.1 9.4 %collective-permute-start.9 = (bf16[528,256]{1,0:T(8,128)(2,1)S(1)}, bf16[528,256]{1,0:T(8,128)(2,1)S(1)}, u32[]{:S(2)}, u32[]{:S(2)}) collective-permute-start(bf16[528,256]{1,0:T(8,128)(2,1)S(1)} %near.1.refs_2_.refs_0_), channel_id=1, source_target_pairs={{0,2},{1,3},{2,0},{3,1},{4,6},{5,7},{6,4},{7,5},{8,10},{9,11},{10,... | collective-permute-start | bytes 811016 | tf_op jit(solution)/shard_map/ppermute | solution.py:361
  30.7 12.9 %collective-permute-start.8 = (bf16[512,256]{1,0:T(8,128)(2,1)S(1)}, bf16[512,256]{1,0:T(8,128)(2,1)S(1)}, u32[]{:S(2)}, u32[]{:S(2)}) collective-permute-start(bf16[512,256]{1,0:T(8,128)(2,1)S(1)} %add_convert_fusion.refs_0_), channel_id=1, source_target_pairs={{0,2},{1,3},{2,0},{3,1},{4,6},{5,7},{6,4},{7,5},{8,10},{9,11},{10,... | collective-permute-start | bytes 786440 | tf_op jit(solution)/shard_map/ppermute | solution.py:361
  45.8 5.1 %collective-permute-start.17 = (bf16[2,128,256]{2,1,0:T(8,128)(2,1)S(1)}, bf16[2,128,256]{2,1,0:T(8,128)(2,1)S(1)}, u32[]{:S(2)}, u32[]{:S(2)}) collective-permute-start(bf16[2,128,256]{2,1,0:T(8,128)(2,1)S(1)} %get-tuple-element.37.refs_0_), channel_id=1, source_target_pairs={{0,4},{4,0},{8,12},{12,8},{16,20},{20,16},{24,28},{28,24},{1,5},{5... | collective-permute-start | bytes 393224 | tf_op jit(solution)/shard_map/ppermute | solution.py:361
  51.0 1.3 %collective-permute-start.18 = (bf16[128,256]{1,0:T(8,128)(2,1)S(1)}, bf16[128,256]{1,0:T(8,128)(2,1)S(1)}, u32[]{:S(2)}, u32[]{:S(2)}) collective-permute-start(bf16[128,256]{1,0:T(8,128)(2,1)S(1)} %fusion.1), channel_id=1, source_target_pairs={{0,1},{1,0},{2,3},{3,2},{4,5},{5,4},{6,7},{7,6},{8,9},{9,8},{10,11... | collective-permute-start | bytes 196616 | tf_op jit(solution)/shard_map/ppermute | solution.py:361
  51.0 5.8 %collective-permute-start.10 = (bf16[512,256]{1,0:T(8,128)(2,1)S(1)}, bf16[512,256]{1,0:T(8,128)(2,1)S(1)}, u32[]{:S(2)}, u32[]{:S(2)}) collective-permute-start(bf16[512,256]{1,0:T(8,128)(2,1)S(1)} %get-tuple-element.30.mine_ref), channel_id=1, source_target_pairs={{0,1},{1,0},{2,3},{3,2},{4,5},{5,4},{6,7},{7,6},{8,9},{9,8},{10,11... | collective-permute-start | bytes 786440 | tf_op jit(solution)/shard_map/ppermute | solution.py:361
  52.3 6.2 %collective-permute-start.19 = (bf16[128,256]{1,0:T(8,128)(2,1)S(1)}, bf16[128,256]{1,0:T(8,128)(2,1)S(1)}, u32[]{:S(2)}, u32[]{:S(2)}) collective-permute-start(bf16[128,256]{1,0:T(8,128)(2,1)S(1)} %fusion), channel_id=1, source_target_pairs={{0,16},{4,20},{8,24},{12,28},{16,0},{20,4},{24,8},{28,12},{1,17},{... | collective-permute-start | bytes 196616 | tf_op jit(solution)/shard_map/ppermute | solution.py:361
  57.9 7.4 %collective-permute-start.14 = (bf16[256,256]{1,0:T(8,128)(2,1)S(1)}, bf16[256,256]{1,0:T(8,128)(2,1)S(1)}, u32[]{:S(2)}, u32[]{:S(2)}) collective-permute-start(bf16[256,256]{1,0:T(8,128)(2,1)S(1)} %get-tuple-element.39), channel_id=1, source_target_pairs={{0,4},{4,0},{8,12},{12,8},{16,20},{20,16},{24,28},{28,24},{1,5},{5... | collective-permute-start | bytes 393224 | tf_op jit(solution)/shard_map/ppermute | solution.py:361
  58.5 4.7 %collective-permute-start.20 = (bf16[128,256]{1,0:T(8,128)(2,1)S(1)}, bf16[128,256]{1,0:T(8,128)(2,1)S(1)}, u32[]{:S(2)}, u32[]{:S(2)}) collective-permute-start(bf16[128,256]{1,0:T(8,128)(2,1)S(1)} %add_convert_fusion.5), channel_id=1, source_target_pairs={{0,8},{4,12},{8,0},{12,4},{16,24},{20,28},{24,16},{28,20},{1,9},{5... | collective-permute-start | bytes 196616 | tf_op jit(solution)/shard_map/ppermute | solution.py:361
  61.1 7.1 %collective-permute-start.13 = (bf16[256,256]{1,0:T(8,128)(2,1)S(1)}, bf16[256,256]{1,0:T(8,128)(2,1)S(1)}, u32[]{:S(2)}, u32[]{:S(2)}) collective-permute-start(bf16[256,256]{1,0:T(8,128)(2,1)S(1)} %get-tuple-element.35), channel_id=1, source_target_pairs={{0,4},{4,0},{8,12},{12,8},{16,20},{20,16},{24,28},{28,24},{1,5},{5... | collective-permute-start | bytes 393224 | tf_op jit(solution)/shard_map/ppermute | solution.py:361
  63.2 5.0 %collective-permute-start.21 = (f32[128,256]{1,0:T(8,128)S(1)}, f32[128,256]{1,0:T(8,128)S(1)}, u32[]{:S(2)}, u32[]{:S(2)}) collective-permute-start(f32[128,256]{1,0:T(8,128)S(1)} %convert_add_fusion.1.refs_0_), channel_id=1, source_target_pairs={{0,2},{1,3},{2,0},{3,1},{4,6},{5,7},{6,4},{7,5},{8,10},{9,11},{10,... | collective-permute-start | bytes 393224 | tf_op jit(solution)/shard_map/ppermute | solution.py:361
  65.3 5.0 %collective-permute-start.15 = (bf16[256,256]{1,0:T(8,128)(2,1)S(1)}, bf16[256,256]{1,0:T(8,128)(2,1)S(1)}, u32[]{:S(2)}, u32[]{:S(2)}) collective-permute-start(bf16[256,256]{1,0:T(8,128)(2,1)S(1)} %add_convert_fusion.3), channel_id=1, source_target_pairs={{0,8},{4,12},{8,0},{12,4},{16,24},{20,28},{24,16},{28,20},{1,9},{5... | collective-permute-start | bytes 393224 | tf_op jit(solution)/shard_map/ppermute | solution.py:361
  67.4 6.4 %collective-permute-start.11 = (bf16[512,256]{1,0:T(8,128)(2,1)S(1)}, bf16[512,256]{1,0:T(8,128)(2,1)S(1)}, u32[]{:S(2)}, u32[]{:S(2)}) collective-permute-start(bf16[512,256]{1,0:T(8,128)(2,1)S(1)} %get-tuple-element.32), channel_id=1, source_target_pairs={{0,4},{4,0},{8,12},{12,8},{16,20},{20,16},{24,28},{28,24},{1,5},{5... | collective-permute-start | bytes 786440 | tf_op jit(solution)/shard_map/ppermute | solution.py:361
  67.7 6.5 %collective-permute-start.22 = (f32[128,256]{1,0:T(8,128)S(1)}, f32[128,256]{1,0:T(8,128)S(1)}, u32[]{:S(2)}, u32[]{:S(2)}) collective-permute-start(f32[128,256]{1,0:T(8,128)S(1)} %convert_add_fusion.1.refs_0_), channel_id=1, source_target_pairs={{0,1},{1,0},{2,3},{3,2},{4,5},{5,4},{6,7},{7,6},{8,9},{9,8},{10,11... | collective-permute-start | bytes 393224 | tf_op jit(solution)/shard_map/ppermute | solution.py:361
  68.2 6.0 %collective-permute-start.23 = (f32[128,256]{1,0:T(8,128)S(1)}, f32[128,256]{1,0:T(8,128)S(1)}, u32[]{:S(2)}, u32[]{:S(2)}) collective-permute-start(f32[128,256]{1,0:T(8,128)S(1)} %collective-permute-done.21.refs_1_), channel_id=1, source_target_pairs={{0,1},{1,0},{2,3},{3,2},{4,5},{5,4},{6,7},{7,6},{8,9},{9,8},{10,11... | collective-permute-start | bytes 393224 | tf_op jit(solution)/shard_map/ppermute | solution.py:361
  70.4 6.4 %collective-permute-start.16 = (bf16[256,256]{1,0:T(8,128)(2,1)S(1)}, bf16[256,256]{1,0:T(8,128)(2,1)S(1)}, u32[]{:S(2)}, u32[]{:S(2)}) collective-permute-start(bf16[256,256]{1,0:T(8,128)(2,1)S(1)} %add_convert_fusion.2), channel_id=1, source_target_pairs={{0,16},{4,20},{8,24},{12,28},{16,0},{20,4},{24,8},{28,12},{1,17},{... | collective-permute-start | bytes 393224 | tf_op jit(solution)/shard_map/ppermute | solution.py:361
  73.8 5.0 %collective-permute-start.12 = (bf16[256,256]{1,0:T(8,128)(2,1)S(1)}, bf16[256,256]{1,0:T(8,128)(2,1)S(1)}, u32[]{:S(2)}, u32[]{:S(2)}) collective-permute-start(bf16[256,256]{1,0:T(8,128)(2,1)S(1)} %add_convert_fusion.4), channel_id=1, source_target_pairs={{0,8},{4,12},{8,0},{12,4},{16,24},{20,28},{24,16},{28,20},{1,9},{5... | collective-permute-start | bytes 393224 | tf_op jit(solution)/shard_map/ppermute | solution.py:361

commit v3 on v2

--- a/solution.py
+++ b/solution.py
@@ -336,7 +336,7 @@
     first = lax.rem(place_ref[1], 2) == 0
     for h in range(n_part):
         here = span(jnp.bitwise_xor(lax.div(place_ref[1], 2), h), mine[h].shape[0])
-        one, two = mine[h][...] * scale, others[h][...] * scale
+        one, two = mine[h][...].astype(f32) * scale, others[h][...].astype(f32) * scale
         self_ref[here, :] = jnp.where(first, one, two)
         neigh_ref[here, :] = jnp.where(first, two, one)
 
@@ -432,12 +432,13 @@
     keep = jnp.where(core, sums[0], sums[1])
     send = jnp.where(core, sums[1], sums[0]).astype(bf16)
     grads = keep + exchange(send, "col", 1).astype(f32)
+    rounded = grads.astype(bf16)
     distance = n_row // 2
     while distance > 1:
-        rounded = grads.astype(bf16)
         came = exchange(rounded, "row", distance)
-        grads = rounded.astype(f32) + came.astype(f32)
+        rounded = (rounded.astype(f32) + came.astype(f32)).astype(bf16)
         distance //= 2
+    grads = rounded
     mine = [grads] + [exchange(grads, "col", 2 * h) for h in range(1, n_part)]
     others = [exchange(value, "col", 1) for value in mine]
     scale = 1.0 / math.sqrt(panel * n_col)

time: 79.8 us -> 81.4 us (1.020)
  starting transfers between devices: 22.6 us -> 25.1 us
  waiting for transfers between devices: 36.6 us -> 35.6 us
    ppermute x24, starting transfers between devices: 22.6 us -> 25.1 us  [exchange(): return lax.ppermute(value, axis, [(i, i ^ distance) for i in range(size)])]
    ppermute x24, waiting for transfers between devices: 36.6 us -> 35.6 us  [exchange(): return lax.ppermute(value, axis, [(i, i ^ distance) for i in range(size)])]
  transfers between devices with their start and end apart: 24 -> 24, of which waited for: 13 -> 12; matrix products, arithmetic and copies ran while one was open for 0% -> 0% of each run, Pallas kernels for 19% -> 18%
where the time goes in v3:
time: 81.4 us; the launch traced here: 81.3 us
  waiting for transfers between devices  35.6 us (44%)
  starting transfers between devices  25.1 us (31%)
  Pallas kernels  17.8 us (22%)
  between operations  1.56 us (2%)
  other arithmetic  1.1 us (1%)
    ppermute x24, waiting for transfers between devices, exchange(): return lax.ppermute(value, axis, [(i, i ^ distance) for i in range(size)])  35.6 us
    ppermute x24, starting transfers between devices, exchange(): return lax.ppermute(value, axis, [(i, i ^ distance) for i in range(size)])  25.1 us
    pallas_call x2, Pallas kernels, unpack(): pl.pallas_call(functools.partial(unpack_kernel, group // width, gather, r...  8.2 us
    pallas_call x2, Pallas kernels, backward(): pl.pallas_call(functools.partial(backward_kernel, groups, place_of, n_par...  2.59 us
    pallas_call x2, Pallas kernels, forward(): pl.pallas_call(functools.partial(forward_kernel, distances, n_col, natura...  2.51 us
  transfers between devices with their start and end apart: 24, of which 12 were waited for; matrix products, arithmetic and copies ran while one was open for 0% of the time, Pallas kernels for 18%

profile of v3, /device:TPU:0, one launch (start us, length us, event | category | flops | bytes accessed | tf_op | source)
XLA Modules:
  0.0 81.3 jit_solution(5688921730954974062)
XLA Ops:
  0.6 0.0 copy-start
  0.6 3.1 %collective-permute-start.3 = (bf16[256,256]{1,0:T(8,128)(2,1)}, bf16[256,256]{1,0:T(8,128)(2,1)S(1)}, u32[]{:S(2)}, u32[]{:S(2)}) collective-permute-start(bf16[256,256]{1,0:T(8,128)(2,1)} %features_hbm.1), channel_id=1, source_target_pairs={{0,8},{4,12},{8,0},{12,4},{16,24},{20,28},{24,16},{28,20},{1,9},{5... | collective-permute-start | bytes 393224 | tf_op jit(solution)/shard_map/ppermute | solution.py:361
  3.8 2.6 %collective-permute-start.5 = (bf16[256,256]{1,0:T(8,128)(2,1)}, bf16[256,256]{1,0:T(8,128)(2,1)S(1)}, u32[]{:S(2)}, u32[]{:S(2)}) collective-permute-start(bf16[256,256]{1,0:T(8,128)(2,1)} %features_hbm.1), channel_id=1, source_target_pairs={{0,16},{4,20},{8,24},{12,28},{16,0},{20,4},{24,8},{28,12},{1,17},{... | collective-permute-start | bytes 393224 | tf_op jit(solution)/shard_map/ppermute | solution.py:361
  6.3 0.0 collective-permute-start
  6.4 1.7 %collective-permute-start.2 = (bf16[256,256]{1,0:T(8,128)(2,1)}, bf16[256,256]{1,0:T(8,128)(2,1)S(1)}, u32[]{:S(2)}, u32[]{:S(2)}) collective-permute-start(bf16[256,256]{1,0:T(8,128)(2,1)} %features_hbm.1), channel_id=1, source_target_pairs={{0,4},{4,0},{8,12},{12,8},{16,20},{20,16},{24,28},{28,24},{1,5},{5... | collective-permute-start | bytes 393224 | tf_op jit(solution)/shard_map/ppermute | solution.py:361
  8.7 0.1 pad_add_fusion.place_ref
  8.8 0.3 collective-permute-done.3.refs_2_
  9.0 1.7 %collective-permute-start.4 = (bf16[256,256]{1,0:T(8,128)(2,1)S(1)}, bf16[256,256]{1,0:T(8,128)(2,1)S(1)}, u32[]{:S(2)}, u32[]{:S(2)}) collective-permute-start(bf16[256,256]{1,0:T(8,128)(2,1)S(1)} %collective-permute-done.3.refs_2_), channel_id=1, source_target_pairs={{0,4},{4,0},{8,12},{12,8},{16,20},{20,16},{24,28},{28,24},{1,5},{5... | collective-permute-start | bytes 393224 | tf_op jit(solution)/shard_map/ppermute | solution.py:361
  10.8 6.1 %collective-permute-done.5.refs_4_ = bf16[256,256]{1,0:T(8,128)(2,1)S(1)} collective-permute-done((bf16[256,256]{1,0:T(8,128)(2,1)}, bf16[256,256]{1,0:T(8,128)(2,1)S(1)}, u32[]{:S(2)}, u32[]{:S(2)}) %collective-permute-start.5) | collective-permute-done | bytes 131104 | tf_op jit(solution)/shard_map/ppermute | solution.py:361
  16.9 1.5 %collective-permute-start.6 = (bf16[256,256]{1,0:T(8,128)(2,1)S(1)}, bf16[256,256]{1,0:T(8,128)(2,1)S(1)}, u32[]{:S(2)}, u32[]{:S(2)}) collective-permute-start(bf16[256,256]{1,0:T(8,128)(2,1)S(1)} %collective-permute-done.5.refs_4_), channel_id=1, source_target_pairs={{0,4},{4,0},{8,12},{12,8},{16,20},{20,16},{24,28},{28,24},{1,5},{5... | collective-permute-start | bytes 393224 | tf_op jit(solution)/shard_map/ppermute | solution.py:361
  18.3 3.7 %unpack_gather.1.adjacency_ref = bf16[1024,2048]{1,0:T(8,128)(2,1)S(1)} custom-call(s32[2]{0:T(128)S(1)} %pad_add_fusion.place_ref, s32[1]{0:T(128)} %bitcast.13.count_ref, s32[1,88]{1,0:T(1,128)} %bitcast.19, s32[88,16,128]{2,1,0:T(8,128)} %bitcast.16), custom_call_target="tpu_custom_call" | custom-call | flops 2000000000 | tf_op jit(solution)/shard_map/unpack_gather/pallas_call | solution.py:127
  22.1 0.0 collective-permute-done.refs_6_
  22.1 0.1 collective-permute-start.1
  22.2 0.0 collective-permute-done.2.refs_1_
  22.2 0.0 collective-permute-done.4.refs_3_
  22.2 0.0 collective-permute-done.6.refs_5_
  22.2 1.7 %forward.1.refs_1_ = f32[1024,256]{1,0:T(8,128)S(1)} custom-call(s32[2]{0:T(128)S(1)} %pad_add_fusion.place_ref, bf16[1024,2048]{1,0:T(8,128)(2,1)S(1)} %unpack_gather.1.adjacency_ref, bf16[256,256]{1,0:T(8,128)(2,1)S(1)} %copy-done, bf16[256,256]{1,0:T(8,128)(2,1)S(1)} %collective-permute-done.2.refs_1_, ...), custom_call_target="tpu_custom_call" | custom-call | flops 1750000000 | tf_op jit(solution)/shard_map/forward/pallas_call | solution.py:208
  23.9 0.0 copy-start.1
  23.9 0.0 copy-start.2
  23.9 0.0 copy-start.3
  23.9 3.2 %collective-permute-done.1.refs_0_ = bf16[256,256]{1,0:T(8,128)(2,1)S(1)} collective-permute-done((bf16[256,256]{1,0:T(8,128)(2,1)S(1)}, bf16[256,256]{1,0:T(8,128)(2,1)S(1)}, u32[]{:S(2)}, u32[]{:S(2)}) %collective-permute-start.1) | collective-permute-done | bytes 131104 | tf_op jit(solution)/shard_map/ppermute | solution.py:361
  27.1 0.8 %forward_last.1 = (f32[512,256]{1,0:T(8,128)S(1)}, bf16[512,256]{1,0:T(8,128)(2,1)S(1)}) custom-call(s32[2]{0:T(128)S(1)} %pad_add_fusion.place_ref, bf16[1024,2048]{1,0:T(8,128)(2,1)S(1)} %unpack_gather.1.adjacency_ref, bf16[256,256]{1,0:T(8,128)(2,1)S(1)} %collective-permute-done.1.refs_0_, f32[1024,256]{1,0:T(8,128)S(1)} %forward.1.refs_1_), custom_call_target="tpu_custom_call" | custom-call | flops 250000000 | tf_op jit(solution)/shard_map/forward_last/pallas_call | solution.py:208
  28.0 0.1 collective-permute-start.7
  28.1 1.0 %near.1.refs_2_.refs_0_ = bf16[528,256]{1,0:T(8,128)(2,1)S(1)} custom-call(s32[1,256]{1,0:T(1,128)} %bitcast.18, bf16[256,256]{1,0:T(8,128)(2,1)} %features_hbm.1, bf16[256,256]{1,0:T(8,128)(2,1)} %cotangents_hbm.1), custom_call_target="tpu_custom_call" | custom-call | flops 500000000 | tf_op jit(solution)/shard_map/near/pallas_call | solution.py:165
  29.1 1.6 %collective-permute-start.9 = (bf16[528,256]{1,0:T(8,128)(2,1)S(1)}, bf16[528,256]{1,0:T(8,128)(2,1)S(1)}, u32[]{:S(2)}, u32[]{:S(2)}) collective-permute-start(bf16[528,256]{1,0:T(8,128)(2,1)S(1)} %near.1.refs_2_.refs_0_), channel_id=1, source_target_pairs={{0,2},{1,3},{2,0},{3,1},{4,6},{5,7},{6,4},{7,5},{8,10},{9,11},{10,... | collective-permute-start | bytes 811016 | tf_op jit(solution)/shard_map/ppermute | solution.py:361
  30.7 0.0 collective-permute-done.7
  30.7 0.1 add_convert_fusion.refs_0_
  30.7 0.6 collective-permute-start.8
  31.3 7.2 %collective-permute-done.9.refs_3_.refs_1_ = bf16[528,256]{1,0:T(8,128)(2,1)S(1)} collective-permute-done((bf16[528,256]{1,0:T(8,128)(2,1)S(1)}, bf16[528,256]{1,0:T(8,128)(2,1)S(1)}, u32[]{:S(2)}, u32[]{:S(2)}) %collective-permute-start.9) | collective-permute-done | bytes 270368 | tf_op jit(solution)/shard_map/ppermute | solution.py:361
  38.5 5.1 %collective-permute-done.8.refs_1_ = bf16[512,256]{1,0:T(8,128)(2,1)S(1)} collective-permute-done((bf16[512,256]{1,0:T(8,128)(2,1)S(1)}, bf16[512,256]{1,0:T(8,128)(2,1)S(1)}, u32[]{:S(2)}, u32[]{:S(2)}) %collective-permute-start.8) | collective-permute-done | bytes 262176 | tf_op jit(solution)/shard_map/ppermute | solution.py:361
  43.6 1.2 %node.1 = (bf16[256,256]{1,0:T(8,128)(2,1)}, bf16[512,256]{1,0:T(8,128)(2,1)S(1)}, bf16[512,256]{1,0:T(8,128)(2,1)S(1)}, bf16[512,256]{1,0:T(8,128)(2,1)S(1)}) custom-call(bf16[512,256]{1,0:T(8,128)(2,1)S(1)} %add_convert_fusion.refs_0_, bf16[512,256]{1,0:T(8,128)(2,1)S(1)} %collective-permute-done.8.refs_1_, bf16[528,256]{1,0:T(8,128)(2,1)S(1)} %near.1.refs_2_.refs_0_, ...), custom_call_target="tpu_custom_call" | custom-call | flops 2000000000 | tf_op jit(solution)/shard_map/node/pallas_call | solution.py:252
  44.9 0.9 %weight.1 = (bf16[2,128,256]{2,1,0:T(8,128)(2,1)S(1)}, f32[256,256]{1,0:T(8,128)S(1)}) custom-call(s32[2]{0:T(128)S(1)} %pad_add_fusion.place_ref, bf16[512,256]{1,0:T(8,128)(2,1)S(1)} %get-tuple-element.26.mean_ref, bf16[512,256]{1,0:T(8,128)(2,1)S(1)} %get-tuple-element.27.grad_ref, bf16[256,256]{1,0:T(8,128)(2,1)S(1)} %copy-done.2, ...), custom_call_target="tpu_custom_call" | custom-call | flops 1300000000 | tf_op jit(solution)/shard_map/weight/pallas_call | solution.py:281
  45.8 0.1 collective-permute-start.17
  45.9 0.1 collective-permute-start.10
  46.0 4.9 %collective-permute-done.17 = bf16[2,128,256]{2,1,0:T(8,128)(2,1)S(1)} collective-permute-done((bf16[2,128,256]{2,1,0:T(8,128)(2,1)S(1)}, bf16[2,128,256]{2,1,0:T(8,128)(2,1)S(1)}, u32[]{:S(2)}, u32[]{:S(2)}) %collective-permute-start.17) | collective-permute-done | bytes 131104 | tf_op jit(solution)/shard_map/ppermute | solution.py:361
  51.0 0.1 collective-permute-start.18
  51.0 4.5 %unpack_spread.1 = (bf16[1536,1024]{1,0:T(8,128)(2,1)S(1)}, bf16[512,1024]{1,0:T(8,128)(2,1)S(1)}) custom-call(s32[2]{0:T(128)S(1)} %pad_add_fusion.place_ref, s32[1]{0:T(128)} %bitcast.14.count_ref, s32[1,88]{1,0:T(1,128)} %bitcast.20, s32[88,16,128]{2,1,0:T(8,128)} %bitcast.17, bf16[512,256]{1,0:T(8,128)(2,1)S(1)} %add_convert_fusion.refs_0_), custom_call_target="tpu_custom_call" | custom-call | flops 2000000000 | tf_op jit(solution)/shard_map/unpack_spread/pallas_call | solution.py:127
  55.5 0.0 collective-permute-done.18
  55.6 0.1 collective-permute-start.19
  55.6 0.0 collective-permute-done.10.other_ref
  55.7 1.0 %backward_far.1 = (bf16[256,256]{1,0:T(8,128)(2,1)S(1)}, bf16[256,256]{1,0:T(8,128)(2,1)S(1)}) custom-call(s32[2]{0:T(128)S(1)} %pad_add_fusion.place_ref, bf16[512,1024]{1,0:T(8,128)(2,1)S(1)} %get-tuple-element.36.adjacency_ref, bf16[512,256]{1,0:T(8,128)(2,1)S(1)} %get-tuple-element.30.mine_ref, bf16[512,256]{1,0:T(8,128)(2,1)S(1)} %collective-permute-done.10.other_ref, ...), custom_call_target="tpu_custom_call" | custom-call | flops 400000000 | tf_op jit(solution)/shard_map/backward_far/pallas_call | solution.py:321
  56.7 0.1 collective-permute-start.14
  56.8 1.6 %backward.1 = (bf16[256,256]{1,0:T(8,128)(2,1)S(1)}, bf16[256,256]{1,0:T(8,128)(2,1)S(1)}, bf16[512,256]{1,0:T(8,128)(2,1)S(1)}, f32[256,256]{1,0:T(8,128)S(1)}, bf16[256,256]{1,0:T(8,128)(2,1)S(1)}) custom-call(s32[2]{0:T(128)S(1)} %pad_add_fusion.place_ref, bf16[1536,1024]{1,0:T(8,128)(2,1)S(1)} %get-tuple-element.29.adjacency_ref, ...), custom_call_target="tpu_custom_call" | custom-call | flops 1200000000 | tf_op jit(solution)/shard_map/backward/pallas_call | solution.py:321
  58.3 2.1 %collective-permute-start.13 = (bf16[256,256]{1,0:T(8,128)(2,1)S(1)}, bf16[256,256]{1,0:T(8,128)(2,1)S(1)}, u32[]{:S(2)}, u32[]{:S(2)}) collective-permute-start(bf16[256,256]{1,0:T(8,128)(2,1)S(1)} %get-tuple-element.35), channel_id=1, source_target_pairs={{0,4},{4,0},{8,12},{12,8},{16,20},{20,16},{24,28},{28,24},{1,5},{5... | collective-permute-start | bytes 393224 | tf_op jit(solution)/shard_map/ppermute | solution.py:361
  60.4 0.5 collective-permute-done.19
  60.9 2.4 %collective-permute-start.20 = (bf16[128,256]{1,0:T(8,128)(2,1)S(1)}, bf16[128,256]{1,0:T(8,128)(2,1)S(1)}, u32[]{:S(2)}, u32[]{:S(2)}) collective-permute-start(bf16[128,256]{1,0:T(8,128)(2,1)S(1)} %add_convert_fusion.6), channel_id=1, source_target_pairs={{0,8},{4,12},{8,0},{12,4},{16,24},{20,28},{24,16},{28,20},{1,9},{5... | collective-permute-start | bytes 196616 | tf_op jit(solution)/shard_map/ppermute | solution.py:361
  63.3 0.0 collective-permute-done.14
  63.4 1.9 %collective-permute-start.15 = (bf16[256,256]{1,0:T(8,128)(2,1)S(1)}, bf16[256,256]{1,0:T(8,128)(2,1)S(1)}, u32[]{:S(2)}, u32[]{:S(2)}) collective-permute-start(bf16[256,256]{1,0:T(8,128)(2,1)S(1)} %add_convert_fusion.3), channel_id=1, source_target_pairs={{0,8},{4,12},{8,0},{12,4},{16,24},{20,28},{24,16},{28,20},{1,9},{5... | collective-permute-start | bytes 393224 | tf_op jit(solution)/shard_map/ppermute | solution.py:361
  65.3 0.3 collective-permute-done.20
  65.6 2.2 %collective-permute-start.21 = (bf16[128,256]{1,0:T(8,128)(2,1)S(1)}, bf16[128,256]{1,0:T(8,128)(2,1)S(1)}, u32[]{:S(2)}, u32[]{:S(2)}) collective-permute-start(bf16[128,256]{1,0:T(8,128)(2,1)S(1)} %add_convert_fusion.5.refs_0_), channel_id=1, source_target_pairs={{0,2},{1,3},{2,0},{3,1},{4,6},{5,7},{6,4},{7,5},{8,10},{9,11},{10,... | collective-permute-start | bytes 196616 | tf_op jit(solution)/shard_map/ppermute | solution.py:361
  67.8 0.5 collective-permute-start.11
  68.3 0.0 collective-permute-start.22
  68.3 1.7 %collective-permute-done.21.refs_1_ = bf16[128,256]{1,0:T(8,128)(2,1)S(1)} collective-permute-done((bf16[128,256]{1,0:T(8,128)(2,1)S(1)}, bf16[128,256]{1,0:T(8,128)(2,1)S(1)}, u32[]{:S(2)}, u32[]{:S(2)}) %collective-permute-start.21) | collective-permute-done | bytes 65568 | tf_op jit(solution)/shard_map/ppermute | solution.py:361
  70.0 0.0 collective-permute-start.23
  70.0 0.0 collective-permute-done.13
  70.0 0.0 collective-permute-done.15
  70.0 0.1 add_convert_fusion.2
  70.1 2.1 %collective-permute-start.16 = (bf16[256,256]{1,0:T(8,128)(2,1)S(1)}, bf16[256,256]{1,0:T(8,128)(2,1)S(1)}, u32[]{:S(2)}, u32[]{:S(2)}) collective-permute-start(bf16[256,256]{1,0:T(8,128)(2,1)S(1)} %add_convert_fusion.2), channel_id=1, source_target_pairs={{0,16},{4,20},{8,24},{12,28},{16,0},{20,4},{24,8},{28,12},{1,17},{... | collective-permute-start | bytes 393224 | tf_op jit(solution)/shard_map/ppermute | solution.py:361
  72.2 2.0 %collective-permute-done.11 = bf16[512,256]{1,0:T(8,128)(2,1)S(1)} collective-permute-done((bf16[512,256]{1,0:T(8,128)(2,1)S(1)}, bf16[512,256]{1,0:T(8,128)(2,1)S(1)}, u32[]{:S(2)}, u32[]{:S(2)}) %collective-permute-start.11) | collective-permute-done | bytes 262176 | tf_op jit(solution)/shard_map/ppermute | solution.py:361
  74.2 0.6 collective-permute-start.12
  74.8 1.4 %join.1 = (f32[256,256]{1,0:T(8,128)}, f32[256,256]{1,0:T(8,128)}) custom-call(s32[2]{0:T(128)S(1)} %pad_add_fusion.place_ref, bf16[128,256]{1,0:T(8,128)(2,1)S(1)} %add_convert_fusion.5.refs_0_, bf16[128,256]{1,0:T(8,128)(2,1)S(1)} %collective-permute-done.21.refs_1_, bf16[128,256]{1,0:T(8,128)(2,1)S(1)} %collective-permute-done.22.refs_2_, ...), custom_call_target="tpu_custom_call" | custom-call | flops 800000000 | tf_op jit(solution)/shard_map/join/pallas_call | solution.py:348
  76.2 3.7 %collective-permute-done.16 = bf16[256,256]{1,0:T(8,128)(2,1)S(1)} collective-permute-done((bf16[256,256]{1,0:T(8,128)(2,1)S(1)}, bf16[256,256]{1,0:T(8,128)(2,1)S(1)}, u32[]{:S(2)}, u32[]{:S(2)}) %collective-permute-start.16) | collective-permute-done | bytes 131104 | tf_op jit(solution)/shard_map/ppermute | solution.py:361
  79.9 0.7 collective-permute-done.12
  80.5 0.7 add_convert_fusion.1
  (13 shorter events, 0.2 us)
Async XLA Ops:
  0.6 21.6 %copy-start = (bf16[256,256]{1,0:T(8,128)(2,1)S(1)}, bf16[256,256]{1,0:T(8,128)(2,1)}, u32[]{:S(2)}) copy-start(bf16[256,256]{1,0:T(8,128)(2,1)} %features_hbm.1) | copy-start | bytes 393220
  0.6 8.4 %collective-permute-start.3 = (bf16[256,256]{1,0:T(8,128)(2,1)}, bf16[256,256]{1,0:T(8,128)(2,1)S(1)}, u32[]{:S(2)}, u32[]{:S(2)}) collective-permute-start(bf16[256,256]{1,0:T(8,128)(2,1)} %features_hbm.1), channel_id=1, source_target_pairs={{0,8},{4,12},{8,0},{12,4},{16,24},{20,28},{24,16},{28,20},{1,9},{5... | collective-permute-start | bytes 393224 | tf_op jit(solution)/shard_map/ppermute | solution.py:361
  3.8 13.1 %collective-permute-start.5 = (bf16[256,256]{1,0:T(8,128)(2,1)}, bf16[256,256]{1,0:T(8,128)(2,1)S(1)}, u32[]{:S(2)}, u32[]{:S(2)}) collective-permute-start(bf16[256,256]{1,0:T(8,128)(2,1)} %features_hbm.1), channel_id=1, source_target_pairs={{0,16},{4,20},{8,24},{12,28},{16,0},{20,4},{24,8},{28,12},{1,17},{... | collective-permute-start | bytes 393224 | tf_op jit(solution)/shard_map/ppermute | solution.py:361
  6.3 15.7 %collective-permute-start = (bf16[256,256]{1,0:T(8,128)(2,1)}, bf16[256,256]{1,0:T(8,128)(2,1)S(1)}, u32[]{:S(2)}, u32[]{:S(2)}) collective-permute-start(bf16[256,256]{1,0:T(8,128)(2,1)} %features_hbm.1), channel_id=1, source_target_pairs={{0,24},{4,28},{8,16},{12,20},{16,8},{20,12},{24,0},{28,4},{1,25},{... | collective-permute-start | bytes 393224 | tf_op jit(solution)/shard_map/ppermute | solution.py:361
  6.4 15.8 %collective-permute-start.2 = (bf16[256,256]{1,0:T(8,128)(2,1)}, bf16[256,256]{1,0:T(8,128)(2,1)S(1)}, u32[]{:S(2)}, u32[]{:S(2)}) collective-permute-start(bf16[256,256]{1,0:T(8,128)(2,1)} %features_hbm.1), channel_id=1, source_target_pairs={{0,4},{4,0},{8,12},{12,8},{16,20},{20,16},{24,28},{28,24},{1,5},{5... | collective-permute-start | bytes 393224 | tf_op jit(solution)/shard_map/ppermute | solution.py:361
  9.0 13.1 %collective-permute-start.4 = (bf16[256,256]{1,0:T(8,128)(2,1)S(1)}, bf16[256,256]{1,0:T(8,128)(2,1)S(1)}, u32[]{:S(2)}, u32[]{:S(2)}) collective-permute-start(bf16[256,256]{1,0:T(8,128)(2,1)S(1)} %collective-permute-done.3.refs_2_), channel_id=1, source_target_pairs={{0,4},{4,0},{8,12},{12,8},{16,20},{20,16},{24,28},{28,24},{1,5},{5... | collective-permute-start | bytes 393224 | tf_op jit(solution)/shard_map/ppermute | solution.py:361
  16.9 5.3 %collective-permute-start.6 = (bf16[256,256]{1,0:T(8,128)(2,1)S(1)}, bf16[256,256]{1,0:T(8,128)(2,1)S(1)}, u32[]{:S(2)}, u32[]{:S(2)}) collective-permute-start(bf16[256,256]{1,0:T(8,128)(2,1)S(1)} %collective-permute-done.5.refs_4_), channel_id=1, source_target_pairs={{0,4},{4,0},{8,12},{12,8},{16,20},{20,16},{24,28},{28,24},{1,5},{5... | collective-permute-start | bytes 393224 | tf_op jit(solution)/shard_map/ppermute | solution.py:361
  22.1 5.0 %collective-permute-start.1 = (bf16[256,256]{1,0:T(8,128)(2,1)S(1)}, bf16[256,256]{1,0:T(8,128)(2,1)S(1)}, u32[]{:S(2)}, u32[]{:S(2)}) collective-permute-start(bf16[256,256]{1,0:T(8,128)(2,1)S(1)} %collective-permute-done.refs_6_), channel_id=1, source_target_pairs={{0,4},{4,0},{8,12},{12,8},{16,20},{20,16},{24,28},{28,24},{1,5},{5... | collective-permute-start | bytes 393224 | tf_op jit(solution)/shard_map/ppermute | solution.py:361
  23.9 19.7 %copy-start.1 = (bf16[256,256]{1,0:T(8,128)(2,1)S(1)}, bf16[256,256]{1,0:T(8,128)(2,1)}, u32[]{:S(2)}) copy-start(bf16[256,256]{1,0:T(8,128)(2,1)} %refs_5_.1) | copy-start | bytes 393220
  23.9 19.7 %copy-start.2 = (bf16[256,256]{1,0:T(8,128)(2,1)S(1)}, bf16[256,256]{1,0:T(8,128)(2,1)}, u32[]{:S(2)}) copy-start(bf16[256,256]{1,0:T(8,128)(2,1)} %w_self.1) | copy-start | bytes 393220
  23.9 19.7 %copy-start.3 = (f32[256]{0:T(256)S(1)}, f32[256]{0:T(256)}, u32[]{:S(2)}) copy-start(f32[256]{0:T(256)} %param.14) | copy-start | bytes 3076
  28.0 2.7 %collective-permute-start.7 = (bf16[512,256]{1,0:T(8,128)(2,1)S(1)}, bf16[512,256]{1,0:T(8,128)(2,1)S(1)}, u32[]{:S(2)}, u32[]{:S(2)}) collective-permute-start(bf16[512,256]{1,0:T(8,128)(2,1)S(1)} %get-tuple-element.24), channel_id=1, source_target_pairs={{0,1},{1,0},{2,3},{3,2},{4,5},{5,4},{6,7},{7,6},{8,9},{9,8},{10,11... | collective-permute-start | bytes 786440 | tf_op jit(solution)/shard_map/ppermute | solution.py:361
  29.1 9.4 %collective-permute-start.9 = (bf16[528,256]{1,0:T(8,128)(2,1)S(1)}, bf16[528,256]{1,0:T(8,128)(2,1)S(1)}, u32[]{:S(2)}, u32[]{:S(2)}) collective-permute-start(bf16[528,256]{1,0:T(8,128)(2,1)S(1)} %near.1.refs_2_.refs_0_), channel_id=1, source_target_pairs={{0,2},{1,3},{2,0},{3,1},{4,6},{5,7},{6,4},{7,5},{8,10},{9,11},{10,... | collective-permute-start | bytes 811016 | tf_op jit(solution)/shard_map/ppermute | solution.py:361
  30.7 12.9 %collective-permute-start.8 = (bf16[512,256]{1,0:T(8,128)(2,1)S(1)}, bf16[512,256]{1,0:T(8,128)(2,1)S(1)}, u32[]{:S(2)}, u32[]{:S(2)}) collective-permute-start(bf16[512,256]{1,0:T(8,128)(2,1)S(1)} %add_convert_fusion.refs_0_), channel_id=1, source_target_pairs={{0,2},{1,3},{2,0},{3,1},{4,6},{5,7},{6,4},{7,5},{8,10},{9,11},{10,... | collective-permute-start | bytes 786440 | tf_op jit(solution)/shard_map/ppermute | solution.py:361
  45.8 5.1 %collective-permute-start.17 = (bf16[2,128,256]{2,1,0:T(8,128)(2,1)S(1)}, bf16[2,128,256]{2,1,0:T(8,128)(2,1)S(1)}, u32[]{:S(2)}, u32[]{:S(2)}) collective-permute-start(bf16[2,128,256]{2,1,0:T(8,128)(2,1)S(1)} %get-tuple-element.37.refs_0_), channel_id=1, source_target_pairs={{0,4},{4,0},{8,12},{12,8},{16,20},{20,16},{24,28},{28,24},{1,5},{5... | collective-permute-start | bytes 393224 | tf_op jit(solution)/shard_map/ppermute | solution.py:361
  45.9 9.8 %collective-permute-start.10 = (bf16[512,256]{1,0:T(8,128)(2,1)S(1)}, bf16[512,256]{1,0:T(8,128)(2,1)S(1)}, u32[]{:S(2)}, u32[]{:S(2)}) collective-permute-start(bf16[512,256]{1,0:T(8,128)(2,1)S(1)} %get-tuple-element.30.mine_ref), channel_id=1, source_target_pairs={{0,1},{1,0},{2,3},{3,2},{4,5},{5,4},{6,7},{7,6},{8,9},{9,8},{10,11... | collective-permute-start | bytes 786440 | tf_op jit(solution)/shard_map/ppermute | solution.py:361
  51.0 4.6 %collective-permute-start.18 = (bf16[128,256]{1,0:T(8,128)(2,1)S(1)}, bf16[128,256]{1,0:T(8,128)(2,1)S(1)}, u32[]{:S(2)}, u32[]{:S(2)}) collective-permute-start(bf16[128,256]{1,0:T(8,128)(2,1)S(1)} %fusion.1), channel_id=1, source_target_pairs={{0,1},{1,0},{2,3},{3,2},{4,5},{5,4},{6,7},{7,6},{8,9},{9,8},{10,11... | collective-permute-start | bytes 196616 | tf_op jit(solution)/shard_map/ppermute | solution.py:361
  55.6 5.3 %collective-permute-start.19 = (bf16[128,256]{1,0:T(8,128)(2,1)S(1)}, bf16[128,256]{1,0:T(8,128)(2,1)S(1)}, u32[]{:S(2)}, u32[]{:S(2)}) collective-permute-start(bf16[128,256]{1,0:T(8,128)(2,1)S(1)} %fusion), channel_id=1, source_target_pairs={{0,16},{4,20},{8,24},{12,28},{16,0},{20,4},{24,8},{28,12},{1,17},{... | collective-permute-start | bytes 196616 | tf_op jit(solution)/shard_map/ppermute | solution.py:361
  56.7 6.7 %collective-permute-start.14 = (bf16[256,256]{1,0:T(8,128)(2,1)S(1)}, bf16[256,256]{1,0:T(8,128)(2,1)S(1)}, u32[]{:S(2)}, u32[]{:S(2)}) collective-permute-start(bf16[256,256]{1,0:T(8,128)(2,1)S(1)} %get-tuple-element.39), channel_id=1, source_target_pairs={{0,4},{4,0},{8,12},{12,8},{16,20},{20,16},{24,28},{28,24},{1,5},{5... | collective-permute-start | bytes 393224 | tf_op jit(solution)/shard_map/ppermute | solution.py:361
  58.3 11.7 %collective-permute-start.13 = (bf16[256,256]{1,0:T(8,128)(2,1)S(1)}, bf16[256,256]{1,0:T(8,128)(2,1)S(1)}, u32[]{:S(2)}, u32[]{:S(2)}) collective-permute-start(bf16[256,256]{1,0:T(8,128)(2,1)S(1)} %get-tuple-element.35), channel_id=1, source_target_pairs={{0,4},{4,0},{8,12},{12,8},{16,20},{20,16},{24,28},{28,24},{1,5},{5... | collective-permute-start | bytes 393224 | tf_op jit(solution)/shard_map/ppermute | solution.py:361
  60.9 4.7 %collective-permute-start.20 = (bf16[128,256]{1,0:T(8,128)(2,1)S(1)}, bf16[128,256]{1,0:T(8,128)(2,1)S(1)}, u32[]{:S(2)}, u32[]{:S(2)}) collective-permute-start(bf16[128,256]{1,0:T(8,128)(2,1)S(1)} %add_convert_fusion.6), channel_id=1, source_target_pairs={{0,8},{4,12},{8,0},{12,4},{16,24},{20,28},{24,16},{28,20},{1,9},{5... | collective-permute-start | bytes 196616 | tf_op jit(solution)/shard_map/ppermute | solution.py:361
  63.4 6.6 %collective-permute-start.15 = (bf16[256,256]{1,0:T(8,128)(2,1)S(1)}, bf16[256,256]{1,0:T(8,128)(2,1)S(1)}, u32[]{:S(2)}, u32[]{:S(2)}) collective-permute-start(bf16[256,256]{1,0:T(8,128)(2,1)S(1)} %add_convert_fusion.3), channel_id=1, source_target_pairs={{0,8},{4,12},{8,0},{12,4},{16,24},{20,28},{24,16},{28,20},{1,9},{5... | collective-permute-start | bytes 393224 | tf_op jit(solution)/shard_map/ppermute | solution.py:361
  65.6 4.4 %collective-permute-start.21 = (bf16[128,256]{1,0:T(8,128)(2,1)S(1)}, bf16[128,256]{1,0:T(8,128)(2,1)S(1)}, u32[]{:S(2)}, u32[]{:S(2)}) collective-permute-start(bf16[128,256]{1,0:T(8,128)(2,1)S(1)} %add_convert_fusion.5.refs_0_), channel_id=1, source_target_pairs={{0,2},{1,3},{2,0},{3,1},{4,6},{5,7},{6,4},{7,5},{8,10},{9,11},{10,... | collective-permute-start | bytes 196616 | tf_op jit(solution)/shard_map/ppermute | solution.py:361
  67.8 6.4 %collective-permute-start.11 = (bf16[512,256]{1,0:T(8,128)(2,1)S(1)}, bf16[512,256]{1,0:T(8,128)(2,1)S(1)}, u32[]{:S(2)}, u32[]{:S(2)}) collective-permute-start(bf16[512,256]{1,0:T(8,128)(2,1)S(1)} %get-tuple-element.32), channel_id=1, source_target_pairs={{0,4},{4,0},{8,12},{12,8},{16,20},{20,16},{24,28},{28,24},{1,5},{5... | collective-permute-start | bytes 786440 | tf_op jit(solution)/shard_map/ppermute | solution.py:361
  68.3 6.5 %collective-permute-start.22 = (bf16[128,256]{1,0:T(8,128)(2,1)S(1)}, bf16[128,256]{1,0:T(8,128)(2,1)S(1)}, u32[]{:S(2)}, u32[]{:S(2)}) collective-permute-start(bf16[128,256]{1,0:T(8,128)(2,1)S(1)} %add_convert_fusion.5.refs_0_), channel_id=1, source_target_pairs={{0,1},{1,0},{2,3},{3,2},{4,5},{5,4},{6,7},{7,6},{8,9},{9,8},{10,11... | collective-permute-start | bytes 196616 | tf_op jit(solution)/shard_map/ppermute | solution.py:361
  70.0 4.8 %collective-permute-start.23 = (bf16[128,256]{1,0:T(8,128)(2,1)S(1)}, bf16[128,256]{1,0:T(8,128)(2,1)S(1)}, u32[]{:S(2)}, u32[]{:S(2)}) collective-permute-start(bf16[128,256]{1,0:T(8,128)(2,1)S(1)} %collective-permute-done.21.refs_1_), channel_id=1, source_target_pairs={{0,1},{1,0},{2,3},{3,2},{4,5},{5,4},{6,7},{7,6},{8,9},{9,8},{10,11... | collective-permute-start | bytes 196616 | tf_op jit(solution)/shard_map/ppermute | solution.py:361
  70.1 9.8 %collective-permute-start.16 = (bf16[256,256]{1,0:T(8,128)(2,1)S(1)}, bf16[256,256]{1,0:T(8,128)(2,1)S(1)}, u32[]{:S(2)}, u32[]{:S(2)}) collective-permute-start(bf16[256,256]{1,0:T(8,128)(2,1)S(1)} %add_convert_fusion.2), channel_id=1, source_target_pairs={{0,16},{4,20},{8,24},{12,28},{16,0},{20,4},{24,8},{28,12},{1,17},{... | collective-permute-start | bytes 393224 | tf_op jit(solution)/shard_map/ppermute | solution.py:361
  74.2 6.4 %collective-permute-start.12 = (bf16[256,256]{1,0:T(8,128)(2,1)S(1)}, bf16[256,256]{1,0:T(8,128)(2,1)S(1)}, u32[]{:S(2)}, u32[]{:S(2)}) collective-permute-start(bf16[256,256]{1,0:T(8,128)(2,1)S(1)} %add_convert_fusion.4), channel_id=1, source_target_pairs={{0,8},{4,12},{8,0},{12,4},{16,24},{20,28},{24,16},{28,20},{1,9},{5... | collective-permute-start | bytes 393224 | tf_op jit(solution)/shard_map/ppermute | solution.py:361

commit v4 on v3

--- a/solution.py
+++ b/solution.py
@@ -122,7 +122,7 @@
 def unpack(gather, place, tiles, after, panel, group, rows=0):
     slot_ids, live_count, masks = tiles
     width = masks.shape[2]
-    heights = [panel - 2 * rows, 2 * rows] if rows else [group if gather else panel]
+    heights = [panel - rows, rows] if rows else [group if gather else panel]
     shapes = [jax.ShapeDtypeStruct((h, panel if gather else group), bf16) for h in heights]
     return pl.pallas_call(
         functools.partial(unpack_kernel, group // width, gather, rows // width),
@@ -174,11 +174,11 @@
     )(in_hbm(degrees.reshape(1, rows)), in_hbm(features), in_hbm(cotangents))
 
 
-def forward_kernel(distances, n_col, natural, last, place_ref, adjacency_ref, *refs):
+def forward_kernel(distances, columns, natural, last, place_ref, adjacency_ref, *refs):
     blocks, refs = refs[: len(distances)], refs[len(distances) :]
     rows = blocks[0].shape[0]
     row, col = place_ref[0], place_ref[1]
-    for e in list(range(1, n_col, 2)) + list(range(0, n_col, 2)):
+    for e in columns:
         own = span(jnp.bitwise_xor(col, e), rows)
         total = refs[0][pl.ds(e * rows, rows), :] if last else None
         for d, block in zip(distances, blocks):
@@ -189,37 +189,55 @@
                 term = mm_tn(adjacency_ref[panel, own], block[...])
             total = term if total is None else total + term
         if last:
-            out = refs[1 + e % 2]
-            out[pl.ds((e // 2) * rows, rows), :] = total.astype(out.dtype)
+            refs[1][pl.ds((e // 2) * rows, rows), :] = total.astype(refs[1].dtype)
         else:
             refs[0][pl.ds(e * rows, rows), :] = total
 
 
-def forward(place, adjacency, natural, blocks, total, n_col):
+def forward(place, adjacency, natural, blocks, total, columns):
     distances, arrays = list(blocks), list(blocks.values())
     rows, width = arrays[0].shape
     last = total is not None
-    if last:
-        half = rows * n_col // 2
-        shapes = [jax.ShapeDtypeStruct((half, width), kind) for kind in (f32, bf16)]
-    else:
-        shapes = [jax.ShapeDtypeStruct((rows * n_col, width), f32)]
+    kind = bf16 if last and columns[0] % 2 else f32
+    shape = jax.ShapeDtypeStruct((rows * len(columns), width), kind)
     inputs = arrays + ([total] if last else [])
     return pl.pallas_call(
-        functools.partial(forward_kernel, distances, n_col, natural, last),
-        out_shape=shapes,
+        functools.partial(forward_kernel, distances, columns, natural, last),
+        out_shape=shape,
         in_specs=[SMEM] + [VMEM] * (1 + len(inputs)),
-        out_specs=[VMEM] * len(shapes),
-        compiler_params=params(adjacency, *inputs, *shapes),
+        out_specs=VMEM,
+        compiler_params=params(adjacency, *inputs, shape),
         cost_estimate=cost(250 * len(distances)),
-        name="forward_last" if last else "forward",
+        name=("forward_other" if kind == bf16 else "forward_mine") if last else "forward",
     )(place, adjacency, *inputs)
+
+
+def own_kernel(n_part, *refs):
+    nears, (w_self, bias, own_ref) = refs[:n_part], refs[n_part:]
+    rows = own_ref.shape[0] // n_part
+    for h in range(n_part):
+        product = mm(nears[h][pl.ds(0, rows), :], w_self[...])
+        own_ref[pl.ds(h * rows, rows), :] = product + bias[...]
+
+
+def own(nears, w_self, bias, rows):
+    n_part, width = len(nears), bias.shape[1]
+    shape = jax.ShapeDtypeStruct((rows * n_part, width), f32)
+    return pl.pallas_call(
+        functools.partial(own_kernel, n_part),
+        out_shape=shape,
+        in_specs=[VMEM] * (n_part + 2),
+        out_specs=VMEM,
+        compiler_params=params(*nears, w_self, shape),
+        cost_estimate=cost(500),
+        name="own",
+    )(*nears, w_self, bias)
 
 
 def node_kernel(n_part, *refs):
     sums, refs = refs[:n_part], refs[n_part:]
     nears, refs = refs[:n_part], refs[n_part:]
-    w_self, w_neigh, bias, out_ref, mean_ref, grad_ref, up_ref = refs
+    own_ref, w_neigh, out_ref, mean_ref, grad_ref, up_ref = refs
     rows = out_ref.shape[0]
     for h in range(n_part):
         parts = [sums[h2][pl.ds((h ^ h2) * rows, rows), :].astype(f32) for h2 in range(n_part)]
@@ -231,19 +249,19 @@
         degree = jnp.sum((digits * scales).T, axis=1, keepdims=True)
         inverse = 1.0 / degree
         mean = (parts[0] * inverse).astype(bf16)
-        preact = mm(nears[h][pl.ds(0, rows), :], w_self[...]) + mm(mean, w_neigh[...]) + bias[...]
+        here = pl.ds(h * rows, rows)
+        preact = own_ref[here, :] + mm(mean, w_neigh[...])
         gate = jax.nn.sigmoid(preact)
         if h == 0:
             out_ref[...] = (preact * gate).astype(bf16)
         grad = nears[h][pl.ds(rows, rows), :].astype(f32) * gate * (1.0 + preact * (1.0 - gate))
         grad = grad.astype(bf16)
-        here = pl.ds(h * rows, rows)
         mean_ref[here, :] = mean
         grad_ref[here, :] = grad
         up_ref[here, :] = (mm_nt(grad, w_neigh[...]) * inverse).astype(bf16)
 
 
-def node(sums, nears, w_self, w_neigh, bias):
+def node(sums, nears, start, w_neigh):
     n_part = len(sums)
     width = nears[0].shape[1]
     rows = sums[0].shape[0] // n_part
@@ -252,26 +270,28 @@
     return pl.pallas_call(
         functools.partial(node_kernel, n_part),
         out_shape=shapes,
-        in_specs=[VMEM] * (2 * n_part + 3),
+        in_specs=[VMEM] * (2 * n_part + 2),
         out_specs=[VMEM] * 4,
-        compiler_params=params(*sums, *nears, w_self, w_neigh, *shapes),
+        compiler_params=params(*sums, *nears, start, w_neigh, *shapes),
         cost_estimate=cost(2000),
         name="node",
-    )(*sums, *nears, w_self, w_neigh, bias)
+    )(*sums, *nears, start, w_neigh)
 
 
 def weight_kernel(n_part, place_ref, mean_ref, grad_ref, w_self, *refs):
-    nears, (slice_ref, base_ref, total_ref) = refs[:n_part], refs[n_part:]
+    nears, (keep_ref, send_ref, base_ref, total_ref) = refs[:n_part], refs[n_part:]
     rows = base_ref.shape[0]
     here = pl.ds(0, rows)
     grad_self = mm_tn(nears[0][here, :], grad_ref[here, :])
     for h in range(1, n_part):
         grad_self = grad_self + mm_tn(nears[h][here, :], grad_ref[pl.ds(h * rows, rows), :])
     grad_neigh = mm_tn(mean_ref[...], grad_ref[...])
-    total_ref[0], total_ref[1] = grad_self, grad_neigh
-    here = span(lax.div(place_ref[1], 2), slice_ref.shape[1])
-    slice_ref[0] = total_ref[0, here, :].astype(bf16)
-    slice_ref[1] = total_ref[1, here, :].astype(bf16)
+    first = lax.rem(place_ref[1], 2) == 0
+    total_ref[0] = jnp.where(first, grad_self, grad_neigh)
+    total_ref[1] = jnp.where(first, grad_neigh, grad_self)
+    here = span(lax.div(place_ref[1], 2), keep_ref.shape[0])
+    keep_ref[...] = total_ref[0, here, :]
+    send_ref[...] = total_ref[1, here, :].astype(bf16)
     base_ref[...] = mm_nt(grad_ref[pl.ds(0, rows), :], w_self[...])
 
 
@@ -281,11 +301,12 @@
     return pl.pallas_call(
         functools.partial(weight_kernel, n_part),
         out_shape=[
-            jax.ShapeDtypeStruct((2, width // n_part, width), bf16),
+            jax.ShapeDtypeStruct((width // n_part, width), f32),
+            jax.ShapeDtypeStruct((width // n_part, width), bf16),
             jax.ShapeDtypeStruct((rows, width), f32),
         ],
         in_specs=[SMEM] + [VMEM] * (3 + n_part),
-        out_specs=[VMEM] * 2,
+        out_specs=[VMEM] * 3,
         scratch_shapes=[pltpu.VMEM((2, width, width), f32)],
         compiler_params=params(mean, grad, w_self, *nears),
         cost_estimate=cost(1300),
@@ -384,29 +405,32 @@
     (dense,) = unpack(both, place, tiles, [], panel, group)
     late = far[-1] ^ 1
     early = {d: blocks[d] for d in range(n_row) if d != late}
-    (total,) = forward(place, dense, both, early, None, n_col)
-    mine, other = forward(place, dense, both, {late: blocks[late]}, total, n_col)
+    columns = list(range(n_col))
+    total = forward(place, dense, both, early, None, columns)
+    other = forward(place, dense, both, {late: blocks[late]}, total, columns[1::2])
     other = exchange(other, "col", 1)
+    mine = forward(place, dense, both, {late: blocks[late]}, total, columns[::2])
     pair = (mine + other.astype(f32)).astype(bf16)
     sums = [pair] + [exchange(pair, "col", 2 * h) for h in range(1, n_part)]
 
-    layer_out, mean, grad, up = node(sums, nears, w_self, w_neigh, bias.reshape(1, width))
+    start = own(nears, w_self, bias.reshape(1, width), rows)
+    layer_out, mean, grad, up = node(sums, nears, start, w_neigh)
     up_other = exchange(up, "col", 1)
-    slices, base = weight(place, mean, grad, w_self, nears)
+    keep, send, base = weight(place, mean, grad, w_self, nears)
     top = n_row // 2
     apart = [d for d in reversed(sorted(far)) if d >= top]
     joined = tuple(d ^ 1 for d in [0] + sorted(far) if d < top)
-    first = [(apart[0] ^ 1,), (apart[0],)]
-    rest = [(d ^ e,) for d in apart[1:] for e in (1, 0)]
+    first = [(apart[0] ^ 1,)]
+    rest = [(d ^ e,) for d in apart[1:] for e in (1, 0)] + [(apart[0],)]
     rest += [joined] + [(d ^ 1,) for d in joined]
     if both:
         near_part, far_part = unpack(False, place, tiles, [pair], panel, group, rows)
-        near_places = {d: d for d in range(n_row - 2)}
-        far_places = {n_row - 2: 0, n_row - 1: 1}
-        backs = backward(place, far_part, far_places, up, up_other, [slices], first, n_part)
+        near_places = {d: d for d in range(n_row - 1)}
+        far_places = {n_row - 1: 0}
+        backs = backward(place, far_part, far_places, up, up_other, [send], first, n_part)
         backs.update(backward(place, near_part, near_places, up, up_other, [], rest, n_part))
     else:
-        backs = backward(place, dense, None, up, up_other, [slices], first + rest, n_part)
+        backs = backward(place, dense, None, up, up_other, [send], first + rest, n_part)
 
     pairs = {}
     for d in apart:
@@ -426,18 +450,11 @@
             total = total + exchange(pairs[d].astype(bf16), "row", d).astype(f32)
     grad_in = total.astype(bf16)
 
-    came = exchange(slices, "row", 1)
-    sums = slices.astype(f32) + came.astype(f32)
-    core = lax.rem(col, 2) == 0
-    keep = jnp.where(core, sums[0], sums[1])
-    send = jnp.where(core, sums[1], sums[0]).astype(bf16)
-    grads = keep + exchange(send, "col", 1).astype(f32)
-    rounded = grads.astype(bf16)
-    distance = n_row // 2
-    while distance > 1:
+    came = exchange(send, "col", 1)
+    rounded = (keep + came.astype(f32)).astype(bf16)
+    for distance in [1] + [n_row >> bit for bit in range(1, n_row.bit_length() - 1)]:
         came = exchange(rounded, "row", distance)
         rounded = (rounded.astype(f32) + came.astype(f32)).astype(bf16)
-        distance //= 2
     grads = rounded
     mine = [grads] + [exchange(grads, "col", 2 * h) for h in range(1, n_part)]
     others = [exchange(value, "col", 1) for value in mine]

time: 81.4 us -> 82 us (level)
  starting transfers between devices: 25.1 us -> 22 us
  waiting for transfers between devices: 35.6 us -> 38.5 us
  Pallas kernels: 17.8 us -> 18.7 us
    ppermute x24, starting transfers between devices: 25.1 us -> 22 us  [exchange(): return lax.ppermute(value, axis, [(i, i ^ distance) for i in range(size)])]
    ppermute x24, waiting for transfers between devices: 35.6 us -> 38.5 us  [exchange(): return lax.ppermute(value, axis, [(i, i ^ distance) for i in range(size)])]
    pallas_call x2 -> x4, Pallas kernels: 2.51 us -> 3.43 us  [the longest x3 3.2 us: forward(): pl.pallas_call(functools.partial(forward_kernel, distances, columns, natu...]
  transfers between devices with their start and end apart: 24 -> 24, of which waited for: 12 -> 13; matrix products, arithmetic and copies ran while one was open for 0% -> 0% of each run, Pallas kernels for 18% -> 19%
where the time goes in v4:
time: 82 us; the launch traced here: 81.8 us
  waiting for transfers between devices  38.5 us (47%)
  starting transfers between devices  22 us (27%)
  Pallas kernels  18.7 us (23%)
  between operations  1.53 us (2%)
  other arithmetic  1.06 us (1%)
    ppermute x24, waiting for transfers between devices, exchange(): return lax.ppermute(value, axis, [(i, i ^ distance) for i in range(size)])  38.5 us
    ppermute x24, starting transfers between devices, exchange(): return lax.ppermute(value, axis, [(i, i ^ distance) for i in range(size)])  22 us
    pallas_call x2, Pallas kernels, unpack(): pl.pallas_call(functools.partial(unpack_kernel, group // width, gather, r...  8.23 us
    pallas_call x3, Pallas kernels, forward(): pl.pallas_call(functools.partial(forward_kernel, distances, columns, natu...  3.2 us
    pallas_call x2, Pallas kernels, backward(): pl.pallas_call(functools.partial(backward_kernel, groups, place_of, n_par...  2.6 us
  transfers between devices with their start and end apart: 24, of which 13 were waited for; matrix products, arithmetic and copies ran while one was open for 0% of the time, Pallas kernels for 19%

profile of v4, /device:TPU:0, one launch (start us, length us, event | category | flops | bytes accessed | tf_op | source)
XLA Modules:
  0.0 81.8 jit_solution(4772581540300292501)
XLA Ops:
  0.6 0.0 copy-start
  0.6 3.1 %collective-permute-start.3 = (bf16[256,256]{1,0:T(8,128)(2,1)}, bf16[256,256]{1,0:T(8,128)(2,1)S(1)}, u32[]{:S(2)}, u32[]{:S(2)}) collective-permute-start(bf16[256,256]{1,0:T(8,128)(2,1)} %features_hbm.1), channel_id=1, source_target_pairs={{0,8},{4,12},{8,0},{12,4},{16,24},{20,28},{24,16},{28,20},{1,9},{5... | collective-permute-start | bytes 393224 | tf_op jit(solution)/shard_map/ppermute | solution.py:382
  3.8 2.6 %collective-permute-start.5 = (bf16[256,256]{1,0:T(8,128)(2,1)}, bf16[256,256]{1,0:T(8,128)(2,1)S(1)}, u32[]{:S(2)}, u32[]{:S(2)}) collective-permute-start(bf16[256,256]{1,0:T(8,128)(2,1)} %features_hbm.1), channel_id=1, source_target_pairs={{0,16},{4,20},{8,24},{12,28},{16,0},{20,4},{24,8},{28,12},{1,17},{... | collective-permute-start | bytes 393224 | tf_op jit(solution)/shard_map/ppermute | solution.py:382
  6.3 0.0 collective-permute-start
  6.4 1.7 %collective-permute-start.2 = (bf16[256,256]{1,0:T(8,128)(2,1)}, bf16[256,256]{1,0:T(8,128)(2,1)S(1)}, u32[]{:S(2)}, u32[]{:S(2)}) collective-permute-start(bf16[256,256]{1,0:T(8,128)(2,1)} %features_hbm.1), channel_id=1, source_target_pairs={{0,4},{4,0},{8,12},{12,8},{16,20},{20,16},{24,28},{28,24},{1,5},{5... | collective-permute-start | bytes 393224 | tf_op jit(solution)/shard_map/ppermute | solution.py:382
  8.7 0.1 pad_add_fusion.place_ref
  8.8 0.3 collective-permute-done.3.refs_2_
  9.0 1.7 %collective-permute-start.4 = (bf16[256,256]{1,0:T(8,128)(2,1)S(1)}, bf16[256,256]{1,0:T(8,128)(2,1)S(1)}, u32[]{:S(2)}, u32[]{:S(2)}) collective-permute-start(bf16[256,256]{1,0:T(8,128)(2,1)S(1)} %collective-permute-done.3.refs_2_), channel_id=1, source_target_pairs={{0,4},{4,0},{8,12},{12,8},{16,20},{20,16},{24,28},{28,24},{1,5},{5... | collective-permute-start | bytes 393224 | tf_op jit(solution)/shard_map/ppermute | solution.py:382
  10.8 6.1 %collective-permute-done.5.refs_4_ = bf16[256,256]{1,0:T(8,128)(2,1)S(1)} collective-permute-done((bf16[256,256]{1,0:T(8,128)(2,1)}, bf16[256,256]{1,0:T(8,128)(2,1)S(1)}, u32[]{:S(2)}, u32[]{:S(2)}) %collective-permute-start.5) | collective-permute-done | bytes 131104 | tf_op jit(solution)/shard_map/ppermute | solution.py:382
  16.9 1.5 %collective-permute-start.6 = (bf16[256,256]{1,0:T(8,128)(2,1)S(1)}, bf16[256,256]{1,0:T(8,128)(2,1)S(1)}, u32[]{:S(2)}, u32[]{:S(2)}) collective-permute-start(bf16[256,256]{1,0:T(8,128)(2,1)S(1)} %collective-permute-done.5.refs_4_), channel_id=1, source_target_pairs={{0,4},{4,0},{8,12},{12,8},{16,20},{20,16},{24,28},{28,24},{1,5},{5... | collective-permute-start | bytes 393224 | tf_op jit(solution)/shard_map/ppermute | solution.py:382
  18.3 3.7 %unpack_gather.1.adjacency_ref = bf16[1024,2048]{1,0:T(8,128)(2,1)S(1)} custom-call(s32[2]{0:T(128)S(1)} %pad_add_fusion.place_ref, s32[1]{0:T(128)} %bitcast.7.count_ref, s32[1,88]{1,0:T(1,128)} %bitcast.13, s32[88,16,128]{2,1,0:T(8,128)} %bitcast.10), custom_call_target="tpu_custom_call" | custom-call | flops 2000000000 | tf_op jit(solution)/shard_map/unpack_gather/pallas_call | solution.py:127
  22.1 0.0 collective-permute-done.refs_6_
  22.1 0.1 collective-permute-start.1
  22.2 0.0 collective-permute-done.2.refs_1_
  22.2 0.0 collective-permute-done.4.refs_3_
  22.2 0.0 collective-permute-done.6.refs_5_
  22.2 1.7 %forward.1.refs_1_ = f32[1024,256]{1,0:T(8,128)S(1)} custom-call(s32[2]{0:T(128)S(1)} %pad_add_fusion.place_ref, bf16[1024,2048]{1,0:T(8,128)(2,1)S(1)} %unpack_gather.1.adjacency_ref, bf16[256,256]{1,0:T(8,128)(2,1)S(1)} %copy-done, bf16[256,256]{1,0:T(8,128)(2,1)S(1)} %collective-permute-done.2.refs_1_, ...), custom_call_target="tpu_custom_call" | custom-call | flops 1750000000 | tf_op jit(solution)/shard_map/forward/pallas_call | solution.py:204
  23.9 3.2 %collective-permute-done.1.refs_0_ = bf16[256,256]{1,0:T(8,128)(2,1)S(1)} collective-permute-done((bf16[256,256]{1,0:T(8,128)(2,1)S(1)}, bf16[256,256]{1,0:T(8,128)(2,1)S(1)}, u32[]{:S(2)}, u32[]{:S(2)}) %collective-permute-start.1) | collective-permute-done | bytes 131104 | tf_op jit(solution)/shard_map/ppermute | solution.py:382
  27.1 0.8 forward_other.1
  27.9 0.1 collective-permute-start.7
  28.0 0.0 copy-start.2
  28.0 0.0 copy-start.3
  28.0 1.0 %near.1.refs_0_.refs_2_ = bf16[528,256]{1,0:T(8,128)(2,1)S(1)} custom-call(s32[1,256]{1,0:T(1,128)} %bitcast.12, bf16[256,256]{1,0:T(8,128)(2,1)} %features_hbm.1, bf16[256,256]{1,0:T(8,128)(2,1)} %cotangents_hbm.1), custom_call_target="tpu_custom_call" | custom-call | flops 500000000 | tf_op jit(solution)/shard_map/near/pallas_call | solution.py:165
  29.1 0.0 copy-start.1
  29.1 1.6 %collective-permute-start.9 = (bf16[528,256]{1,0:T(8,128)(2,1)S(1)}, bf16[528,256]{1,0:T(8,128)(2,1)S(1)}, u32[]{:S(2)}, u32[]{:S(2)}) collective-permute-start(bf16[528,256]{1,0:T(8,128)(2,1)S(1)} %near.1.refs_0_.refs_2_), channel_id=1, source_target_pairs={{0,2},{1,3},{2,0},{3,1},{4,6},{5,7},{6,4},{7,5},{8,10},{9,11},{10,... | collective-permute-start | bytes 811016 | tf_op jit(solution)/shard_map/ppermute | solution.py:382
  30.7 0.8 forward_mine.1
  31.4 0.1 add_convert_fusion.refs_0_
  31.5 0.6 collective-permute-start.8
  32.1 6.4 %collective-permute-done.9.refs_1_.refs_3_ = bf16[528,256]{1,0:T(8,128)(2,1)S(1)} collective-permute-done((bf16[528,256]{1,0:T(8,128)(2,1)S(1)}, bf16[528,256]{1,0:T(8,128)(2,1)S(1)}, u32[]{:S(2)}, u32[]{:S(2)}) %collective-permute-start.9) | collective-permute-done | bytes 270368 | tf_op jit(solution)/shard_map/ppermute | solution.py:382
  38.5 0.2 own.1.refs_4_
  38.7 4.9 %collective-permute-done.8.refs_1_ = bf16[512,256]{1,0:T(8,128)(2,1)S(1)} collective-permute-done((bf16[512,256]{1,0:T(8,128)(2,1)S(1)}, bf16[512,256]{1,0:T(8,128)(2,1)S(1)}, u32[]{:S(2)}, u32[]{:S(2)}) %collective-permute-start.8) | collective-permute-done | bytes 262176 | tf_op jit(solution)/shard_map/ppermute | solution.py:382
  43.6 1.1 %node.1 = (bf16[256,256]{1,0:T(8,128)(2,1)}, bf16[512,256]{1,0:T(8,128)(2,1)S(1)}, bf16[512,256]{1,0:T(8,128)(2,1)S(1)}, bf16[512,256]{1,0:T(8,128)(2,1)S(1)}) custom-call(bf16[512,256]{1,0:T(8,128)(2,1)S(1)} %add_convert_fusion.refs_0_, bf16[512,256]{1,0:T(8,128)(2,1)S(1)} %collective-permute-done.8.refs_1_, bf16[528,256]{1,0:T(8,128)(2,1)S(1)} %near.1.refs_0_.refs_2_, ...), custom_call_target="tpu_custom_call" | custom-call | flops 2000000000 | tf_op jit(solution)/shard_map/node/pallas_call | solution.py:270
  44.7 0.9 %weight.1 = (f32[128,256]{1,0:T(8,128)S(1)}, bf16[128,256]{1,0:T(8,128)(2,1)S(1)}, f32[256,256]{1,0:T(8,128)S(1)}) custom-call(s32[2]{0:T(128)S(1)} %pad_add_fusion.place_ref, bf16[512,256]{1,0:T(8,128)(2,1)S(1)} %get-tuple-element.22.mean_ref, bf16[512,256]{1,0:T(8,128)(2,1)S(1)} %get-tuple-element.23.grad_ref, bf16[256,256]{1,0:T(8,128)(2,1)S(1)} %copy-done.2, ...), custom_call_target="tpu_custom_call" | custom-call | flops 1300000000 | tf_op jit(solution)/shard_map/weight/pallas_call | solution.py:301
  45.6 0.1 collective-permute-start.17
  45.7 1.2 %collective-permute-done.17 = bf16[128,256]{1,0:T(8,128)(2,1)S(1)} collective-permute-done((bf16[128,256]{1,0:T(8,128)(2,1)S(1)}, bf16[128,256]{1,0:T(8,128)(2,1)S(1)}, u32[]{:S(2)}, u32[]{:S(2)}) %collective-permute-start.17) | collective-permute-done | bytes 65568 | tf_op jit(solution)/shard_map/ppermute | solution.py:382
  46.9 0.1 collective-permute-start.18
  47.0 0.2 collective-permute-start.10
  47.2 4.0 %collective-permute-done.18 = bf16[128,256]{1,0:T(8,128)(2,1)S(1)} collective-permute-done((bf16[128,256]{1,0:T(8,128)(2,1)S(1)}, bf16[128,256]{1,0:T(8,128)(2,1)S(1)}, u32[]{:S(2)}, u32[]{:S(2)}) %collective-permute-start.18) | collective-permute-done | bytes 65568 | tf_op jit(solution)/shard_map/ppermute | solution.py:382
  51.3 0.1 collective-permute-start.19
  51.4 4.5 %unpack_spread.1 = (bf16[1792,1024]{1,0:T(8,128)(2,1)S(1)}, bf16[256,1024]{1,0:T(8,128)(2,1)S(1)}) custom-call(s32[2]{0:T(128)S(1)} %pad_add_fusion.place_ref, s32[1]{0:T(128)} %bitcast.8.count_ref, s32[1,88]{1,0:T(1,128)} %bitcast.14, s32[88,16,128]{2,1,0:T(8,128)} %bitcast.11, bf16[512,256]{1,0:T(8,128)(2,1)S(1)} %add_convert_fusion.refs_0_), custom_call_target="tpu_custom_call" | custom-call | flops 2000000000 | tf_op jit(solution)/shard_map/unpack_spread/pallas_call | solution.py:127
  55.9 0.7 collective-permute-done.19
  56.6 0.8 collective-permute-start.20
  57.4 0.9 %backward_far.1 = bf16[256,256]{1,0:T(8,128)(2,1)S(1)} custom-call(s32[2]{0:T(128)S(1)} %pad_add_fusion.place_ref, bf16[256,1024]{1,0:T(8,128)(2,1)S(1)} %get-tuple-element.33.adjacency_ref, bf16[512,256]{1,0:T(8,128)(2,1)S(1)} %get-tuple-element.26.mine_ref, bf16[512,256]{1,0:T(8,128)(2,1)S(1)} %collective-permute-done.10.other_ref, ...), custom_call_target="tpu_custom_call" | custom-call | flops 200000000 | tf_op jit(solution)/shard_map/backward_far/pallas_call | solution.py:342
  58.3 0.1 collective-permute-start.14
  58.4 1.7 %backward.1 = (bf16[256,256]{1,0:T(8,128)(2,1)S(1)}, bf16[256,256]{1,0:T(8,128)(2,1)S(1)}, bf16[256,256]{1,0:T(8,128)(2,1)S(1)}, bf16[512,256]{1,0:T(8,128)(2,1)...) custom-call(s32[2]{0:T(128)S(1)} %pad_add_fusion.place_ref, ...), custom_call_target="tpu_custom_call" | custom-call | flops 1400000000 | tf_op jit(solution)/shard_map/backward/pallas_call | solution.py:342
  60.1 2.1 %collective-permute-start.13 = (bf16[256,256]{1,0:T(8,128)(2,1)S(1)}, bf16[256,256]{1,0:T(8,128)(2,1)S(1)}, u32[]{:S(2)}, u32[]{:S(2)}) collective-permute-start(bf16[256,256]{1,0:T(8,128)(2,1)S(1)} %get-tuple-element.31), channel_id=1, source_target_pairs={{0,4},{4,0},{8,12},{12,8},{16,20},{20,16},{24,28},{28,24},{1,5},{5... | collective-permute-start | bytes 393224 | tf_op jit(solution)/shard_map/ppermute | solution.py:382
  62.2 1.9 %collective-permute-done.14 = bf16[256,256]{1,0:T(8,128)(2,1)S(1)} collective-permute-done((bf16[256,256]{1,0:T(8,128)(2,1)S(1)}, bf16[256,256]{1,0:T(8,128)(2,1)S(1)}, u32[]{:S(2)}, u32[]{:S(2)}) %collective-permute-start.14) | collective-permute-done | bytes 131104 | tf_op jit(solution)/shard_map/ppermute | solution.py:382
  64.1 0.9 %collective-permute-start.15 = (bf16[256,256]{1,0:T(8,128)(2,1)S(1)}, bf16[256,256]{1,0:T(8,128)(2,1)S(1)}, u32[]{:S(2)}, u32[]{:S(2)}) collective-permute-start(bf16[256,256]{1,0:T(8,128)(2,1)S(1)} %add_convert_fusion.3), channel_id=1, source_target_pairs={{0,8},{4,12},{8,0},{12,4},{16,24},{20,28},{24,16},{28,20},{1,9},{5... | collective-permute-start | bytes 393224 | tf_op jit(solution)/shard_map/ppermute | solution.py:382
  64.9 0.0 collective-permute-done.20
  64.9 2.7 %collective-permute-start.21 = (bf16[128,256]{1,0:T(8,128)(2,1)S(1)}, bf16[128,256]{1,0:T(8,128)(2,1)S(1)}, u32[]{:S(2)}, u32[]{:S(2)}) collective-permute-start(bf16[128,256]{1,0:T(8,128)(2,1)S(1)} %add_convert_fusion.5.refs_0_), channel_id=1, source_target_pairs={{0,2},{1,3},{2,0},{3,1},{4,6},{5,7},{6,4},{7,5},{8,10},{9,11},{10,... | collective-permute-start | bytes 196616 | tf_op jit(solution)/shard_map/ppermute | solution.py:382
  67.7 0.7 collective-permute-start.11
  68.3 0.0 collective-permute-start.22
  68.3 1.6 %collective-permute-done.21.refs_1_ = bf16[128,256]{1,0:T(8,128)(2,1)S(1)} collective-permute-done((bf16[128,256]{1,0:T(8,128)(2,1)S(1)}, bf16[128,256]{1,0:T(8,128)(2,1)S(1)}, u32[]{:S(2)}, u32[]{:S(2)}) %collective-permute-start.21) | collective-permute-done | bytes 65568 | tf_op jit(solution)/shard_map/ppermute | solution.py:382
  69.9 0.0 collective-permute-start.23
  69.9 0.0 collective-permute-done.13
  69.9 0.0 collective-permute-done.15
  69.9 0.1 add_convert_fusion.2
  70.0 1.1 %collective-permute-start.16 = (bf16[256,256]{1,0:T(8,128)(2,1)S(1)}, bf16[256,256]{1,0:T(8,128)(2,1)S(1)}, u32[]{:S(2)}, u32[]{:S(2)}) collective-permute-start(bf16[256,256]{1,0:T(8,128)(2,1)S(1)} %add_convert_fusion.2), channel_id=1, source_target_pairs={{0,16},{4,20},{8,24},{12,28},{16,0},{20,4},{24,8},{28,12},{1,17},{... | collective-permute-start | bytes 393224 | tf_op jit(solution)/shard_map/ppermute | solution.py:382
  71.1 2.9 %collective-permute-done.11 = bf16[512,256]{1,0:T(8,128)(2,1)S(1)} collective-permute-done((bf16[512,256]{1,0:T(8,128)(2,1)S(1)}, bf16[512,256]{1,0:T(8,128)(2,1)S(1)}, u32[]{:S(2)}, u32[]{:S(2)}) %collective-permute-start.11) | collective-permute-done | bytes 262176 | tf_op jit(solution)/shard_map/ppermute | solution.py:382
  74.1 0.3 collective-permute-start.12
  74.4 1.4 %join.1 = (f32[256,256]{1,0:T(8,128)}, f32[256,256]{1,0:T(8,128)}) custom-call(s32[2]{0:T(128)S(1)} %pad_add_fusion.place_ref, bf16[128,256]{1,0:T(8,128)(2,1)S(1)} %add_convert_fusion.5.refs_0_, bf16[128,256]{1,0:T(8,128)(2,1)S(1)} %collective-permute-done.21.refs_1_, bf16[128,256]{1,0:T(8,128)(2,1)S(1)} %collective-permute-done.22.refs_2_, ...), custom_call_target="tpu_custom_call" | custom-call | flops 800000000 | tf_op jit(solution)/shard_map/join/pallas_call | solution.py:369
  75.8 4.0 %collective-permute-done.16 = bf16[256,256]{1,0:T(8,128)(2,1)S(1)} collective-permute-done((bf16[256,256]{1,0:T(8,128)(2,1)S(1)}, bf16[256,256]{1,0:T(8,128)(2,1)S(1)}, u32[]{:S(2)}, u32[]{:S(2)}) %collective-permute-start.16) | collective-permute-done | bytes 131104 | tf_op jit(solution)/shard_map/ppermute | solution.py:382
  79.8 1.3 %collective-permute-done.12 = bf16[256,256]{1,0:T(8,128)(2,1)S(1)} collective-permute-done((bf16[256,256]{1,0:T(8,128)(2,1)S(1)}, bf16[256,256]{1,0:T(8,128)(2,1)S(1)}, u32[]{:S(2)}, u32[]{:S(2)}) %collective-permute-start.12) | collective-permute-done | bytes 131104 | tf_op jit(solution)/shard_map/ppermute | solution.py:382
  81.1 0.7 add_convert_fusion.1
  (14 shorter events, 0.2 us)
Async XLA Ops:
  0.6 21.6 %copy-start = (bf16[256,256]{1,0:T(8,128)(2,1)S(1)}, bf16[256,256]{1,0:T(8,128)(2,1)}, u32[]{:S(2)}) copy-start(bf16[256,256]{1,0:T(8,128)(2,1)} %features_hbm.1) | copy-start | bytes 393220
  0.6 8.4 %collective-permute-start.3 = (bf16[256,256]{1,0:T(8,128)(2,1)}, bf16[256,256]{1,0:T(8,128)(2,1)S(1)}, u32[]{:S(2)}, u32[]{:S(2)}) collective-permute-start(bf16[256,256]{1,0:T(8,128)(2,1)} %features_hbm.1), channel_id=1, source_target_pairs={{0,8},{4,12},{8,0},{12,4},{16,24},{20,28},{24,16},{28,20},{1,9},{5... | collective-permute-start | bytes 393224 | tf_op jit(solution)/shard_map/ppermute | solution.py:382
  3.8 13.1 %collective-permute-start.5 = (bf16[256,256]{1,0:T(8,128)(2,1)}, bf16[256,256]{1,0:T(8,128)(2,1)S(1)}, u32[]{:S(2)}, u32[]{:S(2)}) collective-permute-start(bf16[256,256]{1,0:T(8,128)(2,1)} %features_hbm.1), channel_id=1, source_target_pairs={{0,16},{4,20},{8,24},{12,28},{16,0},{20,4},{24,8},{28,12},{1,17},{... | collective-permute-start | bytes 393224 | tf_op jit(solution)/shard_map/ppermute | solution.py:382
  6.3 15.7 %collective-permute-start = (bf16[256,256]{1,0:T(8,128)(2,1)}, bf16[256,256]{1,0:T(8,128)(2,1)S(1)}, u32[]{:S(2)}, u32[]{:S(2)}) collective-permute-start(bf16[256,256]{1,0:T(8,128)(2,1)} %features_hbm.1), channel_id=1, source_target_pairs={{0,24},{4,28},{8,16},{12,20},{16,8},{20,12},{24,0},{28,4},{1,25},{... | collective-permute-start | bytes 393224 | tf_op jit(solution)/shard_map/ppermute | solution.py:382
  6.4 15.8 %collective-permute-start.2 = (bf16[256,256]{1,0:T(8,128)(2,1)}, bf16[256,256]{1,0:T(8,128)(2,1)S(1)}, u32[]{:S(2)}, u32[]{:S(2)}) collective-permute-start(bf16[256,256]{1,0:T(8,128)(2,1)} %features_hbm.1), channel_id=1, source_target_pairs={{0,4},{4,0},{8,12},{12,8},{16,20},{20,16},{24,28},{28,24},{1,5},{5... | collective-permute-start | bytes 393224 | tf_op jit(solution)/shard_map/ppermute | solution.py:382
  9.0 13.1 %collective-permute-start.4 = (bf16[256,256]{1,0:T(8,128)(2,1)S(1)}, bf16[256,256]{1,0:T(8,128)(2,1)S(1)}, u32[]{:S(2)}, u32[]{:S(2)}) collective-permute-start(bf16[256,256]{1,0:T(8,128)(2,1)S(1)} %collective-permute-done.3.refs_2_), channel_id=1, source_target_pairs={{0,4},{4,0},{8,12},{12,8},{16,20},{20,16},{24,28},{28,24},{1,5},{5... | collective-permute-start | bytes 393224 | tf_op jit(solution)/shard_map/ppermute | solution.py:382
  16.9 5.3 %collective-permute-start.6 = (bf16[256,256]{1,0:T(8,128)(2,1)S(1)}, bf16[256,256]{1,0:T(8,128)(2,1)S(1)}, u32[]{:S(2)}, u32[]{:S(2)}) collective-permute-start(bf16[256,256]{1,0:T(8,128)(2,1)S(1)} %collective-permute-done.5.refs_4_), channel_id=1, source_target_pairs={{0,4},{4,0},{8,12},{12,8},{16,20},{20,16},{24,28},{28,24},{1,5},{5... | collective-permute-start | bytes 393224 | tf_op jit(solution)/shard_map/ppermute | solution.py:382
  22.1 5.0 %collective-permute-start.1 = (bf16[256,256]{1,0:T(8,128)(2,1)S(1)}, bf16[256,256]{1,0:T(8,128)(2,1)S(1)}, u32[]{:S(2)}, u32[]{:S(2)}) collective-permute-start(bf16[256,256]{1,0:T(8,128)(2,1)S(1)} %collective-permute-done.refs_6_), channel_id=1, source_target_pairs={{0,4},{4,0},{8,12},{12,8},{16,20},{20,16},{24,28},{28,24},{1,5},{5... | collective-permute-start | bytes 393224 | tf_op jit(solution)/shard_map/ppermute | solution.py:382
  27.9 3.5 %collective-permute-start.7 = (bf16[512,256]{1,0:T(8,128)(2,1)S(1)}, bf16[512,256]{1,0:T(8,128)(2,1)S(1)}, u32[]{:S(2)}, u32[]{:S(2)}) collective-permute-start(bf16[512,256]{1,0:T(8,128)(2,1)S(1)} %forward_other.1), channel_id=1, source_target_pairs={{0,1},{1,0},{2,3},{3,2},{4,5},{5,4},{6,7},{7,6},{8,9},{9,8},{10,11... | collective-permute-start | bytes 786440 | tf_op jit(solution)/shard_map/ppermute | solution.py:382
  28.0 10.5 %copy-start.2 = (bf16[256,256]{1,0:T(8,128)(2,1)S(1)}, bf16[256,256]{1,0:T(8,128)(2,1)}, u32[]{:S(2)}) copy-start(bf16[256,256]{1,0:T(8,128)(2,1)} %w_self.1) | copy-start | bytes 393220
  28.0 10.5 %copy-start.3 = (f32[256]{0:T(256)S(1)}, f32[256]{0:T(256)}, u32[]{:S(2)}) copy-start(f32[256]{0:T(256)} %param.14) | copy-start | bytes 3076
  29.1 14.6 %copy-start.1 = (bf16[256,256]{1,0:T(8,128)(2,1)S(1)}, bf16[256,256]{1,0:T(8,128)(2,1)}, u32[]{:S(2)}) copy-start(bf16[256,256]{1,0:T(8,128)(2,1)} %refs_5_.1) | copy-start | bytes 393220
  29.1 9.4 %collective-permute-start.9 = (bf16[528,256]{1,0:T(8,128)(2,1)S(1)}, bf16[528,256]{1,0:T(8,128)(2,1)S(1)}, u32[]{:S(2)}, u32[]{:S(2)}) collective-permute-start(bf16[528,256]{1,0:T(8,128)(2,1)S(1)} %near.1.refs_0_.refs_2_), channel_id=1, source_target_pairs={{0,2},{1,3},{2,0},{3,1},{4,6},{5,7},{6,4},{7,5},{8,10},{9,11},{10,... | collective-permute-start | bytes 811016 | tf_op jit(solution)/shard_map/ppermute | solution.py:382
  31.5 12.1 %collective-permute-start.8 = (bf16[512,256]{1,0:T(8,128)(2,1)S(1)}, bf16[512,256]{1,0:T(8,128)(2,1)S(1)}, u32[]{:S(2)}, u32[]{:S(2)}) collective-permute-start(bf16[512,256]{1,0:T(8,128)(2,1)S(1)} %add_convert_fusion.refs_0_), channel_id=1, source_target_pairs={{0,2},{1,3},{2,0},{3,1},{4,6},{5,7},{6,4},{7,5},{8,10},{9,11},{10,... | collective-permute-start | bytes 786440 | tf_op jit(solution)/shard_map/ppermute | solution.py:382
  45.6 1.3 %collective-permute-start.17 = (bf16[128,256]{1,0:T(8,128)(2,1)S(1)}, bf16[128,256]{1,0:T(8,128)(2,1)S(1)}, u32[]{:S(2)}, u32[]{:S(2)}) collective-permute-start(bf16[128,256]{1,0:T(8,128)(2,1)S(1)} %get-tuple-element.34.refs_0_), channel_id=1, source_target_pairs={{0,1},{1,0},{2,3},{3,2},{4,5},{5,4},{6,7},{7,6},{8,9},{9,8},{10,11... | collective-permute-start | bytes 196616 | tf_op jit(solution)/shard_map/ppermute | solution.py:382
  46.9 4.3 %collective-permute-start.18 = (bf16[128,256]{1,0:T(8,128)(2,1)S(1)}, bf16[128,256]{1,0:T(8,128)(2,1)S(1)}, u32[]{:S(2)}, u32[]{:S(2)}) collective-permute-start(bf16[128,256]{1,0:T(8,128)(2,1)S(1)} %add_convert_fusion.8), channel_id=1, source_target_pairs={{0,4},{4,0},{8,12},{12,8},{16,20},{20,16},{24,28},{28,24},{1,5},{5... | collective-permute-start | bytes 196616 | tf_op jit(solution)/shard_map/ppermute | solution.py:382
  47.0 10.4 %collective-permute-start.10 = (bf16[512,256]{1,0:T(8,128)(2,1)S(1)}, bf16[512,256]{1,0:T(8,128)(2,1)S(1)}, u32[]{:S(2)}, u32[]{:S(2)}) collective-permute-start(bf16[512,256]{1,0:T(8,128)(2,1)S(1)} %get-tuple-element.26.mine_ref), channel_id=1, source_target_pairs={{0,1},{1,0},{2,3},{3,2},{4,5},{5,4},{6,7},{7,6},{8,9},{9,8},{10,11... | collective-permute-start | bytes 786440 | tf_op jit(solution)/shard_map/ppermute | solution.py:382
  51.3 5.3 %collective-permute-start.19 = (bf16[128,256]{1,0:T(8,128)(2,1)S(1)}, bf16[128,256]{1,0:T(8,128)(2,1)S(1)}, u32[]{:S(2)}, u32[]{:S(2)}) collective-permute-start(bf16[128,256]{1,0:T(8,128)(2,1)S(1)} %add_convert_fusion.7), channel_id=1, source_target_pairs={{0,16},{4,20},{8,24},{12,28},{16,0},{20,4},{24,8},{28,12},{1,17},{... | collective-permute-start | bytes 196616 | tf_op jit(solution)/shard_map/ppermute | solution.py:382
  56.6 8.3 %collective-permute-start.20 = (bf16[128,256]{1,0:T(8,128)(2,1)S(1)}, bf16[128,256]{1,0:T(8,128)(2,1)S(1)}, u32[]{:S(2)}, u32[]{:S(2)}) collective-permute-start(bf16[128,256]{1,0:T(8,128)(2,1)S(1)} %add_convert_fusion.6), channel_id=1, source_target_pairs={{0,8},{4,12},{8,0},{12,4},{16,24},{20,28},{24,16},{28,20},{1,9},{5... | collective-permute-start | bytes 196616 | tf_op jit(solution)/shard_map/ppermute | solution.py:382
  58.3 5.7 %collective-permute-start.14 = (bf16[256,256]{1,0:T(8,128)(2,1)S(1)}, bf16[256,256]{1,0:T(8,128)(2,1)S(1)}, u32[]{:S(2)}, u32[]{:S(2)}) collective-permute-start(bf16[256,256]{1,0:T(8,128)(2,1)S(1)} %backward_far.1), channel_id=1, source_target_pairs={{0,4},{4,0},{8,12},{12,8},{16,20},{20,16},{24,28},{28,24},{1,5},{5... | collective-permute-start | bytes 393224 | tf_op jit(solution)/shard_map/ppermute | solution.py:382
  60.1 9.8 %collective-permute-start.13 = (bf16[256,256]{1,0:T(8,128)(2,1)S(1)}, bf16[256,256]{1,0:T(8,128)(2,1)S(1)}, u32[]{:S(2)}, u32[]{:S(2)}) collective-permute-start(bf16[256,256]{1,0:T(8,128)(2,1)S(1)} %get-tuple-element.31), channel_id=1, source_target_pairs={{0,4},{4,0},{8,12},{12,8},{16,20},{20,16},{24,28},{28,24},{1,5},{5... | collective-permute-start | bytes 393224 | tf_op jit(solution)/shard_map/ppermute | solution.py:382
  64.1 5.9 %collective-permute-start.15 = (bf16[256,256]{1,0:T(8,128)(2,1)S(1)}, bf16[256,256]{1,0:T(8,128)(2,1)S(1)}, u32[]{:S(2)}, u32[]{:S(2)}) collective-permute-start(bf16[256,256]{1,0:T(8,128)(2,1)S(1)} %add_convert_fusion.3), channel_id=1, source_target_pairs={{0,8},{4,12},{8,0},{12,4},{16,24},{20,28},{24,16},{28,20},{1,9},{5... | collective-permute-start | bytes 393224 | tf_op jit(solution)/shard_map/ppermute | solution.py:382
  64.9 5.0 %collective-permute-start.21 = (bf16[128,256]{1,0:T(8,128)(2,1)S(1)}, bf16[128,256]{1,0:T(8,128)(2,1)S(1)}, u32[]{:S(2)}, u32[]{:S(2)}) collective-permute-start(bf16[128,256]{1,0:T(8,128)(2,1)S(1)} %add_convert_fusion.5.refs_0_), channel_id=1, source_target_pairs={{0,2},{1,3},{2,0},{3,1},{4,6},{5,7},{6,4},{7,5},{8,10},{9,11},{10,... | collective-permute-start | bytes 196616 | tf_op jit(solution)/shard_map/ppermute | solution.py:382
  67.7 6.4 %collective-permute-start.11 = (bf16[512,256]{1,0:T(8,128)(2,1)S(1)}, bf16[512,256]{1,0:T(8,128)(2,1)S(1)}, u32[]{:S(2)}, u32[]{:S(2)}) collective-permute-start(bf16[512,256]{1,0:T(8,128)(2,1)S(1)} %get-tuple-element.28), channel_id=1, source_target_pairs={{0,4},{4,0},{8,12},{12,8},{16,20},{20,16},{24,28},{28,24},{1,5},{5... | collective-permute-start | bytes 786440 | tf_op jit(solution)/shard_map/ppermute | solution.py:382
  68.3 6.0 %collective-permute-start.22 = (bf16[128,256]{1,0:T(8,128)(2,1)S(1)}, bf16[128,256]{1,0:T(8,128)(2,1)S(1)}, u32[]{:S(2)}, u32[]{:S(2)}) collective-permute-start(bf16[128,256]{1,0:T(8,128)(2,1)S(1)} %add_convert_fusion.5.refs_0_), channel_id=1, source_target_pairs={{0,1},{1,0},{2,3},{3,2},{4,5},{5,4},{6,7},{7,6},{8,9},{9,8},{10,11... | collective-permute-start | bytes 196616 | tf_op jit(solution)/shard_map/ppermute | solution.py:382
  69.9 4.5 %collective-permute-start.23 = (bf16[128,256]{1,0:T(8,128)(2,1)S(1)}, bf16[128,256]{1,0:T(8,128)(2,1)S(1)}, u32[]{:S(2)}, u32[]{:S(2)}) collective-permute-start(bf16[128,256]{1,0:T(8,128)(2,1)S(1)} %collective-permute-done.21.refs_1_), channel_id=1, source_target_pairs={{0,1},{1,0},{2,3},{3,2},{4,5},{5,4},{6,7},{7,6},{8,9},{9,8},{10,11... | collective-permute-start | bytes 196616 | tf_op jit(solution)/shard_map/ppermute | solution.py:382
  70.0 9.8 %collective-permute-start.16 = (bf16[256,256]{1,0:T(8,128)(2,1)S(1)}, bf16[256,256]{1,0:T(8,128)(2,1)S(1)}, u32[]{:S(2)}, u32[]{:S(2)}) collective-permute-start(bf16[256,256]{1,0:T(8,128)(2,1)S(1)} %add_convert_fusion.2), channel_id=1, source_target_pairs={{0,16},{4,20},{8,24},{12,28},{16,0},{20,4},{24,8},{28,12},{1,17},{... | collective-permute-start | bytes 393224 | tf_op jit(solution)/shard_map/ppermute | solution.py:382
  74.1 7.0 %collective-permute-start.12 = (bf16[256,256]{1,0:T(8,128)(2,1)S(1)}, bf16[256,256]{1,0:T(8,128)(2,1)S(1)}, u32[]{:S(2)}, u32[]{:S(2)}) collective-permute-start(bf16[256,256]{1,0:T(8,128)(2,1)S(1)} %add_convert_fusion.4), channel_id=1, source_target_pairs={{0,8},{4,12},{8,0},{12,4},{16,24},{20,28},{24,16},{28,20},{1,9},{5... | collective-permute-start | bytes 393224 | tf_op jit(solution)/shard_map/ppermute | solution.py:382
